TPU v7x, 32 devices: a whole 2x2x4 slice. The times are simulated.
32 devices in a mesh: tm: 2 (over core), tile: 16 (over z, y, x).
Axes of the slice: x: 2, y: 2, z: 4, core: 2. Of those that a mesh axis runs over, the one named last changes fastest.
Arguments:
- frames: bfloat16 [8, 16, 64, 32, 128], P('tm', 'tile'), may hold values from -6 to 6
- w_in: bfloat16 [3, 3, 128, 128], replicated, may hold values from -0.1875 to 0.1875
- w_out: bfloat16 [3, 3, 128, 128], replicated, may hold values from -0.1875 to 0.1875
- decay: float32 [8, 128], P('tm'), may hold values from 0 to 1
- skip: float32 [128], replicated, may hold values from 0.5 to 1.5
Outputs:
- mixed: bfloat16 [8, 16, 64, 32, 128], P('tm', 'tile')
All inputs are finite; a program needn't handle non-finite values.
Results may differ from a plain program's by a relative error of at most 0.006.
Values may be sent and summed in bfloat16 or wider, within the bound.
No kernel may reach another device: no remote copies, remote signals or barrier semaphores. Data moves between devices by JAX's collectives and lax.ppermute only.
A program may use at most 64 MiB of HBM per device.

v0:
```python
import jax
import jax.numpy as jnp
from jax import lax
from jax.sharding import PartitionSpec as P

TROWS = 4


def passed_along(value, axis, by):
    size = lax.axis_size(axis)
    return lax.ppermute(value, axis, [(i, (i + by) % size) for i in range(size)])


def from_behind(value, axis, steps):
    count = lax.axis_size(axis)
    initial, last = (max(0, -steps), min(count, count - steps))
    return lax.ppermute(value, axis, [(source, source + steps) for source in range(initial, last)])


def side_edge(piece, by):
    return passed_along(piece, "tile", by)


def row_edge(piece, by):
    return passed_along(piece, "tile", by)


def bordered(field, column, row_index, tcols, trows):
    edges = [
        side_edge(field[:, :, -1:, :] if by == 1 else field[:, :, :1, :], by) for by in (1, -1)
    ]
    left_col = jnp.where(column > 0, edges[0], jnp.zeros_like(edges[0]))
    right_col = jnp.where(column < tcols - 1, edges[1], jnp.zeros_like(edges[1]))
    widened = jnp.concatenate([left_col, field, right_col], axis=2)
    rims = [
        row_edge(widened[:, -1:] if by == tcols else widened[:, :1], by) for by in (tcols, -tcols)
    ]
    upper_rim = jnp.where(row_index > 0, rims[0], jnp.zeros_like(rims[0]))
    lower_rim = jnp.where(row_index < trows - 1, rims[1], jnp.zeros_like(rims[1]))
    return jnp.concatenate([upper_rim, widened, lower_rim], axis=1)


def convolve(padded, weight, rows, cols):
    count = padded.shape[0]
    depth = padded.shape[3]
    total = jnp.zeros((count * rows * cols, weight.shape[3]), jnp.float32)
    for shift_row in range(3):
        for shift_col in range(3):
            window = padded[
                :, shift_row : shift_row + rows, shift_col : shift_col + cols, :
            ].reshape(-1, depth)
            total = total + jnp.dot(
                window, weight[shift_row, shift_col], preferred_element_type=jnp.float32
            )
    return total.reshape(count, rows, cols, weight.shape[3])


def per_device(frames, w_in, w_out, decay, skip):
    tile_count = lax.axis_size("tile")
    tcols = tile_count // TROWS
    tile_number = (lax.axis_index("tile") + tile_count - 1) % tile_count
    column = tile_number % tcols
    row_index = tile_number // tcols
    video = frames[:, 0]
    count, rows, cols, _ = video.shape
    drive = convolve(bordered(video, column, row_index, tcols, TROWS), w_in, rows, cols)
    state = jnp.zeros((rows, cols, w_in.shape[3]), jnp.float32)
    factor = jnp.ones((w_in.shape[3],), jnp.float32)
    local_states = []
    factors = []
    for frame in range(count):
        state = decay[frame] * state + drive[frame]
        factor = factor * decay[frame]
        local_states.append(state)
        factors.append(factor)
    incoming = from_behind(state.astype(jnp.bfloat16), "tm", 1).astype(state.dtype)
    states_bf = jnp.stack(
        [local_states[frame] + factors[frame] * incoming for frame in range(count)]
    ).astype(jnp.bfloat16)
    readout = convolve(bordered(states_bf, column, row_index, tcols, TROWS), w_out, rows, cols)
    mixed = readout + skip * video.astype(jnp.float32)
    return mixed.astype(jnp.bfloat16)[:, None]


def solution(mesh):
    return jax.shard_map(
        per_device,
        mesh=mesh,
        in_specs=(P("tm", "tile", None, None, None), P(), P(), P("tm", None), P()),
        out_specs=P("tm", "tile", None, None, None),
        check_vma=False,
    )
```

profile of v0, /device:TPU:0, one launch (start us, length us, event | category | flops | bytes accessed | tf_op | source)
XLA Modules:
  0.0 78.5 jit_solution(17578366186284825853)
XLA Ops:
  0.0 1.6 %fusion.62 = (bf16[4,64,1,128]{3,2,1,0:T(2,128)(2,1)S(1)}, bf16[4,64,1,128]{3,2,1,0:T(2,128)(2,1)S(1)}) fusion(bf16[4,64,32,128]{3,2,1,0:T(8,128)(2,1)} %bitcast.127), kind=kLoop, calls=%fused_computation.121 | loop fusion | bytes 262144 | tf_op jit(solution)/shard_map/slice | solution.py:30
  1.6 7.0 %collective-permute-start.1 = (bf16[4,64,1,128]{3,2,1,0:T(2,128)(2,1)S(1)}, bf16[4,64,1,128]{3,2,1,0:T(2,128)(2,1)S(1)}, u32[]{:S(2)}, u32[]{:S(2)}) collective-permute-start(bf16[4,64,1,128]{3,2,1,0:T(2,128)(2,1)S(1)} %get-tuple-element.42), channel_id=1, source_target_pairs={{0,15},{1,0},{2,1},{3,2},{4,3},{5,4},{6,5},{7,6},{8,7},{9,8},{10,9... | collective-permute-start | bytes 196616 | tf_op jit(solution)/shard_map/ppermute | solution.py:11
  8.6 0.8 %slice_bitcast_fusion.3 = (f32[128]{0:T(128)S(1)}, f32[128]{0:T(128)S(1)}, f32[128]{0:T(128)S(1)}, f32[128]{0:T(128)S(1)}) fusion(f32[4,128]{1,0:T(4,128)} %param.8), kind=kLoop, calls=%fused_computation.109 | loop fusion | bytes 4096 | tf_op jit(solution)/shard_map/mul | solution.py:72
  9.4 0.8 %fusion.50 = (f32[128]{0:T(128)S(1)}, f32[128]{0:T(128)S(1)}, f32[128]{0:T(128)S(1)}, f32[128]{0:T(128)S(1)}) fusion(f32[4,128]{1,0:T(4,128)} %param.8), kind=kLoop, calls=%fused_computation.111 | loop fusion | flops 512 | bytes 4096 | tf_op jit(solution)/shard_map/mul | solution.py:73
  10.3 1.1 %collective-permute-done.1 = bf16[4,64,1,128]{3,2,1,0:T(2,128)(2,1)S(1)} collective-permute-done((bf16[4,64,1,128]{3,2,1,0:T(2,128)(2,1)S(1)}, bf16[4,64,1,128]{3,2,1,0:T(2,128)(2,1)S(1)}, u32[]{:S(2)}, u32[]{:S(2)}) %collective-permute-start.1) | collective-permute-done | bytes 65568 | tf_op jit(solution)/shard_map/ppermute | solution.py:11
  11.5 5.7 %collective-permute-done = bf16[4,64,1,128]{3,2,1,0:T(2,128)(2,1)S(1)} collective-permute-done((bf16[4,64,1,128]{3,2,1,0:T(2,128)(2,1)S(1)}, bf16[4,64,1,128]{3,2,1,0:T(2,128)(2,1)S(1)}, u32[]{:S(2)}, u32[]{:S(2)}) %collective-permute-start) | collective-permute-done | bytes 65568 | tf_op jit(solution)/shard_map/ppermute | solution.py:11
  17.4 0.8 %pad_maximum_fusion.19 = (bf16[4,1,34,128]{3,2,1,0:T(8,128)(2,1)S(1)}, bf16[4,1,34,128]{3,2,1,0:T(8,128)(2,1)S(1)}) fusion(bf16[4,64,1,128]{3,2,1,0:T(2,128)(2,1)S(1)} %broadcast_select_fusion.1, bf16[4,64,32,128]{3,2,1,0:T(8,128)(2,1)} %bitcast.128, bf16[4,64,1,128]{3,2,1,0:T(2,128)(2,1)S(1)} %broadcast_select_fusion.3), kind=kLoop, calls=%fused_computation.61 | loop fusion | flops 208896 | bytes 2297856 | tf_op jit(solution)/shard_map/concatenate | solution.py:34
  18.3 2.3 %pad_maximum_fusion.10 = (bf16[4,64,32,128]{3,2,1,0:T(8,128)(2,1)S(1)}, bf16[4,64,32,128]{3,2,1,0:T(8,128)(2,1)S(1)}) fusion(bf16[4,64,1,128]{3,2,1,0:T(2,128)(2,1)S(1)} %broadcast_select_fusion.1, bf16[4,64,32,128]{3,2,1,0:T(8,128)(2,1)S(1)} %bitcast.129, bf16[4,64,1,128]{3,2,1,0:T(2,128)(2,1)S(1)} %broadcast_select_fusion.3), kind=kLoop, calls=%fused_computation.29 | loop fusion | flops 8388608 | bytes 6422528 | tf_op jit(solution)/shard_map/concatenate | solution.py:34
  20.6 2.2 %collective-permute-start.2 = (bf16[4,1,34,128]{3,2,1,0:T(8,128)(2,1)S(1)}, bf16[4,1,34,128]{3,2,1,0:T(8,128)(2,1)S(1)}, u32[]{:S(2)}, u32[]{:S(2)}) collective-permute-start(bf16[4,1,34,128]{3,2,1,0:T(8,128)(2,1)S(1)} %get-tuple-element.34), channel_id=1, source_target_pairs={{0,4},{1,5},{2,6},{3,7},{4,8},{5,9},{6,10},{7,11},{8,12},{9,13},{1... | collective-permute-start | bytes 104456 | tf_op jit(solution)/shard_map/ppermute | solution.py:11
  22.9 3.8 %collective-permute-done.2 = bf16[4,1,34,128]{3,2,1,0:T(8,128)(2,1)S(1)} collective-permute-done((bf16[4,1,34,128]{3,2,1,0:T(8,128)(2,1)S(1)}, bf16[4,1,34,128]{3,2,1,0:T(8,128)(2,1)S(1)}, u32[]{:S(2)}, u32[]{:S(2)}) %collective-permute-start.2) | collective-permute-done | bytes 34848 | tf_op jit(solution)/shard_map/ppermute | solution.py:11
  26.6 3.2 %pad_maximum_fusion = (bf16[4,65,34,128]{3,2,1,0:T(8,128)(2,1)S(1)}, bf16[4,65,34,128]{3,2,1,0:T(8,128)(2,1)S(1)}) fusion(bf16[4,1,34,128]{3,2,1,0:T(8,128)(2,1)S(1)} %broadcast_select_fusion.5, bf16[4,64,1,128]{3,2,1,0:T(2,128)(2,1)S(1)} %broadcast_select_fusion.1, bf16[4,64,32,128]{3,2,1,0:T(8,128)(2,1)S(1)} %bitcast.130, ...), kind=kLoop, calls=%fused_computation.18 | loop fusion | flops 18104320 | bytes 6823936 | tf_op jit(solution)/shard_map/concatenate | solution.py:40
  29.8 3.0 %fusion.59 = (bf16[4,64,32,128]{3,2,1,0:T(8,128)(2,1)S(1)}, bf16[4,64,32,128]{3,2,1,0:T(8,128)(2,1)S(1)}, bf16[4,64,32,128]{3,2,1,0:T(8,128)(2,1)S(1)}, bf16[4,6...) fusion(bf16[4,65,34,128]{3,2,1,0:T(8,128)(2,1)S(1)} %get-tuple-element.3, ...), kind=kLoop, calls=%fused_computation.118 | loop fusion | bytes 25165824 | tf_op jit(solution)/shard_map/slice | solution.py:49
  40.1 1.3 %collective-permute-start.4 = (bf16[64,32,128]{2,1,0:T(8,128)(2,1)S(1)}, bf16[64,32,128]{2,1,0:T(8,128)(2,1)S(1)}, u32[]{:S(2)}, u32[]{:S(2)}) collective-permute-start(bf16[64,32,128]{2,1,0:T(8,128)(2,1)S(1)} %get-tuple-element.8), channel_id=1, source_target_pairs={{0,16},{1,17},{2,18},{3,19},{4,20},{5,21},{6,22},{7,23},{8,24},{9,... | collective-permute-start | bytes 1572872 | tf_op jit(solution)/shard_map/ppermute | solution.py:17
  41.4 1.5 %collective-permute-done.4 = bf16[64,32,128]{2,1,0:T(8,128)(2,1)S(1)} collective-permute-done((bf16[64,32,128]{2,1,0:T(8,128)(2,1)S(1)}, bf16[64,32,128]{2,1,0:T(8,128)(2,1)S(1)}, u32[]{:S(2)}, u32[]{:S(2)}) %collective-permute-start.4) | collective-permute-done | bytes 524320 | tf_op jit(solution)/shard_map/ppermute | solution.py:17
  44.0 2.0 %collective-permute-start.5 = (bf16[4,64,1,128]{3,2,1,0:T(2,128)(2,1)S(1)}, bf16[4,64,1,128]{3,2,1,0:T(2,128)(2,1)S(1)}, u32[]{:S(2)}, u32[]{:S(2)}) collective-permute-start(bf16[4,64,1,128]{3,2,1,0:T(2,128)(2,1)S(1)} %get-tuple-element.37), channel_id=1, source_target_pairs={{0,1},{1,2},{2,3},{3,4},{4,5},{5,6},{6,7},{7,8},{8,9},{9,10},{10,1... | collective-permute-start | bytes 196616 | tf_op jit(solution)/shard_map/ppermute | solution.py:11
  46.0 4.3 %collective-permute-done.6 = bf16[4,64,1,128]{3,2,1,0:T(2,128)(2,1)S(1)} collective-permute-done((bf16[4,64,1,128]{3,2,1,0:T(2,128)(2,1)S(1)}, bf16[4,64,1,128]{3,2,1,0:T(2,128)(2,1)S(1)}, u32[]{:S(2)}, u32[]{:S(2)}) %collective-permute-start.6) | collective-permute-done | bytes 65568 | tf_op jit(solution)/shard_map/ppermute | solution.py:11
  50.5 3.0 %collective-permute-done.5 = bf16[4,64,1,128]{3,2,1,0:T(2,128)(2,1)S(1)} collective-permute-done((bf16[4,64,1,128]{3,2,1,0:T(2,128)(2,1)S(1)}, bf16[4,64,1,128]{3,2,1,0:T(2,128)(2,1)S(1)}, u32[]{:S(2)}, u32[]{:S(2)}) %collective-permute-start.5) | collective-permute-done | bytes 65568 | tf_op jit(solution)/shard_map/ppermute | solution.py:11
  54.0 2.8 %pad_maximum_fusion.2 = (bf16[4,64,32,128]{3,2,1,0:T(8,128)(2,1)S(1)}, bf16[4,64,32,128]{3,2,1,0:T(8,128)(2,1)S(1)}) fusion(bf16[4,64,1,128]{3,2,1,0:T(2,128)(2,1)S(1)} %broadcast_select_fusion, bf16[1,64,32,128]{3,2,1,0:T(8,128)(2,1)S(1)} %get-tuple-element.46, bf16[1,64,32,128]{3,2,1,0:T(8,128)(2,1)S(1)} %get-tuple-element.44, ...), kind=kLoop, calls=%fused_computation.21 | loop fusion | flops 20971520 | bytes 6422528 | tf_op jit(solution)/shard_map/concatenate | solution.py:34
  56.9 2.0 %collective-permute-start.7 = (bf16[4,1,34,128]{3,2,1,0:T(8,128)(2,1)S(1)}, bf16[4,1,34,128]{3,2,1,0:T(8,128)(2,1)S(1)}, u32[]{:S(2)}, u32[]{:S(2)}) collective-permute-start(bf16[4,1,34,128]{3,2,1,0:T(8,128)(2,1)S(1)} %get-tuple-element.30), channel_id=1, source_target_pairs={{0,4},{1,5},{2,6},{3,7},{4,8},{5,9},{6,10},{7,11},{8,12},{9,13},{1... | collective-permute-start | bytes 104456 | tf_op jit(solution)/shard_map/ppermute | solution.py:11
  58.9 3.8 %collective-permute-done.7 = bf16[4,1,34,128]{3,2,1,0:T(8,128)(2,1)S(1)} collective-permute-done((bf16[4,1,34,128]{3,2,1,0:T(8,128)(2,1)S(1)}, bf16[4,1,34,128]{3,2,1,0:T(8,128)(2,1)S(1)}, u32[]{:S(2)}, u32[]{:S(2)}) %collective-permute-start.7) | collective-permute-done | bytes 34848 | tf_op jit(solution)/shard_map/ppermute | solution.py:11
  62.7 4.4 %pad_maximum_fusion.1 = (bf16[4,65,34,128]{3,2,1,0:T(8,128)(2,1)S(1)}, bf16[4,65,34,128]{3,2,1,0:T(8,128)(2,1)S(1)}) fusion(bf16[4,1,34,128]{3,2,1,0:T(8,128)(2,1)S(1)} %broadcast_select_fusion.4, bf16[4,64,1,128]{3,2,1,0:T(2,128)(2,1)S(1)} %broadcast_select_fusion, bf16[1,64,32,128]{3,2,1,0:T(8,128)(2,1)S(1)} %get-tuple-element.46, ...), kind=kLoop, calls=%fused_computation.20 | loop fusion | flops 31682560 | bytes 6823936 | tf_op jit(solution)/shard_map/concatenate | solution.py:40
  67.2 1.5 %fusion.58 = (bf16[4,64,32,128]{3,2,1,0:T(8,128)(2,1)S(1)}, bf16[4,64,32,128]{3,2,1,0:T(8,128)(2,1)S(1)}, bf16[4,64,32,128]{3,2,1,0:T(8,128)(2,1)S(1)}) fusion(bf16[4,65,34,128]{3,2,1,0:T(8,128)(2,1)S(1)} %get-tuple-element.28), kind=kLoop, calls=%fused_computation.117 | loop fusion | bytes 12582912 | tf_op jit(solution)/shard_map/slice | solution.py:49
  68.6 1.3 %fusion.57 = (bf16[4,64,32,128]{3,2,1,0:T(8,128)(2,1)S(1)}, bf16[4,64,32,128]{3,2,1,0:T(8,128)(2,1)S(1)}, bf16[4,64,32,128]{3,2,1,0:T(8,128)(2,1)S(1)}) fusion(bf16[4,65,34,128]{3,2,1,0:T(8,128)(2,1)S(1)} %get-tuple-element.27), kind=kLoop, calls=%fused_computation.116 | loop fusion | bytes 12582912 | tf_op jit(solution)/shard_map/slice | solution.py:49
  76.4 2.1 %add_convert_fusion = bf16[4,1,64,32,128]{4,3,2,1,0:T(8,128)(2,1)} fusion(f32[4,1,64,32,128]{4,3,2,1,0:T(8,128)S(1)} %bitcast.132, bf16[4,1,64,32,128]{4,3,2,1,0:T(8,128)(2,1)S(1)} %copy-done, f32[128]{0:T(128)S(1)} %copy-done.3), kind=kLoop, calls=%fused_computation.16 | loop fusion | flops 4194304 | bytes 8389120 | tf_op jit(solution)/shard_map/convert_element_type | solution.py:82
  (46 shorter events, 15.6 us)
Async XLA Ops:
  0.0 18.3 %copy-start = (bf16[4,1,64,32,128]{4,3,2,1,0:T(8,128)(2,1)S(1)}, bf16[4,1,64,32,128]{4,3,2,1,0:T(8,128)(2,1)}, u32[]{:S(2)}) copy-start(bf16[4,1,64,32,128]{4,3,2,1,0:T(8,128)(2,1)} %param.5) | copy-start | bytes 6291460
  1.6 9.8 %collective-permute-start.1 = (bf16[4,64,1,128]{3,2,1,0:T(2,128)(2,1)S(1)}, bf16[4,64,1,128]{3,2,1,0:T(2,128)(2,1)S(1)}, u32[]{:S(2)}, u32[]{:S(2)}) collective-permute-start(bf16[4,64,1,128]{3,2,1,0:T(2,128)(2,1)S(1)} %get-tuple-element.42), channel_id=1, source_target_pairs={{0,15},{1,0},{2,1},{3,2},{4,3},{5,4},{6,5},{7,6},{8,7},{9,8},{10,9... | collective-permute-start | bytes 196616 | tf_op jit(solution)/shard_map/ppermute | solution.py:11
  8.6 8.7 %collective-permute-start = (bf16[4,64,1,128]{3,2,1,0:T(2,128)(2,1)S(1)}, bf16[4,64,1,128]{3,2,1,0:T(2,128)(2,1)S(1)}, u32[]{:S(2)}, u32[]{:S(2)}) collective-permute-start(bf16[4,64,1,128]{3,2,1,0:T(2,128)(2,1)S(1)} %get-tuple-element.41), channel_id=1, source_target_pairs={{0,1},{1,2},{2,3},{3,4},{4,5},{5,6},{6,7},{7,8},{8,9},{9,10},{10,1... | collective-permute-start | bytes 196616 | tf_op jit(solution)/shard_map/ppermute | solution.py:11
  18.2 4.6 %collective-permute-start.3 = (bf16[4,1,34,128]{3,2,1,0:T(8,128)(2,1)S(1)}, bf16[4,1,34,128]{3,2,1,0:T(8,128)(2,1)S(1)}, u32[]{:S(2)}, u32[]{:S(2)}) collective-permute-start(bf16[4,1,34,128]{3,2,1,0:T(8,128)(2,1)S(1)} %get-tuple-element.33), channel_id=1, source_target_pairs={{0,12},{1,13},{2,14},{3,15},{4,0},{5,1},{6,2},{7,3},{8,4},{9,5},{1... | collective-permute-start | bytes 104456 | tf_op jit(solution)/shard_map/ppermute | solution.py:11
  20.6 6.0 %collective-permute-start.2 = (bf16[4,1,34,128]{3,2,1,0:T(8,128)(2,1)S(1)}, bf16[4,1,34,128]{3,2,1,0:T(8,128)(2,1)S(1)}, u32[]{:S(2)}, u32[]{:S(2)}) collective-permute-start(bf16[4,1,34,128]{3,2,1,0:T(8,128)(2,1)S(1)} %get-tuple-element.34), channel_id=1, source_target_pairs={{0,4},{1,5},{2,6},{3,7},{4,8},{5,9},{6,10},{7,11},{8,12},{9,13},{1... | collective-permute-start | bytes 104456 | tf_op jit(solution)/shard_map/ppermute | solution.py:11
  29.8 3.0 %copy-start.1 = (bf16[3,3,128,128]{3,2,1,0:T(8,128)(2,1)S(1)}, bf16[3,3,128,128]{3,2,1,0:T(8,128)(2,1)}, u32[]{:S(2)}) copy-start(bf16[3,3,128,128]{3,2,1,0:T(8,128)(2,1)} %param.6) | copy-start | bytes 884740
  40.1 2.8 %collective-permute-start.4 = (bf16[64,32,128]{2,1,0:T(8,128)(2,1)S(1)}, bf16[64,32,128]{2,1,0:T(8,128)(2,1)S(1)}, u32[]{:S(2)}, u32[]{:S(2)}) collective-permute-start(bf16[64,32,128]{2,1,0:T(8,128)(2,1)S(1)} %get-tuple-element.8), channel_id=1, source_target_pairs={{0,16},{1,17},{2,18},{3,19},{4,20},{5,21},{6,22},{7,23},{8,24},{9,... | collective-permute-start | bytes 1572872 | tf_op jit(solution)/shard_map/ppermute | solution.py:17
  44.0 6.4 %collective-permute-start.6 = (bf16[4,64,1,128]{3,2,1,0:T(2,128)(2,1)S(1)}, bf16[4,64,1,128]{3,2,1,0:T(2,128)(2,1)S(1)}, u32[]{:S(2)}, u32[]{:S(2)}) collective-permute-start(bf16[4,64,1,128]{3,2,1,0:T(2,128)(2,1)S(1)} %get-tuple-element.38), channel_id=1, source_target_pairs={{0,15},{1,0},{2,1},{3,2},{4,3},{5,4},{6,5},{7,6},{8,7},{9,8},{10,9... | collective-permute-start | bytes 196616 | tf_op jit(solution)/shard_map/ppermute | solution.py:11
  44.0 9.5 %collective-permute-start.5 = (bf16[4,64,1,128]{3,2,1,0:T(2,128)(2,1)S(1)}, bf16[4,64,1,128]{3,2,1,0:T(2,128)(2,1)S(1)}, u32[]{:S(2)}, u32[]{:S(2)}) collective-permute-start(bf16[4,64,1,128]{3,2,1,0:T(2,128)(2,1)S(1)} %get-tuple-element.37), channel_id=1, source_target_pairs={{0,1},{1,2},{2,3},{3,4},{4,5},{5,6},{6,7},{7,8},{8,9},{9,10},{10,1... | collective-permute-start | bytes 196616 | tf_op jit(solution)/shard_map/ppermute | solution.py:11
  53.8 5.2 %collective-permute-start.8 = (bf16[4,1,34,128]{3,2,1,0:T(8,128)(2,1)S(1)}, bf16[4,1,34,128]{3,2,1,0:T(8,128)(2,1)S(1)}, u32[]{:S(2)}, u32[]{:S(2)}) collective-permute-start(bf16[4,1,34,128]{3,2,1,0:T(8,128)(2,1)S(1)} %get-tuple-element.29), channel_id=1, source_target_pairs={{0,12},{1,13},{2,14},{3,15},{4,0},{5,1},{6,2},{7,3},{8,4},{9,5},{1... | collective-permute-start | bytes 104456 | tf_op jit(solution)/shard_map/ppermute | solution.py:11
  56.9 5.9 %collective-permute-start.7 = (bf16[4,1,34,128]{3,2,1,0:T(8,128)(2,1)S(1)}, bf16[4,1,34,128]{3,2,1,0:T(8,128)(2,1)S(1)}, u32[]{:S(2)}, u32[]{:S(2)}) collective-permute-start(bf16[4,1,34,128]{3,2,1,0:T(8,128)(2,1)S(1)} %get-tuple-element.30), channel_id=1, source_target_pairs={{0,4},{1,5},{2,6},{3,7},{4,8},{5,9},{6,10},{7,11},{8,12},{9,13},{1... | collective-permute-start | bytes 104456 | tf_op jit(solution)/shard_map/ppermute | solution.py:11
  68.6 1.3 %copy-start.2 = (bf16[3,3,128,128]{3,2,1,0:T(8,128)(2,1)S(1)}, bf16[3,3,128,128]{3,2,1,0:T(8,128)(2,1)}, u32[]{:S(2)}) copy-start(bf16[3,3,128,128]{3,2,1,0:T(8,128)(2,1)} %param.7) | copy-start | bytes 884740
  75.6 0.7 copy-start.3
where the time goes:
time: 78.7 us; the launch traced here: 78.5 us
  waiting for transfers between devices  23.3 us (30%)
  other arithmetic  18.5 us (24%)
  starting transfers between devices  15 us (19%)
  matrix products  12.7 us (16%)
  local copies, waits for them, and re-layouts  8.67 us (11%)
    ppermute x8, waiting for transfers between devices, passed_along(): lax.ppermute(value, axis, [(i, (i + by) % size) for i in range(size)])  21.8 us
    ppermute x8, starting transfers between devices, passed_along(): lax.ppermute(value, axis, [(i, (i + by) % size) for i in range(size)])  13.7 us
    dot_general x18, matrix products, convolve(): jnp.dot(window, weight[shift_row, shift_col], preferred_element_type=jnp....  12.7 us
    concatenate x2, other arithmetic, bordered(): return jnp.concatenate([upper_rim, widened, lower_rim], axis=1)  7.59 us
    concatenate x4, other arithmetic, bordered(): widened = jnp.concatenate([left_col, field, right_col], axis=2)  5.97 us
    slice x3, local copies, waits for them, and re-layouts, convolve(): padded[:, shift_row:shift_row + rows, shift_col:shift_col + cols, :]  5.76 us
    convert_element_type x1, other arithmetic, per_device(): return mixed.astype(jnp.bfloat16)[:, None]  2.12 us
    slice x2, local copies, waits for them, and re-layouts, bordered(): field[:, :, -1:, :]  1.78 us
  transfers between devices with their start and end apart: 9, of which 7 were waited for; matrix products, arithmetic and copies ran while one was open for 9% of the time, Pallas kernels for 0%

commit v1 on v0

v1 whole, which is shorter than its diff:
```python
import functools

import jax
import jax.numpy as jnp
from jax import lax
from jax.experimental import pallas as pl
from jax.experimental.pallas import tpu as pltpu
from jax.sharding import PartitionSpec as P

TROWS = 4
BF = jnp.bfloat16
F32 = jnp.float32
LIMIT = 24 << 20
BLOCK = 16
VM = pl.BlockSpec(memory_space=pltpu.VMEM)


def shifted(value, axis, by):
    size = lax.axis_size(axis)
    return lax.ppermute(value, axis, [(i, (i + by) % size) for i in range(size)])


def place():
    count = lax.axis_size("tile")
    tcols = count // TROWS
    number = lax.rem(lax.axis_index("tile") + count - 1, count)
    return lax.rem(number, tcols), lax.div(number, tcols), tcols


def dot(a, b):
    return jnp.dot(a, b, preferred_element_type=F32)


def spread(w_ref, wide):
    c, n = w_ref.shape[2:]
    zero = jnp.zeros((c, n), BF)
    for tap in range(3):
        for row in range(4):
            for out in range(2):
                at = tap * 2 * n + out * n
                k = row - out
                wide[row * c : (row + 1) * c, at : at + n] = w_ref[k, tap] if 0 <= k <= 2 else zero


def gathered(y, pairs, cols, n2):
    y = y.reshape(pairs, cols, 3 * n2)
    left, mid, right = y[:, :, :n2], y[:, :, n2 : 2 * n2], y[:, :, 2 * n2 :]
    col = lax.broadcasted_iota(jnp.int32, mid.shape, 1)
    left = jnp.where(col > 0, pltpu.roll(left, 1, 1), 0.0)
    right = jnp.where(col < cols - 1, pltpu.roll(right, cols - 1, 1), 0.0)
    return mid + left + right


def gathered_edge(y, pairs, n2):
    y = y.reshape(pairs, 8, 3 * n2)
    left, mid, right = y[:, :, :n2], y[:, :, n2 : 2 * n2], y[:, :, 2 * n2 :]
    col = lax.broadcasted_iota(jnp.int32, mid.shape, 1)
    full = (col == 2) | (col == 5)
    left = jnp.where(full | (col == 6), pltpu.roll(left, 1, 1), 0.0)
    right = jnp.where(full | (col == 1), pltpu.roll(right, 7, 1), 0.0)
    return jnp.where(full, mid, 0.0) + left + right


def blocks(pairs):
    return [(q, min(BLOCK, pairs - q)) for q in range(1, pairs, BLOCK)]


def main_kernel(x_ref, w_ref, d_ref, s_ref, wide):
    frames, pairs, _, cols, c = x_ref.shape
    n2 = s_ref.shape[3]
    spread(w_ref, wide)

    def rows(f, p, n):
        return jnp.concatenate(
            [x_ref[f, p : p + n, r].reshape(n * cols, c) for r in range(2)], axis=-1
        )

    for q, n in [(0, 1), *blocks(pairs), (pairs, 1)]:
        state = None
        for f in range(frames):
            y = None
            if q > 0:
                y = dot(rows(f, q - 1, n), wide[: 2 * c])
            if q < pairs:
                low = dot(rows(f, q, n), wide[2 * c :])
                y = low if y is None else y + low
            y = gathered(y, n, cols, n2)
            keep = jnp.concatenate([d_ref[f : f + 1]] * 2, axis=-1).reshape(1, 1, n2)
            state = y if f == 0 else keep * state + y
            s_ref[f, q : q + n] = state


def edge_kernel(x_ref, lo_ref, hi_ref, fl_ref, fr_ref, e_ref, top_ref, bot_ref):
    frames, pairs, _, cols, c = x_ref.shape
    column, _, tcols = place()
    has_left, has_right = column > 0, column < tcols - 1
    for f in range(frames):
        for r in range(2):
            lane = pl.ds(r * c, c)
            e_ref[f, :, 0:2, lane] = hi_ref[f, :, r]
            e_ref[f, :, 2:4, lane] = jnp.where(has_right, fr_ref[f, :, r], 0).astype(BF)
            e_ref[f, :, 4:6, lane] = jnp.where(has_left, fl_ref[f, :, r], 0).astype(BF)
            e_ref[f, :, 6:8, lane] = lo_ref[f, :, r]
            top_ref[f, 0:cols, lane] = x_ref[f, 0, r]
            bot_ref[f, 0:cols, lane] = x_ref[f, pairs - 1, r]
        top_ref[f, cols:, :] = e_ref[f, 0]
        bot_ref[f, cols:, :] = e_ref[f, pairs - 1]


def ring_kernel(e_ref, up_ref, dn_ref, s_ref, w_ref, d_ref, r_ref, c_ref, m_ref, wide):
    frames, pairs, _, c2 = e_ref.shape
    n2 = r_ref.shape[3]
    cols = up_ref.shape[1] - 8
    _, row, _ = place()
    has_up, has_dn = row > 0, row < TROWS - 1
    spread(w_ref, wide)
    state = None
    rim = [None, None]
    for f in range(frames):
        keep = jnp.concatenate([d_ref[f : f + 1]] * 2, axis=-1).reshape(1, 1, n2)
        e = e_ref[f].reshape(pairs * 8, c2)
        high, low = dot(e, wide[:c2]), dot(e, wide[c2:])
        blank = jnp.zeros((8, 3 * n2), F32)
        y = jnp.concatenate([blank, high]) + jnp.concatenate([low, blank])
        y = gathered_edge(y, pairs + 1, n2)
        state = y if f == 0 else keep * state + y
        r_ref[f] = state
        for side, (ref, there) in enumerate(((up_ref, has_up), (dn_ref, has_dn))):
            v = jnp.where(there, ref[f], 0).astype(BF)
            y = dot(v, wide[c2:] if side else wide[:c2])
            mid = gathered(y[:cols], 1, cols, n2)
            end = gathered_edge(y[cols:], 1, n2)
            y = jnp.concatenate([mid, end], axis=1)
            rim[side] = y if f == 0 else keep * rim[side] + y
            c_ref[f, side : side + 1] = rim[side][:, :cols]
            at = side * pairs
            r_ref[f, at : at + 1] = r_ref[f, at : at + 1] + rim[side][:, cols:]
    last = frames - 1
    whole, ends = merged(s_ref, r_ref, c_ref, last)
    m_ref[:, :cols] = whole.astype(BF)
    m_ref[:, cols:] = ends.astype(BF)


def merged(s_ref, r_ref, c_ref, f):
    rim = c_ref[f]
    body = s_ref[f]
    n, cols, n2 = body.shape
    body = jnp.concatenate([body[:1] + rim[:1], body[1 : n - 1], body[n - 1 :] + rim[1:]])
    ends = r_ref[f]
    col = lax.broadcasted_iota(jnp.int32, ends.shape, 1)
    first = body[:, :8] + jnp.where(col == 0, pltpu.roll(ends, 2, 1), 0.0)
    final = body[:, cols - 8 :] + jnp.where(col == 7, pltpu.roll(ends, 6, 1), 0.0)
    return jnp.concatenate([first, body[:, 8 : cols - 8], final], axis=1), ends


def read_kernel(
    s_ref, r_ref, c_ref, m_ref, w_ref, d_ref, skip_ref, x_ref, o_ref, wide, held, ends_held, out, sems
):
    frames, pairs, _, cols, c = x_ref.shape
    n2 = s_ref.shape[3]
    spread(w_ref, wide)
    column, row, tcols = place()
    later = (lax.axis_index("tm") > 0).astype(F32)
    has_up, has_dn = row > 0, row < TROWS - 1
    has_left, has_right = column > 0, column < tcols - 1
    gain = jnp.concatenate([skip_ref[...]] * 2, axis=-1)
    factor = jnp.full((1, n2), 1.0, F32) * later
    lane = lax.broadcasted_iota(jnp.int32, (1, 1, n2), 2)
    copies = []
    for f in range(frames):
        factor = factor * jnp.concatenate([d_ref[f : f + 1]] * 2, axis=-1)
        body, ends = merged(s_ref, r_ref, c_ref, f)
        far = factor.reshape(1, 1, n2)
        body = body + far * m_ref[:, :cols].astype(F32)
        ends = ends + far * m_ref[:, cols:].astype(F32)
        col = lax.broadcasted_iota(jnp.int32, ends.shape, 1)
        ends = jnp.where(((col == 2) & has_right) | ((col == 5) & has_left), ends, 0.0)
        for value, ref in ((body, held), (ends, ends_held)):
            ref[...] = value.astype(BF)
            ref[0:1] = jnp.where(has_up | (lane >= n2 // 2), value[0:1], 0.0).astype(BF)
            ref[pairs : pairs + 1] = jnp.where(
                has_dn | (lane < n2 // 2), value[pairs : pairs + 1], 0.0
            ).astype(BF)
        for p in range(0, pairs, BLOCK):
            n = min(BLOCK, pairs - p)
            y = dot(held[p : p + n].reshape(n * cols, n2), wide[:n2])
            y = y + dot(held[p + 1 : p + 1 + n].reshape(n * cols, n2), wide[n2:])
            y = gathered(y, n, cols, n2)
            e = dot(ends_held[p : p + n].reshape(n * 8, n2), wide[:n2])
            e = e + dot(ends_held[p + 1 : p + 1 + n].reshape(n * 8, n2), wide[n2:])
            e = e.reshape(n, 8, 3 * n2)
            col = lax.broadcasted_iota(jnp.int32, (n, 8, n2), 1)
            first = y[:, :8] + jnp.where(col == 0, pltpu.roll(e[:, :, :n2], 3, 1), 0.0)
            final = y[:, cols - 8 :] + jnp.where(col == 7, pltpu.roll(e[:, :, 2 * n2 :], 5, 1), 0.0)
            y = jnp.concatenate([first, y[:, 8 : cols - 8], final], axis=1)
            half = n2 // 2
            for r in range(2):
                v = y[:, :, r * half : (r + 1) * half]
                v = v + gain[:, :half].reshape(1, 1, half) * x_ref[f, p : p + n, r].astype(F32)
                out[f, p : p + n, r] = v.astype(BF)
        copy = pltpu.make_async_copy(out.at[f], o_ref.at[f], sems.at[f])
        copy.start()
        copies.append(copy)
    for copy in copies:
        copy.wait()


def call(body, outs, ins, scratch=(), out_specs=None, name=None):
    return pl.pallas_call(
        body,
        out_shape=outs,
        in_specs=[VM] * len(ins),
        out_specs=out_specs if out_specs is not None else jax.tree.map(lambda _: VM, outs),
        scratch_shapes=list(scratch),
        compiler_params=pltpu.CompilerParams(vmem_limit_bytes=LIMIT),
        name=name,
    )(*ins)


def per_device(frames, w_in, w_out, decay, skip):
    shape = jax.ShapeDtypeStruct
    count, _, rows, cols, c = frames.shape
    n2 = 2 * w_in.shape[3]
    pairs = rows // 2
    tcols = lax.axis_size("tile") // TROWS
    video = frames.reshape(count, pairs, 2, cols, c)
    low, high = video[:, :, :, :2], video[:, :, :, cols - 2 :]
    from_left = shifted(high, "tile", 1)
    from_right = shifted(low, "tile", -1)
    local = call(
        main_kernel,
        shape((count, pairs + 1, cols, n2), F32),
        (video, w_in, decay),
        [pltpu.VMEM((4 * c, 3 * n2), BF)],
        name="main",
    )
    edge, top, bottom = call(
        edge_kernel,
        (
            shape((count, pairs, 8, 2 * c), BF),
            shape((count, cols + 8, 2 * c), BF),
            shape((count, cols + 8, 2 * c), BF),
        ),
        (video, low, high, from_left, from_right),
        name="edge",
    )
    above = shifted(bottom, "tile", tcols)
    below = shifted(top, "tile", -tcols)
    ends, rim, message = call(
        ring_kernel,
        (
            shape((count, pairs + 1, 8, n2), F32),
            shape((count, 2, cols, n2), F32),
            shape((pairs + 1, cols + 8, n2), BF),
        ),
        (edge, above, below, local, w_in, decay),
        [pltpu.VMEM((4 * c, 3 * n2), BF)],
        name="ring",
    )
    before = shifted(message, "tm", 1)
    mixed = call(
        read_kernel,
        shape((count, pairs, 2, cols, c), BF),
        (local, ends, rim, before, w_out, decay, skip.reshape(1, c), video),
        [
            pltpu.VMEM((2 * n2, 3 * 2 * c), BF),
            pltpu.VMEM((pairs + 1, cols, n2), BF),
            pltpu.VMEM((pairs + 1, 8, n2), BF),
            pltpu.VMEM((count, pairs, 2, cols, c), BF),
            pltpu.SemaphoreType.DMA((count,)),
        ],
        out_specs=pl.BlockSpec(memory_space=pl.ANY),
        name="read",
    )
    return mixed.reshape(count, 1, rows, cols, c)


def solution(mesh):
    return jax.shard_map(
        per_device,
        mesh=mesh,
        in_specs=(P("tm", "tile", None, None, None), P(), P(), P("tm", None), P()),
        out_specs=P("tm", "tile", None, None, None),
        check_vma=False,
    )
```

time: 78.7 us -> 31.8 us (0.40)
  other arithmetic: 18.5 us -> 0 us
  waiting for transfers between devices: 23.3 us -> 5.65 us
  matrix products: 12.7 us -> 0 us
  Pallas kernels: 0 us -> 11.8 us
  local copies, waits for them, and re-layouts: 8.67 us -> 3.09 us
  starting transfers between devices: 15 us -> 11 us
    ppermute x9 -> x5, waiting for transfers between devices: 23.3 us -> 5.65 us  [shifted(): lax.ppermute(value, axis, [(i, (i + by) % size) for i in range(size)])]
    concatenate x6 -> x0, other arithmetic: 13.6 us -> none  [the longest x2 7.59 us: bordered(): return jnp.concatenate([upper_rim, widened, lower_rim], axis=1)]
    dot_general x18 -> x0, matrix products: 12.7 us -> none  [convolve(): jnp.dot(window, weight[shift_row, shift_col], preferred_element_type=jnp....]
    pallas_call x0 -> x4, Pallas kernels: none -> 11.8 us  [call(): pl.pallas_call(body, out_shape=outs, in_specs=[VM] * len(ins), out_specs=...]
    slice x6 -> x1, local copies, waits for them, and re-layouts: 7.81 us -> 1.47 us  [per_device(): low, high = (video[:, :, :, :2], video[:, :, :, cols - 2:])]
    ppermute x9 -> x5, starting transfers between devices: 15 us -> 11 us  [shifted(): lax.ppermute(value, axis, [(i, (i + by) % size) for i in range(size)])]
    convert_element_type x2 -> x0, other arithmetic: 2.65 us -> none  [the longest x1 2.12 us: per_device(): return mixed.astype(jnp.bfloat16)[:, None]]
    unnamed x8 -> x12, local copies, waits for them, and re-layouts: 0.02 us -> 1.62 us
  transfers between devices with their start and end apart: 9 -> 5, of which waited for: 7 -> 2; matrix products, arithmetic and copies ran while one was open for 9% -> 0% of each run, Pallas kernels for 0% -> 13%
where the time goes in v1:
time: 31.8 us; the launch traced here: 31.7 us
  Pallas kernels  11.8 us (37%)
  starting transfers between devices  11 us (35%)
  waiting for transfers between devices  5.65 us (18%)
  local copies, waits for them, and re-layouts  3.09 us (10%)
    pallas_call x4, Pallas kernels, call(): pl.pallas_call(body, out_shape=outs, in_specs=[VM] * len(ins), out_specs=...  11.8 us
    ppermute x5, starting transfers between devices, shifted(): lax.ppermute(value, axis, [(i, (i + by) % size) for i in range(size)])  11 us
    ppermute x5, waiting for transfers between devices, shifted(): lax.ppermute(value, axis, [(i, (i + by) % size) for i in range(size)])  5.65 us
    unnamed x12, local copies, waits for them, and re-layouts  1.62 us
    slice x1, local copies, waits for them, and re-layouts, per_device(): low, high = (video[:, :, :, :2], video[:, :, :, cols - 2:])  1.47 us
  transfers between devices with their start and end apart: 5, of which 2 were waited for; matrix products, arithmetic and copies ran while one was open for 0% of the time, Pallas kernels for 13%

profile of v1, /device:TPU:0, one launch (start us, length us, event | category | flops | bytes accessed | tf_op | source)
XLA Modules:
  0.0 31.7 jit_solution(14796953461844783456)
XLA Ops:
  0.0 1.5 %fusion = (bf16[4,32,2,2,128]{4,3,2,1,0:T(2,128)(2,1)S(1)}, bf16[4,32,2,2,128]{4,3,2,1,0:T(2,128)(2,1)S(1)}) fusion(bf16[4,32,2,32,128]{4,3,2,1,0:T(8,128)(2,1)} %bitcast.5), kind=kLoop, calls=%fused_computation | loop fusion | bytes 524288 | tf_op jit(solution)/shard_map/slice | solution.py:227
  1.5 3.0 %collective-permute-start = (bf16[4,32,2,2,128]{4,3,2,1,0:T(2,128)(2,1)S(1)}, bf16[4,32,2,2,128]{4,3,2,1,0:T(2,128)(2,1)S(1)}, u32[]{:S(2)}, u32[]{:S(2)}) collective-permute-start(bf16[4,32,2,2,128]{4,3,2,1,0:T(2,128)(2,1)S(1)} %get-tuple-element.17.hi_ref), channel_id=1, source_target_pairs={{0,1},{1,2},{2,3},{3,4},{4,5},{5,6},{6,7},{7,8},{8,9},{9,10},{10,1... | collective-permute-start | bytes 393224 | tf_op jit(solution)/shard_map/ppermute | solution.py:20
  4.5 4.1 %collective-permute-start.1 = (bf16[4,32,2,2,128]{4,3,2,1,0:T(2,128)(2,1)S(1)}, bf16[4,32,2,2,128]{4,3,2,1,0:T(2,128)(2,1)S(1)}, u32[]{:S(2)}, u32[]{:S(2)}) collective-permute-start(bf16[4,32,2,2,128]{4,3,2,1,0:T(2,128)(2,1)S(1)} %get-tuple-element.18.lo_ref), channel_id=1, source_target_pairs={{0,15},{1,0},{2,1},{3,2},{4,3},{5,4},{6,5},{7,6},{8,7},{9,8},{10,9... | collective-permute-start | bytes 393224 | tf_op jit(solution)/shard_map/ppermute | solution.py:20
  8.6 3.5 %collective-permute-done.fl_ref = bf16[4,32,2,2,128]{4,3,2,1,0:T(2,128)(2,1)S(1)} collective-permute-done((bf16[4,32,2,2,128]{4,3,2,1,0:T(2,128)(2,1)S(1)}, bf16[4,32,2,2,128]{4,3,2,1,0:T(2,128)(2,1)S(1)}, u32[]{:S(2)}, u32[]{:S(2)}) %collective-permute-start) | collective-permute-done | bytes 131104 | tf_op jit(solution)/shard_map/ppermute | solution.py:20
  12.1 0.0 collective-permute-done.1.fr_ref
  12.1 1.6 %copy-done = bf16[4,1,64,32,128]{4,3,2,1,0:T(8,128)(2,1)S(1)} copy-done((bf16[4,1,64,32,128]{4,3,2,1,0:T(8,128)(2,1)S(1)}, bf16[4,1,64,32,128]{4,3,2,1,0:T(8,128)(2,1)}, u32[]{:S(2)}) %copy-start) | copy-done | bytes 2097176
  13.7 0.6 %edge.1 = (bf16[4,32,8,256]{3,2,1,0:T(8,128)(2,1)S(1)}, bf16[4,40,256]{2,1,0:T(8,128)(2,1)S(1)}, bf16[4,40,256]{2,1,0:T(8,128)(2,1)S(1)}) custom-call(bf16[4,32,2,32,128]{4,3,2,1,0:T(8,128)(2,1)S(1)} %bitcast.6, bf16[4,32,2,2,128]{4,3,2,1,0:T(2,128)(2,1)S(1)} %get-tuple-element.18.lo_ref, bf16[4,32,2,2,128]{4,3,2,1,0:T(2,128)(2,1)S(1)} %get-tuple-element.17.hi_ref, ...), custom_call_target="tpu_custom_call" | custom-call | tf_op jit(solution)/shard_map/edge/pallas_call | solution.py:209
  14.3 1.5 %collective-permute-start.2 = (bf16[4,40,256]{2,1,0:T(8,128)(2,1)S(1)}, bf16[4,40,256]{2,1,0:T(8,128)(2,1)S(1)}, u32[]{:S(2)}, u32[]{:S(2)}) collective-permute-start(bf16[4,40,256]{2,1,0:T(8,128)(2,1)S(1)} %get-tuple-element.12), channel_id=1, source_target_pairs={{0,4},{1,5},{2,6},{3,7},{4,8},{5,9},{6,10},{7,11},{8,12},{9,13},{1... | collective-permute-start | bytes 245768 | tf_op jit(solution)/shard_map/ppermute | solution.py:20
  15.9 2.3 %collective-permute-start.3 = (bf16[4,40,256]{2,1,0:T(8,128)(2,1)S(1)}, bf16[4,40,256]{2,1,0:T(8,128)(2,1)S(1)}, u32[]{:S(2)}, u32[]{:S(2)}) collective-permute-start(bf16[4,40,256]{2,1,0:T(8,128)(2,1)S(1)} %get-tuple-element.13), channel_id=1, source_target_pairs={{0,12},{1,13},{2,14},{3,15},{4,0},{5,1},{6,2},{7,3},{8,4},{9,5},{1... | collective-permute-start | bytes 245768 | tf_op jit(solution)/shard_map/ppermute | solution.py:20
  18.2 0.0 copy-done.4
  18.2 0.0 copy-done.2
  18.2 4.0 %main.1.s_ref = f32[4,33,32,256]{3,2,1,0:T(8,128)S(1)} custom-call(bf16[4,32,2,32,128]{4,3,2,1,0:T(8,128)(2,1)S(1)} %bitcast.7, bf16[3,3,128,128]{3,2,1,0:T(8,128)(2,1)S(1)} %copy-done.2, f32[4,128]{1,0:T(4,128)S(1)} %copy-done.4), custom_call_target="tpu_custom_call" | custom-call | tf_op jit(solution)/shard_map/main/pallas_call | solution.py:209
  22.2 0.0 collective-permute-done.2.up_ref
  22.2 0.0 collective-permute-done.3.dn_ref
  22.2 0.0 copy-start.1
  22.2 0.0 copy-start.3
  22.2 0.0 copy-start.5
  22.2 1.7 %ring.1 = (f32[4,33,8,256]{3,2,1,0:T(8,128)S(1)}, f32[4,2,32,256]{3,2,1,0:T(8,128)S(1)}, bf16[33,40,256]{2,1,0:T(8,128)(2,1)S(1)}) custom-call(bf16[4,32,8,256]{3,2,1,0:T(8,128)(2,1)S(1)} %get-tuple-element.11.e_ref, bf16[4,40,256]{2,1,0:T(8,128)(2,1)S(1)} %collective-permute-done.2.up_ref, bf16[4,40,256]{2,1,0:T(8,128)(2,1)S(1)} %collective-permute-done.3.dn_ref, ...), custom_call_target="tpu_custom_call" | custom-call | tf_op jit(solution)/shard_map/ring/pallas_call | solution.py:209
  24.0 0.1 collective-permute-start.4
  24.1 2.1 %collective-permute-done.4.m_ref = bf16[33,40,256]{2,1,0:T(8,128)(2,1)S(1)} collective-permute-done((bf16[33,40,256]{2,1,0:T(8,128)(2,1)S(1)}, bf16[33,40,256]{2,1,0:T(8,128)(2,1)S(1)}, u32[]{:S(2)}, u32[]{:S(2)}) %collective-permute-start.4) | collective-permute-done | bytes 675872 | tf_op jit(solution)/shard_map/ppermute | solution.py:20
  26.2 0.0 copy-done.1
  26.2 0.0 copy-done.3
  26.2 0.0 copy-done.5
  26.2 5.5 %read.1 = bf16[4,32,2,32,128]{4,3,2,1,0:T(8,128)(2,1)} custom-call(f32[4,33,32,256]{3,2,1,0:T(8,128)S(1)} %main.1.s_ref, f32[4,33,8,256]{3,2,1,0:T(8,128)S(1)} %get-tuple-element.14.r_ref, f32[4,2,32,256]{3,2,1,0:T(8,128)S(1)} %get-tuple-element.15.c_ref, bf16[33,40,256]{2,1,0:T(8,128)(2,1)S(1)} %collective-permute-done.4.m_ref, ...), custom_call_target="tpu_custom_call" | custom-call | tf_op jit(solution)/shard_map/read/pallas_call | solution.py:209
  (3 shorter events, 0.0 us)
Async XLA Ops:
  0.0 18.2 %copy-start.4 = (f32[4,128]{1,0:T(4,128)S(1)}, f32[4,128]{1,0:T(4,128)}, u32[]{:S(2)}) copy-start(f32[4,128]{1,0:T(4,128)} %d_ref.5) | copy-start | bytes 6148
  0.0 18.2 %copy-start.2 = (bf16[3,3,128,128]{3,2,1,0:T(8,128)(2,1)S(1)}, bf16[3,3,128,128]{3,2,1,0:T(8,128)(2,1)}, u32[]{:S(2)}) copy-start(bf16[3,3,128,128]{3,2,1,0:T(8,128)(2,1)} %w_ref.4) | copy-start | bytes 884740
  1.5 10.6 %collective-permute-start = (bf16[4,32,2,2,128]{4,3,2,1,0:T(2,128)(2,1)S(1)}, bf16[4,32,2,2,128]{4,3,2,1,0:T(2,128)(2,1)S(1)}, u32[]{:S(2)}, u32[]{:S(2)}) collective-permute-start(bf16[4,32,2,2,128]{4,3,2,1,0:T(2,128)(2,1)S(1)} %get-tuple-element.17.hi_ref), channel_id=1, source_target_pairs={{0,1},{1,2},{2,3},{3,4},{4,5},{5,6},{6,7},{7,8},{8,9},{9,10},{10,1... | collective-permute-start | bytes 393224 | tf_op jit(solution)/shard_map/ppermute | solution.py:20
  4.5 7.6 %collective-permute-start.1 = (bf16[4,32,2,2,128]{4,3,2,1,0:T(2,128)(2,1)S(1)}, bf16[4,32,2,2,128]{4,3,2,1,0:T(2,128)(2,1)S(1)}, u32[]{:S(2)}, u32[]{:S(2)}) collective-permute-start(bf16[4,32,2,2,128]{4,3,2,1,0:T(2,128)(2,1)S(1)} %get-tuple-element.18.lo_ref), channel_id=1, source_target_pairs={{0,15},{1,0},{2,1},{3,2},{4,3},{5,4},{6,5},{7,6},{8,7},{9,8},{10,9... | collective-permute-start | bytes 393224 | tf_op jit(solution)/shard_map/ppermute | solution.py:20
  12.1 1.6 %copy-start = (bf16[4,1,64,32,128]{4,3,2,1,0:T(8,128)(2,1)S(1)}, bf16[4,1,64,32,128]{4,3,2,1,0:T(8,128)(2,1)}, u32[]{:S(2)}) copy-start(bf16[4,1,64,32,128]{4,3,2,1,0:T(8,128)(2,1)} %param.5) | copy-start | bytes 6291460
  14.3 7.9 %collective-permute-start.2 = (bf16[4,40,256]{2,1,0:T(8,128)(2,1)S(1)}, bf16[4,40,256]{2,1,0:T(8,128)(2,1)S(1)}, u32[]{:S(2)}, u32[]{:S(2)}) collective-permute-start(bf16[4,40,256]{2,1,0:T(8,128)(2,1)S(1)} %get-tuple-element.12), channel_id=1, source_target_pairs={{0,4},{1,5},{2,6},{3,7},{4,8},{5,9},{6,10},{7,11},{8,12},{9,13},{1... | collective-permute-start | bytes 245768 | tf_op jit(solution)/shard_map/ppermute | solution.py:20
  15.9 6.3 %collective-permute-start.3 = (bf16[4,40,256]{2,1,0:T(8,128)(2,1)S(1)}, bf16[4,40,256]{2,1,0:T(8,128)(2,1)S(1)}, u32[]{:S(2)}, u32[]{:S(2)}) collective-permute-start(bf16[4,40,256]{2,1,0:T(8,128)(2,1)S(1)} %get-tuple-element.13), channel_id=1, source_target_pairs={{0,12},{1,13},{2,14},{3,15},{4,0},{5,1},{6,2},{7,3},{8,4},{9,5},{1... | collective-permute-start | bytes 245768 | tf_op jit(solution)/shard_map/ppermute | solution.py:20
  22.2 4.0 %copy-start.1 = (bf16[4,1,64,32,128]{4,3,2,1,0:T(8,128)(2,1)S(1)}, bf16[4,1,64,32,128]{4,3,2,1,0:T(8,128)(2,1)}, u32[]{:S(2)}) copy-start(bf16[4,1,64,32,128]{4,3,2,1,0:T(8,128)(2,1)} %param.5) | copy-start | bytes 6291460
  22.2 4.0 %copy-start.3 = (bf16[3,3,128,128]{3,2,1,0:T(8,128)(2,1)S(1)}, bf16[3,3,128,128]{3,2,1,0:T(8,128)(2,1)}, u32[]{:S(2)}) copy-start(bf16[3,3,128,128]{3,2,1,0:T(8,128)(2,1)} %w_ref.5) | copy-start | bytes 884740
  22.2 4.0 %copy-start.5 = (f32[128]{0:T(128)S(1)}, f32[128]{0:T(128)}, u32[]{:S(2)}) copy-start(f32[128]{0:T(128)} %param.9) | copy-start | bytes 1540
  24.0 2.2 %collective-permute-start.4 = (bf16[33,40,256]{2,1,0:T(8,128)(2,1)S(1)}, bf16[33,40,256]{2,1,0:T(8,128)(2,1)S(1)}, u32[]{:S(2)}, u32[]{:S(2)}) collective-permute-start(bf16[33,40,256]{2,1,0:T(8,128)(2,1)S(1)} %get-tuple-element.16), channel_id=1, source_target_pairs={{0,16},{16,0},{1,17},{17,1},{2,18},{18,2},{3,19},{19,3},{4,20},{20... | collective-permute-start | bytes 2027528 | tf_op jit(solution)/shard_map/ppermute | solution.py:20

commit v2 on v1

--- a/solution.py
+++ b/solution.py
@@ -13,11 +13,22 @@
 LIMIT = 24 << 20
 BLOCK = 16
 VM = pl.BlockSpec(memory_space=pltpu.VMEM)
-
-
-def shifted(value, axis, by):
-    size = lax.axis_size(axis)
-    return lax.ppermute(value, axis, [(i, (i + by) % size) for i in range(size)])
+ANY = pl.BlockSpec(memory_space=pl.ANY)
+
+
+def swapped(value, across, first):
+    count = lax.axis_size("tile")
+    tcols = count // TROWS
+    pairs = []
+    for number in range(count):
+        row, column = divmod(number, tcols)
+        at, size = (column, tcols) if across else (row, TROWS)
+        other = at + 1 if at >= first and (at - first) % 2 == 0 else at - 1
+        if not first <= other < size:
+            other = at
+        there = row * tcols + other if across else other * tcols + column
+        pairs.append(((number + 1) % count, (there + 1) % count))
+    return lax.ppermute(value, "tile", pairs)
 
 
 def place():
@@ -90,27 +101,51 @@
             s_ref[f, q : q + n] = state
 
 
-def edge_kernel(x_ref, lo_ref, hi_ref, fl_ref, fr_ref, e_ref, top_ref, bot_ref):
+def pack_kernel(f_ref, x_ref, a_ref, b_ref, sems):
+    frames, _, _, cols, _ = x_ref.shape
+    column, _, _ = place()
+    even = lax.rem(column, 2) == 0
+    copies = [
+        pltpu.make_async_copy(f_ref.at[f], x_ref.at[f], sems.at[f]) for f in range(frames)
+    ]
+    for copy in copies:
+        copy.start()
+    for f, copy in enumerate(copies):
+        copy.wait()
+        low, high = x_ref[f, :, :, :2], x_ref[f, :, :, cols - 2 :]
+        a_ref[f] = jnp.where(even, high, low)
+        b_ref[f] = jnp.where(even, low, high)
+
+
+def edge_kernel(x_ref, fa_ref, fb_ref, e_ref, a_ref, b_ref):
     frames, pairs, _, cols, c = x_ref.shape
-    column, _, tcols = place()
+    column, row, tcols = place()
     has_left, has_right = column > 0, column < tcols - 1
+    even = lax.rem(column, 2) == 0
+    upper = lax.rem(row, 2) == 0
     for f in range(frames):
         for r in range(2):
             lane = pl.ds(r * c, c)
-            e_ref[f, :, 0:2, lane] = hi_ref[f, :, r]
-            e_ref[f, :, 2:4, lane] = jnp.where(has_right, fr_ref[f, :, r], 0).astype(BF)
-            e_ref[f, :, 4:6, lane] = jnp.where(has_left, fl_ref[f, :, r], 0).astype(BF)
-            e_ref[f, :, 6:8, lane] = lo_ref[f, :, r]
-            top_ref[f, 0:cols, lane] = x_ref[f, 0, r]
-            bot_ref[f, 0:cols, lane] = x_ref[f, pairs - 1, r]
-        top_ref[f, cols:, :] = e_ref[f, 0]
-        bot_ref[f, cols:, :] = e_ref[f, pairs - 1]
-
-
-def ring_kernel(e_ref, up_ref, dn_ref, s_ref, w_ref, d_ref, r_ref, c_ref, m_ref, wide):
+            fa, fb = fa_ref[f, :, r], fb_ref[f, :, r]
+            right = jnp.where(has_right, jnp.where(even, fa, fb), 0).astype(BF)
+            left = jnp.where(has_left, jnp.where(even, fb, fa), 0).astype(BF)
+            e_ref[f, :, 0:2, lane] = x_ref[f, :, r, cols - 2 :]
+            e_ref[f, :, 2:4, lane] = right
+            e_ref[f, :, 4:6, lane] = left
+            e_ref[f, :, 6:8, lane] = x_ref[f, :, r, :2]
+            top, bottom = x_ref[f, 0, r], x_ref[f, pairs - 1, r]
+            a_ref[f, 0:cols, lane] = jnp.where(upper, bottom, top)
+            b_ref[f, 0:cols, lane] = jnp.where(upper, top, bottom)
+        top, bottom = e_ref[f, 0], e_ref[f, pairs - 1]
+        a_ref[f, cols:, :] = jnp.where(upper, bottom, top)
+        b_ref[f, cols:, :] = jnp.where(upper, top, bottom)
+
+
+def ring_kernel(e_ref, va_ref, vb_ref, s_ref, w_ref, d_ref, r_ref, c_ref, m_ref, wide):
     frames, pairs, _, c2 = e_ref.shape
     n2 = r_ref.shape[3]
-    cols = up_ref.shape[1] - 8
+    cols = va_ref.shape[1] - 8
+    upper = lax.rem(place()[1], 2) == 0
     _, row, _ = place()
     has_up, has_dn = row > 0, row < TROWS - 1
     spread(w_ref, wide)
@@ -125,8 +160,10 @@
         y = gathered_edge(y, pairs + 1, n2)
         state = y if f == 0 else keep * state + y
         r_ref[f] = state
-        for side, (ref, there) in enumerate(((up_ref, has_up), (dn_ref, has_dn))):
-            v = jnp.where(there, ref[f], 0).astype(BF)
+        va, vb = va_ref[f], vb_ref[f]
+        near = (jnp.where(upper, vb, va), jnp.where(upper, va, vb))
+        for side, there in enumerate((has_up, has_dn)):
+            v = jnp.where(there, near[side], 0).astype(BF)
             y = dot(v, wide[c2:] if side else wide[:c2])
             mid = gathered(y[:cols], 1, cols, n2)
             end = gathered_edge(y[cols:], 1, n2)
@@ -205,14 +242,14 @@
         copy.wait()
 
 
-def call(body, outs, ins, scratch=(), out_specs=None, name=None):
+def call(body, outs, ins, scratch=(), in_specs=None, out_specs=None, name=None, limit=LIMIT):
     return pl.pallas_call(
         body,
         out_shape=outs,
-        in_specs=[VM] * len(ins),
+        in_specs=in_specs or [VM] * len(ins),
         out_specs=out_specs if out_specs is not None else jax.tree.map(lambda _: VM, outs),
         scratch_shapes=list(scratch),
-        compiler_params=pltpu.CompilerParams(vmem_limit_bytes=LIMIT),
+        compiler_params=pltpu.CompilerParams(vmem_limit_bytes=limit),
         name=name,
     )(*ins)
 
@@ -222,30 +259,36 @@
     count, _, rows, cols, c = frames.shape
     n2 = 2 * w_in.shape[3]
     pairs = rows // 2
-    tcols = lax.axis_size("tile") // TROWS
     video = frames.reshape(count, pairs, 2, cols, c)
-    low, high = video[:, :, :, :2], video[:, :, :, cols - 2 :]
-    from_left = shifted(high, "tile", 1)
-    from_right = shifted(low, "tile", -1)
+    side = shape((count, pairs, 2, 2, c), BF)
+    across = shape((count, cols + 8, 2 * c), BF)
+    here, side_a, side_b = call(
+        pack_kernel,
+        (shape(video.shape, BF), side, side),
+        (pltpu.with_memory_space_constraint(video, pltpu.HBM),),
+        [pltpu.SemaphoreType.DMA((count,))],
+        in_specs=[pl.BlockSpec(memory_space=pltpu.HBM)],
+        name="pack",
+        limit=LIMIT,
+    )
+    from_a = swapped(side_a, True, 0)
+    from_b = swapped(side_b, True, 1)
     local = call(
         main_kernel,
         shape((count, pairs + 1, cols, n2), F32),
-        (video, w_in, decay),
+        (here, w_in, decay),
         [pltpu.VMEM((4 * c, 3 * n2), BF)],
         name="main",
     )
-    edge, top, bottom = call(
+    from_a, from_b, local = lax.optimization_barrier((from_a, from_b, local))
+    edge, row_a, row_b = call(
         edge_kernel,
-        (
-            shape((count, pairs, 8, 2 * c), BF),
-            shape((count, cols + 8, 2 * c), BF),
-            shape((count, cols + 8, 2 * c), BF),
-        ),
-        (video, low, high, from_left, from_right),
+        (shape((count, pairs, 8, 2 * c), BF), across, across),
+        (here, from_a, from_b),
         name="edge",
     )
-    above = shifted(bottom, "tile", tcols)
-    below = shifted(top, "tile", -tcols)
+    rows_a = swapped(row_a, False, 0)
+    rows_b = swapped(row_b, False, 1)
     ends, rim, message = call(
         ring_kernel,
         (
@@ -253,15 +296,16 @@
             shape((count, 2, cols, n2), F32),
             shape((pairs + 1, cols + 8, n2), BF),
         ),
-        (edge, above, below, local, w_in, decay),
+        (edge, rows_a, rows_b, local, w_in, decay),
         [pltpu.VMEM((4 * c, 3 * n2), BF)],
         name="ring",
     )
-    before = shifted(message, "tm", 1)
+    groups = lax.axis_size("tm")
+    before = lax.ppermute(message, "tm", [(i, (i + 1) % groups) for i in range(groups)])
     mixed = call(
         read_kernel,
         shape((count, pairs, 2, cols, c), BF),
-        (local, ends, rim, before, w_out, decay, skip.reshape(1, c), video),
+        (local, ends, rim, before, w_out, decay, skip.reshape(1, c), here),
         [
             pltpu.VMEM((2 * n2, 3 * 2 * c), BF),
             pltpu.VMEM((pairs + 1, cols, n2), BF),
@@ -269,7 +313,7 @@
             pltpu.VMEM((count, pairs, 2, cols, c), BF),
             pltpu.SemaphoreType.DMA((count,)),
         ],
-        out_specs=pl.BlockSpec(memory_space=pl.ANY),
+        out_specs=ANY,
         name="read",
     )
     return mixed.reshape(count, 1, rows, cols, c)

time: 31.8 us -> 30.5 us (0.959)
  local copies, waits for them, and re-layouts: 3.09 us -> 0.01 us
  starting transfers between devices: 11 us -> 8.93 us
  waiting for transfers between devices: 5.65 us -> 7.63 us
  Pallas kernels: 11.8 us -> 13.7 us
    ppermute x5, starting transfers between devices: 11 us -> 8.93 us  [the longest x4 8.86 us: swapped(): return lax.ppermute(value, 'tile', pairs)]
    ppermute x5, waiting for transfers between devices: 5.65 us -> 7.63 us  [the longest x4 5.52 us: swapped(): return lax.ppermute(value, 'tile', pairs)]
    pallas_call x4 -> x5, Pallas kernels: 11.8 us -> 13.7 us  [call(): pl.pallas_call(body, out_shape=outs, in_specs=in_specs or [VM] * len(ins)...]
    unnamed x12 -> x8, local copies, waits for them, and re-layouts: 1.62 us -> 0.01 us
    slice x1 -> x0, local copies, waits for them, and re-layouts: 1.47 us -> none  [per_device(): low, high = (video[:, :, :, :2], video[:, :, :, cols - 2:])]
where the time goes in v2:
time: 30.5 us; the launch traced here: 30.4 us
  Pallas kernels  13.7 us (45%)
  starting transfers between devices  8.93 us (29%)
  waiting for transfers between devices  7.63 us (25%)
    pallas_call x5, Pallas kernels, call(): pl.pallas_call(body, out_shape=outs, in_specs=in_specs or [VM] * len(ins)...  13.7 us
    ppermute x4, starting transfers between devices, swapped(): return lax.ppermute(value, 'tile', pairs)  8.86 us
    ppermute x4, waiting for transfers between devices, swapped(): return lax.ppermute(value, 'tile', pairs)  5.52 us
    ppermute x1, waiting for transfers between devices, per_device(): lax.ppermute(message, 'tm', [(i, (i + 1) % groups) for i in range(groups)])  2.11 us
  transfers between devices with their start and end apart: 5, of which 2 were waited for; matrix products, arithmetic and copies ran while one was open for 0% of the time, Pallas kernels for 13%

profile of v2, /device:TPU:0, one launch (start us, length us, event | category | flops | bytes accessed | tf_op | source)
XLA Modules:
  0.0 30.4 jit_solution(6369857896291887144)
XLA Ops:
  0.0 0.0 copy-start.2
  0.0 0.0 copy-start
  0.0 1.7 %pack.1 = (bf16[4,32,2,32,128]{4,3,2,1,0:T(8,128)(2,1)S(1)}, bf16[4,32,2,2,128]{4,3,2,1,0:T(2,128)(2,1)S(1)}, bf16[4,32,2,2,128]{4,3,2,1,0:T(2,128)(2,1)S(1)}) custom-call(bf16[4,32,2,32,128]{4,3,2,1,0:T(8,128)(2,1)} %bitcast.6), custom_call_target="tpu_custom_call" | custom-call | tf_op jit(solution)/shard_map/pack/pallas_call | solution.py:246
  1.7 7.0 %collective-permute-start = (bf16[4,32,2,2,128]{4,3,2,1,0:T(2,128)(2,1)S(1)}, bf16[4,32,2,2,128]{4,3,2,1,0:T(2,128)(2,1)S(1)}, u32[]{:S(2)}, u32[]{:S(2)}) collective-permute-start(bf16[4,32,2,2,128]{4,3,2,1,0:T(2,128)(2,1)S(1)} %get-tuple-element.17), channel_id=1, source_target_pairs={{1,2},{2,1},{3,4},{4,3},{5,6},{6,5},{7,8},{8,7},{9,10},{10,9},{11,... | collective-permute-start | bytes 393224 | tf_op jit(solution)/shard_map/ppermute | solution.py:31
  8.7 0.7 %collective-permute-start.1 = (bf16[4,32,2,2,128]{4,3,2,1,0:T(2,128)(2,1)S(1)}, bf16[4,32,2,2,128]{4,3,2,1,0:T(2,128)(2,1)S(1)}, u32[]{:S(2)}, u32[]{:S(2)}) collective-permute-start(bf16[4,32,2,2,128]{4,3,2,1,0:T(2,128)(2,1)S(1)} %get-tuple-element.18), channel_id=1, source_target_pairs={{1,1},{2,3},{3,2},{4,4},{5,5},{6,7},{7,6},{8,8},{9,9},{10,11},{11,... | collective-permute-start | bytes 393224 | tf_op jit(solution)/shard_map/ppermute | solution.py:31
  9.4 0.0 copy-done.2
  9.4 0.0 copy-done
  9.4 4.1 %main.1.s_ref = f32[4,33,32,256]{3,2,1,0:T(8,128)S(1)} custom-call(bf16[4,32,2,32,128]{4,3,2,1,0:T(8,128)(2,1)S(1)} %get-tuple-element.19.x_ref, bf16[3,3,128,128]{3,2,1,0:T(8,128)(2,1)S(1)} %copy-done, f32[4,128]{1,0:T(4,128)S(1)} %copy-done.2), custom_call_target="tpu_custom_call" | custom-call | tf_op jit(solution)/shard_map/main/pallas_call | solution.py:246
  13.5 0.0 collective-permute-done.fa_ref
  13.5 0.0 collective-permute-done.1.fb_ref
  13.5 0.7 %edge.1 = (bf16[4,32,8,256]{3,2,1,0:T(8,128)(2,1)S(1)}, bf16[4,40,256]{2,1,0:T(8,128)(2,1)S(1)}, bf16[4,40,256]{2,1,0:T(8,128)(2,1)S(1)}) custom-call(bf16[4,32,2,32,128]{4,3,2,1,0:T(8,128)(2,1)S(1)} %get-tuple-element.19.x_ref, bf16[4,32,2,2,128]{4,3,2,1,0:T(2,128)(2,1)S(1)} %collective-permute-done.fa_ref, ...), custom_call_target="tpu_custom_call" | custom-call | tf_op jit(solution)/shard_map/edge/pallas_call | solution.py:246
  14.3 0.5 %collective-permute-start.2 = (bf16[4,40,256]{2,1,0:T(8,128)(2,1)S(1)}, bf16[4,40,256]{2,1,0:T(8,128)(2,1)S(1)}, u32[]{:S(2)}, u32[]{:S(2)}) collective-permute-start(bf16[4,40,256]{2,1,0:T(8,128)(2,1)S(1)} %get-tuple-element.24), channel_id=1, source_target_pairs={{1,5},{2,6},{3,7},{4,8},{5,1},{6,2},{7,3},{8,4},{9,13},{10,14},{11... | collective-permute-start | bytes 245768 | tf_op jit(solution)/shard_map/ppermute | solution.py:31
  14.8 0.7 %collective-permute-start.3 = (bf16[4,40,256]{2,1,0:T(8,128)(2,1)S(1)}, bf16[4,40,256]{2,1,0:T(8,128)(2,1)S(1)}, u32[]{:S(2)}, u32[]{:S(2)}) collective-permute-start(bf16[4,40,256]{2,1,0:T(8,128)(2,1)S(1)} %get-tuple-element.25), channel_id=1, source_target_pairs={{1,1},{2,2},{3,3},{4,4},{5,9},{6,10},{7,11},{8,12},{9,5},{10,6},{1... | collective-permute-start | bytes 245768 | tf_op jit(solution)/shard_map/ppermute | solution.py:31
  15.5 5.5 %collective-permute-done.2.va_ref = bf16[4,40,256]{2,1,0:T(8,128)(2,1)S(1)} collective-permute-done((bf16[4,40,256]{2,1,0:T(8,128)(2,1)S(1)}, bf16[4,40,256]{2,1,0:T(8,128)(2,1)S(1)}, u32[]{:S(2)}, u32[]{:S(2)}) %collective-permute-start.2) | collective-permute-done | bytes 81952 | tf_op jit(solution)/shard_map/ppermute | solution.py:31
  21.0 0.0 collective-permute-done.3.vb_ref
  21.0 0.0 copy-start.1
  21.0 0.0 copy-start.3
  21.0 1.7 %ring.1 = (f32[4,33,8,256]{3,2,1,0:T(8,128)S(1)}, f32[4,2,32,256]{3,2,1,0:T(8,128)S(1)}, bf16[33,40,256]{2,1,0:T(8,128)(2,1)S(1)}) custom-call(bf16[4,32,8,256]{3,2,1,0:T(8,128)(2,1)S(1)} %get-tuple-element.23.e_ref, bf16[4,40,256]{2,1,0:T(8,128)(2,1)S(1)} %collective-permute-done.2.va_ref, bf16[4,40,256]{2,1,0:T(8,128)(2,1)S(1)} %collective-permute-done.3.vb_ref, ...), custom_call_target="tpu_custom_call" | custom-call | tf_op jit(solution)/shard_map/ring/pallas_call | solution.py:246
  22.7 0.1 collective-permute-start.4
  22.8 2.1 %collective-permute-done.4.m_ref = bf16[33,40,256]{2,1,0:T(8,128)(2,1)S(1)} collective-permute-done((bf16[33,40,256]{2,1,0:T(8,128)(2,1)S(1)}, bf16[33,40,256]{2,1,0:T(8,128)(2,1)S(1)}, u32[]{:S(2)}, u32[]{:S(2)}) %collective-permute-start.4) | collective-permute-done | bytes 675872 | tf_op jit(solution)/shard_map/ppermute | solution.py:304
  24.9 0.0 copy-done.1
  24.9 0.0 copy-done.3
  24.9 5.5 %read.1 = bf16[4,32,2,32,128]{4,3,2,1,0:T(8,128)(2,1)} custom-call(f32[4,33,32,256]{3,2,1,0:T(8,128)S(1)} %main.1.s_ref, f32[4,33,8,256]{3,2,1,0:T(8,128)S(1)} %get-tuple-element.26.r_ref, f32[4,2,32,256]{3,2,1,0:T(8,128)S(1)} %get-tuple-element.27.c_ref, bf16[33,40,256]{2,1,0:T(8,128)(2,1)S(1)} %collective-permute-done.4.m_ref, ...), custom_call_target="tpu_custom_call" | custom-call | tf_op jit(solution)/shard_map/read/pallas_call | solution.py:246
Async XLA Ops:
  0.0 9.4 %copy-start.2 = (f32[4,128]{1,0:T(4,128)S(1)}, f32[4,128]{1,0:T(4,128)}, u32[]{:S(2)}) copy-start(f32[4,128]{1,0:T(4,128)} %d_ref.5) | copy-start | bytes 6148
  0.0 9.4 %copy-start = (bf16[3,3,128,128]{3,2,1,0:T(8,128)(2,1)S(1)}, bf16[3,3,128,128]{3,2,1,0:T(8,128)(2,1)}, u32[]{:S(2)}) copy-start(bf16[3,3,128,128]{3,2,1,0:T(8,128)(2,1)} %w_ref.4) | copy-start | bytes 884740
  1.7 11.8 %collective-permute-start = (bf16[4,32,2,2,128]{4,3,2,1,0:T(2,128)(2,1)S(1)}, bf16[4,32,2,2,128]{4,3,2,1,0:T(2,128)(2,1)S(1)}, u32[]{:S(2)}, u32[]{:S(2)}) collective-permute-start(bf16[4,32,2,2,128]{4,3,2,1,0:T(2,128)(2,1)S(1)} %get-tuple-element.17), channel_id=1, source_target_pairs={{1,2},{2,1},{3,4},{4,3},{5,6},{6,5},{7,8},{8,7},{9,10},{10,9},{11,... | collective-permute-start | bytes 393224 | tf_op jit(solution)/shard_map/ppermute | solution.py:31
  8.7 4.8 %collective-permute-start.1 = (bf16[4,32,2,2,128]{4,3,2,1,0:T(2,128)(2,1)S(1)}, bf16[4,32,2,2,128]{4,3,2,1,0:T(2,128)(2,1)S(1)}, u32[]{:S(2)}, u32[]{:S(2)}) collective-permute-start(bf16[4,32,2,2,128]{4,3,2,1,0:T(2,128)(2,1)S(1)} %get-tuple-element.18), channel_id=1, source_target_pairs={{1,1},{2,3},{3,2},{4,4},{5,5},{6,7},{7,6},{8,8},{9,9},{10,11},{11,... | collective-permute-start | bytes 393224 | tf_op jit(solution)/shard_map/ppermute | solution.py:31
  14.3 6.7 %collective-permute-start.2 = (bf16[4,40,256]{2,1,0:T(8,128)(2,1)S(1)}, bf16[4,40,256]{2,1,0:T(8,128)(2,1)S(1)}, u32[]{:S(2)}, u32[]{:S(2)}) collective-permute-start(bf16[4,40,256]{2,1,0:T(8,128)(2,1)S(1)} %get-tuple-element.24), channel_id=1, source_target_pairs={{1,5},{2,6},{3,7},{4,8},{5,1},{6,2},{7,3},{8,4},{9,13},{10,14},{11... | collective-permute-start | bytes 245768 | tf_op jit(solution)/shard_map/ppermute | solution.py:31
  14.8 6.2 %collective-permute-start.3 = (bf16[4,40,256]{2,1,0:T(8,128)(2,1)S(1)}, bf16[4,40,256]{2,1,0:T(8,128)(2,1)S(1)}, u32[]{:S(2)}, u32[]{:S(2)}) collective-permute-start(bf16[4,40,256]{2,1,0:T(8,128)(2,1)S(1)} %get-tuple-element.25), channel_id=1, source_target_pairs={{1,1},{2,2},{3,3},{4,4},{5,9},{6,10},{7,11},{8,12},{9,5},{10,6},{1... | collective-permute-start | bytes 245768 | tf_op jit(solution)/shard_map/ppermute | solution.py:31
  21.0 3.9 %copy-start.1 = (bf16[3,3,128,128]{3,2,1,0:T(8,128)(2,1)S(1)}, bf16[3,3,128,128]{3,2,1,0:T(8,128)(2,1)}, u32[]{:S(2)}) copy-start(bf16[3,3,128,128]{3,2,1,0:T(8,128)(2,1)} %w_ref.5) | copy-start | bytes 884740
  21.0 3.9 %copy-start.3 = (f32[128]{0:T(128)S(1)}, f32[128]{0:T(128)}, u32[]{:S(2)}) copy-start(f32[128]{0:T(128)} %param.9) | copy-start | bytes 1540
  22.7 2.2 %collective-permute-start.4 = (bf16[33,40,256]{2,1,0:T(8,128)(2,1)S(1)}, bf16[33,40,256]{2,1,0:T(8,128)(2,1)S(1)}, u32[]{:S(2)}, u32[]{:S(2)}) collective-permute-start(bf16[33,40,256]{2,1,0:T(8,128)(2,1)S(1)} %get-tuple-element.28), channel_id=1, source_target_pairs={{0,16},{16,0},{1,17},{17,1},{2,18},{18,2},{3,19},{19,3},{4,20},{20... | collective-permute-start | bytes 2027528 | tf_op jit(solution)/shard_map/ppermute | solution.py:304

commit v3 on v2

v3 whole, which is shorter than its diff:
```python
import functools

import jax
import jax.numpy as jnp
from jax import lax
from jax.experimental import pallas as pl
from jax.experimental.pallas import tpu as pltpu
from jax.sharding import PartitionSpec as P

TROWS = 4
BF = jnp.bfloat16
F32 = jnp.float32
LIMIT = 24 << 20
BLOCK = 16
VM = pl.BlockSpec(memory_space=pltpu.VMEM)
ANY = pl.BlockSpec(memory_space=pl.ANY)


def swapped(value, across, first):
    count = lax.axis_size("tile")
    tcols = count // TROWS
    pairs = []
    for number in range(count):
        row, column = divmod(number, tcols)
        at, size = (column, tcols) if across else (row, TROWS)
        other = at + 1 if at >= first and (at - first) % 2 == 0 else at - 1
        if not first <= other < size:
            other = at
        there = row * tcols + other if across else other * tcols + column
        pairs.append(((number + 1) % count, (there + 1) % count))
    return lax.ppermute(value, "tile", pairs)


def onward(value):
    groups = lax.axis_size("tm")
    return lax.ppermute(value, "tm", [(i, (i + 1) % groups) for i in range(groups)])


def place():
    count = lax.axis_size("tile")
    tcols = count // TROWS
    number = lax.rem(lax.axis_index("tile") + count - 1, count)
    return lax.rem(number, tcols), lax.div(number, tcols), tcols


def dot(a, b):
    return jnp.dot(a, b, preferred_element_type=F32)


def spread(w_ref, wide):
    c, n = w_ref.shape[2:]
    zero = jnp.zeros((c, n), BF)
    for tap in range(3):
        for row in range(4):
            for out in range(2):
                at = tap * 2 * n + out * n
                k = row - out
                wide[row * c : (row + 1) * c, at : at + n] = w_ref[k, tap] if 0 <= k <= 2 else zero


def gathered(y, pairs, cols, n2):
    y = y.reshape(pairs, cols, 3 * n2)
    left, mid, right = y[:, :, :n2], y[:, :, n2 : 2 * n2], y[:, :, 2 * n2 :]
    col = lax.broadcasted_iota(jnp.int32, mid.shape, 1)
    left = jnp.where(col > 0, pltpu.roll(left, 1, 1), 0.0)
    right = jnp.where(col < cols - 1, pltpu.roll(right, cols - 1, 1), 0.0)
    return mid + left + right


def gathered_edge(y, pairs, n2):
    y = y.reshape(pairs, 8, 3 * n2)
    left, mid, right = y[:, :, :n2], y[:, :, n2 : 2 * n2], y[:, :, 2 * n2 :]
    col = lax.broadcasted_iota(jnp.int32, mid.shape, 1)
    full = (col == 2) | (col == 5)
    left = jnp.where(full | (col == 6), pltpu.roll(left, 1, 1), 0.0)
    right = jnp.where(full | (col == 1), pltpu.roll(right, 7, 1), 0.0)
    return jnp.where(full, mid, 0.0) + left + right


def blocks(pairs):
    return [(q, min(BLOCK, pairs - q)) for q in range(1, pairs, BLOCK)]


def main_kernel(x_ref, w_ref, d_ref, s_ref, m_ref, wide):
    frames, pairs, _, cols, c = x_ref.shape
    n2 = s_ref.shape[3]
    spread(w_ref, wide)

    def rows(f, p, n):
        return jnp.concatenate(
            [x_ref[f, p : p + n, r].reshape(n * cols, c) for r in range(2)], axis=-1
        )

    for q, n in [(0, 1), *blocks(pairs), (pairs, 1)]:
        state = None
        for f in range(frames):
            y = None
            if q > 0:
                y = dot(rows(f, q - 1, n), wide[: 2 * c])
            if q < pairs:
                low = dot(rows(f, q, n), wide[2 * c :])
                y = low if y is None else y + low
            y = gathered(y, n, cols, n2)
            keep = jnp.concatenate([d_ref[f : f + 1]] * 2, axis=-1).reshape(1, 1, n2)
            state = y if f == 0 else keep * state + y
            s_ref[f, q : q + n] = state
        m_ref[q : q + n] = state.astype(BF)


def pack_kernel(f_ref, x_ref, a_ref, b_ref, sems):
    frames, _, _, cols, _ = x_ref.shape
    column, _, _ = place()
    even = lax.rem(column, 2) == 0
    copies = [
        pltpu.make_async_copy(f_ref.at[f], x_ref.at[f], sems.at[f]) for f in range(frames)
    ]
    for copy in copies:
        copy.start()
    for f, copy in enumerate(copies):
        copy.wait()
        low, high = x_ref[f, :, :, :2], x_ref[f, :, :, cols - 2 :]
        a_ref[f] = jnp.where(even, high, low)
        b_ref[f] = jnp.where(even, low, high)


def edge_kernel(x_ref, fa_ref, fb_ref, e_ref, a_ref, b_ref):
    frames, pairs, _, cols, c = x_ref.shape
    column, row, tcols = place()
    has_left, has_right = column > 0, column < tcols - 1
    even = lax.rem(column, 2) == 0
    upper = lax.rem(row, 2) == 0
    for f in range(frames):
        for r in range(2):
            lane = pl.ds(r * c, c)
            fa, fb = fa_ref[f, :, r], fb_ref[f, :, r]
            right = jnp.where(has_right, jnp.where(even, fa, fb), 0).astype(BF)
            left = jnp.where(has_left, jnp.where(even, fb, fa), 0).astype(BF)
            e_ref[f, :, 0:2, lane] = x_ref[f, :, r, cols - 2 :]
            e_ref[f, :, 2:4, lane] = right
            e_ref[f, :, 4:6, lane] = left
            e_ref[f, :, 6:8, lane] = x_ref[f, :, r, :2]
            top, bottom = x_ref[f, 0, r], x_ref[f, pairs - 1, r]
            a_ref[f, 0:cols, lane] = jnp.where(upper, bottom, top)
            b_ref[f, 0:cols, lane] = jnp.where(upper, top, bottom)
        top, bottom = e_ref[f, 0], e_ref[f, pairs - 1]
        a_ref[f, cols:, :] = jnp.where(upper, bottom, top)
        b_ref[f, cols:, :] = jnp.where(upper, top, bottom)


def twice(ref, f):
    return jnp.concatenate([ref[f : f + 1]] * 2, axis=-1)


def inner_kernel(e_ref, w_ref, d_ref, r_ref, wide):
    frames, pairs, _, c2 = e_ref.shape
    n2 = r_ref.shape[3]
    spread(w_ref, wide)
    state = None
    blank = jnp.zeros((8, 3 * n2), F32)
    for f in range(frames):
        e = e_ref[f].reshape(pairs * 8, c2)
        high, low = dot(e, wide[:c2]), dot(e, wide[c2:])
        y = jnp.concatenate([blank, high]) + jnp.concatenate([low, blank])
        y = gathered_edge(y, pairs + 1, n2)
        state = y if f == 0 else twice(d_ref, f).reshape(1, 1, n2) * state + y
        r_ref[f] = state


def ring_kernel(va_ref, vb_ref, p_ref, w_ref, d_ref, r_ref, c_ref, m_ref, wide):
    frames, size, c2 = va_ref.shape
    pairs, n2 = r_ref.shape[1] - 1, r_ref.shape[3]
    cols = size - 8
    _, row, _ = place()
    upper = lax.rem(row, 2) == 0
    spread(w_ref, wide)
    last = frames - 1
    r_ref[...] = p_ref[...]
    for side, there in enumerate((row > 0, row < TROWS - 1)):
        take_a = upper == (side == 1)
        v = jnp.where(there, jnp.where(take_a, va_ref[...], vb_ref[...]), 0).astype(BF)
        y = dot(v.reshape(frames * size, c2), wide[c2:] if side else wide[:c2])
        y = y.reshape(frames, size, 3 * n2)
        mid = gathered(y[:, :cols], frames, cols, n2)
        end = gathered_edge(y[:, cols:], frames, n2)
        y = jnp.concatenate([mid, end], axis=1)
        at = side * pairs
        state = None
        for f in range(frames):
            state = y[f] if f == 0 else twice(d_ref, f) * state + y[f]
            c_ref[f, side] = state[:cols]
            r_ref[f, at] = p_ref[f, at] + state[cols:]
        for k in range(cols // 8):
            m_ref[pairs + 1 + side * (cols // 8) + k] = state[8 * k : 8 * k + 8].astype(BF)
    m_ref[: pairs + 1] = r_ref[last].astype(BF)


def row_masked(value, q, pairs):
    _, row, _ = place()
    _, _, n2 = value.shape
    pair = lax.broadcasted_iota(jnp.int32, value.shape, 0) + q
    lane = lax.broadcasted_iota(jnp.int32, value.shape, 2)
    off = ((pair == 0) & (lane < n2 // 2) & (row == 0)) | (
        (pair == pairs) & (lane >= n2 // 2) & (row == TROWS - 1)
    )
    return jnp.where(off, 0.0, value)


def read_kernel(first, *refs):
    s_ref, m_ref, w_ref, d_ref, skip_ref, x_ref = refs[:6]
    o_ref, side_ref, rim_ref, wide, held, out, sems = refs[-7:]
    _, pairs, _, cols, _ = x_ref.shape
    n2 = s_ref.shape[3]
    half = n2 // 2
    spread(w_ref, wide)
    later = (lax.axis_index("tm") > 0).astype(F32)
    gain = skip_ref[...].reshape(1, 1, half)
    factor = jnp.full((1, n2), 1.0, F32) * later
    for f in range(first):
        factor = factor * twice(d_ref, f)
    copies = []
    for i in range(side_ref.shape[0]):
        f = first + i
        factor = factor * twice(d_ref, f)
        body = s_ref[f] + factor.reshape(1, 1, n2) * m_ref[...].astype(F32)
        held[...] = body.astype(BF)
        held[0:1] = row_masked(body[0:1], 0, pairs).astype(BF)
        held[pairs:] = row_masked(body[pairs:], pairs, pairs).astype(BF)
        for p in range(0, pairs, BLOCK):
            n = min(BLOCK, pairs - p)
            y = dot(held[p : p + n].reshape(n * cols, n2), wide[:n2])
            y = y + dot(held[p + 1 : p + 1 + n].reshape(n * cols, n2), wide[n2:])
            y = gathered(y, n, cols, n2)
            for r in range(2):
                lane = pl.ds(r * half, half)
                v = y[:, :, r * half : (r + 1) * half]
                v = v + gain * x_ref[f, p : p + n, r].astype(F32)
                out[i, p : p + n, r] = v[:, 8 : cols - 8].astype(BF)
                side_ref[i, p : p + n, 0:8, lane] = v[:, :8]
                side_ref[i, p : p + n, 8:16, lane] = v[:, cols - 8 :]
                if p == 0:
                    rim_ref[i, 0, :, lane] = v[0, 8 : cols - 8]
                if p + n == pairs:
                    rim_ref[i, 1, :, lane] = v[n - 1, 8 : cols - 8]
        copy = pltpu.make_async_copy(
            out.at[i], o_ref.at[f, :, :, pl.ds(8, cols - 16)], sems.at[i]
        )
        copy.start()
        copies.append(copy)
    for copy in copies:
        copy.wait()


def last_kernel(r_ref, c_ref, m_ref, w_ref, d_ref, *refs):
    count = (len(refs) - 7) // 2
    sides, rims = refs[:count], refs[count : 2 * count]
    o_ref, wide, held, left, right, rows, sems = refs[2 * count :][-7:]
    frames, rest, _, n2 = r_ref.shape
    pairs, half = rest - 1, n2 // 2
    cols = c_ref.shape[2]
    spread(w_ref, wide)
    column, _, tcols = place()
    later = (lax.axis_index("tm") > 0).astype(F32)
    factor = jnp.full((1, n2), 1.0, F32) * later
    ends, rim = [], []
    for f in range(frames):
        factor = factor * twice(d_ref, f)
        far = factor.reshape(1, 1, n2)
        e = r_ref[f] + far * m_ref[: pairs + 1].astype(F32)
        col = lax.broadcasted_iota(jnp.int32, e.shape, 1)
        e = jnp.where(((col == 2) & (column == tcols - 1)) | ((col == 5) & (column == 0)), 0.0, e)
        ends.append(row_masked(e, 0, pairs))
        more = m_ref[pairs + 1 :].astype(F32).reshape(2, cols, n2)
        rim.append(row_masked(c_ref[f] + far * more, 0, 1).astype(BF))
    for f in range(0, frames, 2):
        e = ends[f]
        if f + 1 < frames:
            col = lax.broadcasted_iota(jnp.int32, e.shape, 1)
            own = (col == 1) | (col == 2) | (col == 5) | (col == 6)
            e = jnp.where(own, e, pltpu.roll(ends[f + 1], 2, 1))
        held[f // 2] = e.astype(BF)
    edge_rows = []
    for side in range(2):
        v = jnp.stack([rim[f][side] for f in range(frames)]).reshape(frames * cols, n2)
        y = dot(v, wide[n2:] if side else wide[:n2])
        edge_rows.append(gathered(y, frames, cols, n2))
    copies = []
    for f in range(frames):
        if f % 2 == 0:
            e = held[f // 2]
            y = dot(e[:pairs].reshape(pairs * 8, n2), wide[:n2])
            y = y + dot(e[1:].reshape(pairs * 8, n2), wide[n2:])
            y = y.reshape(pairs, 8, 3 * n2)
            y0, y1, y2 = y[:, :, :n2], y[:, :, n2 : 2 * n2], y[:, :, 2 * n2 :]
        col = lax.broadcasted_iota(jnp.int32, (pairs, 8, n2), 1)
        a, b, d, g = (3, 2, 5, 6) if f % 2 == 0 else (1, 0, 3, 4)
        near = jnp.where(col < 2, pltpu.roll(y0, a, 1), 0.0)
        near = near + jnp.where(col == 0, pltpu.roll(y1, b, 1) if b else y1, 0.0)
        far = jnp.where(col >= 6, pltpu.roll(y2, d, 1), 0.0)
        far = far + jnp.where(col == 7, pltpu.roll(y1, g, 1), 0.0)
        which, i = divmod(f, sides[0].shape[0])
        for at, part, ref, base in ((0, near, left, 0), (8, far, right, cols - 8)):
            total = sides[which][i, :, at : at + 8] + part
            for r in range(2):
                ref[f, :, r] = total[:, :, r * half : (r + 1) * half].astype(BF)
                lane = slice(r * half, (r + 1) * half)
                top = total[:1, :, lane] + edge_rows[0][f : f + 1, base : base + 8, lane]
                low = total[pairs - 1 :, :, lane] + edge_rows[1][f : f + 1, base : base + 8, lane]
                ref[f, 0:1, r] = top.astype(BF)
                ref[f, pairs - 1 :, r] = low.astype(BF)
        for k in range(2):
            v = rims[which][i, k] + edge_rows[k][f, 8 : cols - 8]
            for r in range(2):
                rows[f, k, r] = v[:, r * half : (r + 1) * half].astype(BF)
        ends_of = ((0, 0), (pairs - 1, 1))
        mine = [
            (left.at[f], o_ref.at[f, :, :, pl.ds(0, 8)]),
            (right.at[f], o_ref.at[f, :, :, pl.ds(cols - 8, 8)]),
            *((rows.at[f, k], o_ref.at[f, p, :, pl.ds(8, cols - 16)]) for p, k in ends_of),
        ]
        for k, (source, target) in enumerate(mine):
            copy = pltpu.make_async_copy(source, target, sems.at[f, k])
            copy.start()
            copies.append(copy)
    for copy in copies:
        copy.wait()


def call(body, outs, ins, scratch=(), in_specs=None, out_specs=None, aliases=None):
    return pl.pallas_call(
        body,
        out_shape=outs,
        in_specs=in_specs or [VM] * len(ins),
        out_specs=out_specs if out_specs is not None else jax.tree.map(lambda _: VM, outs),
        scratch_shapes=list(scratch),
        compiler_params=pltpu.CompilerParams(vmem_limit_bytes=LIMIT),
        input_output_aliases=aliases or {},
    )(*ins)


def per_device(frames, w_in, w_out, decay, skip):
    shape = jax.ShapeDtypeStruct
    count, _, rows, cols, c = frames.shape
    n2 = 2 * w_in.shape[3]
    pairs = rows // 2
    video = frames.reshape(count, pairs, 2, cols, c)
    side = shape((count, pairs, 2, 2, c), BF)
    across = shape((count, cols + 8, 2 * c), BF)
    here, side_a, side_b = call(
        pack_kernel,
        (shape(video.shape, BF), side, side),
        (pltpu.with_memory_space_constraint(video, pltpu.HBM),),
        [pltpu.SemaphoreType.DMA((count,))],
        in_specs=[pl.BlockSpec(memory_space=pltpu.HBM)],
    )
    from_a = swapped(side_a, True, 0)
    from_b = swapped(side_b, True, 1)
    wide_in = pltpu.VMEM((4 * c, 3 * n2), BF)
    wide_out = pltpu.VMEM((2 * n2, 3 * 2 * c), BF)
    local, message = call(
        main_kernel,
        (shape((count, pairs + 1, cols, n2), F32), shape((pairs + 1, cols, n2), BF)),
        (here, w_in, decay),
        [wide_in],
    )
    before = onward(message)
    from_a, from_b, local = lax.optimization_barrier((from_a, from_b, local))
    edge, row_a, row_b = call(
        edge_kernel, (shape((count, pairs, 8, 2 * c), BF), across, across), (here, from_a, from_b)
    )
    rows_a = swapped(row_a, False, 0)
    rows_b = swapped(row_b, False, 1)
    edge_states = shape((count, pairs + 1, 8, n2), F32)
    edge, local, before = lax.optimization_barrier((edge, local, before))
    partial = call(inner_kernel, edge_states, (edge, w_in, decay), [wide_in])
    part = count // 2

    def read(first, mixed, local):
        given = (local, before, w_out, decay, skip.reshape(1, c), here)
        return call(
            functools.partial(read_kernel, first),
            (
                shape(video.shape, BF),
                shape((part, pairs, 16, n2), F32),
                shape((part, 2, cols - 16, n2), F32),
            ),
            given if mixed is None else (*given, mixed),
            [
                wide_out,
                pltpu.VMEM((pairs + 1, cols, n2), BF),
                pltpu.VMEM((part, pairs, 2, cols - 16, c), BF),
                pltpu.SemaphoreType.DMA((part,)),
            ],
            in_specs=[VM] * len(given) + ([] if mixed is None else [ANY]),
            out_specs=(ANY, VM, VM),
            aliases={} if mixed is None else {len(given): 0},
        )

    mixed, side_0, rim_0 = read(0, None, local)
    rows_a, rows_b, partial, side_0, local = lax.optimization_barrier(
        (rows_a, rows_b, partial, side_0, local)
    )
    ends, rim, message = call(
        ring_kernel,
        (edge_states, shape((count, 2, cols, n2), F32), shape((pairs + 1 + cols // 4, 8, n2), BF)),
        (rows_a, rows_b, partial, w_in, decay),
        [wide_in],
    )
    ring_before = onward(message)
    ends, local = lax.optimization_barrier((ends, local))
    mixed, side_1, rim_1 = read(part, mixed, local)
    ring_before, side_1 = lax.optimization_barrier((ring_before, side_1))
    given = (ends, rim, ring_before, w_out, decay, side_0, side_1, rim_0, rim_1)
    mixed = call(
        last_kernel,
        shape(video.shape, BF),
        (*given, mixed),
        [
            wide_out,
            pltpu.VMEM(((count + 1) // 2, pairs + 1, 8, n2), BF),
            pltpu.VMEM((count, pairs, 2, 8, c), BF),
            pltpu.VMEM((count, pairs, 2, 8, c), BF),
            pltpu.VMEM((count, 2, 2, cols - 16, c), BF),
            pltpu.SemaphoreType.DMA((count, 4)),
        ],
        in_specs=[VM] * len(given) + [ANY],
        out_specs=ANY,
        aliases={len(given): 0},
    )
    return mixed.reshape(count, 1, rows, cols, c)


def solution(mesh):
    return jax.shard_map(
        per_device,
        mesh=mesh,
        in_specs=(P("tm", "tile", None, None, None), P(), P(), P("tm", None), P()),
        out_specs=P("tm", "tile", None, None, None),
        check_vma=False,
    )
```

time: 30.5 us -> 31.3 us (1.026)
  the two profiles are of different devices: /device:TPU:0 before, /device:TPU:13 now
where the time goes in v3:
time: 31.3 us; the launch traced here: 31.2 us
  Pallas kernels  15.6 us (50%)
  starting transfers between devices  10.8 us (35%)
  waiting for transfers between devices  4.65 us (15%)
    pallas_call x8, Pallas kernels, call(): pl.pallas_call(body, out_shape=outs, in_specs=in_specs or [VM] * len(ins)...  15.6 us
    ppermute x4, starting transfers between devices, swapped(): return lax.ppermute(value, 'tile', pairs)  8.87 us
    ppermute x4, waiting for transfers between devices, swapped(): return lax.ppermute(value, 'tile', pairs)  4.64 us
    ppermute x2, starting transfers between devices, onward(): lax.ppermute(value, 'tm', [(i, (i + 1) % groups) for i in range(groups)])  1.96 us
  transfers between devices with their start and end apart: 6, of which 2 were waited for; matrix products, arithmetic and copies ran while one was open for 0% of the time, Pallas kernels for 23%

profile of v3, /device:TPU:13, one launch (start us, length us, event | category | flops | bytes accessed | tf_op | source)
XLA Modules:
  0.0 31.2 jit_solution(6165083479396218749)
XLA Ops:
  0.0 1.7 %shard_map.55 = (bf16[4,32,2,32,128]{4,3,2,1,0:T(8,128)(2,1)S(1)}, bf16[4,32,2,2,128]{4,3,2,1,0:T(2,128)(2,1)S(1)}, bf16[4,32,2,2,128]{4,3,2,1,0:T(2,128)(2,1)S(1)}) custom-call(bf16[4,32,2,32,128]{4,3,2,1,0:T(8,128)(2,1)} %bitcast.7), custom_call_target="tpu_custom_call" | custom-call | tf_op jit(solution)/shard_map/pallas_call | solution.py:329
  1.7 0.0 copy-done.2
  1.7 0.0 copy-done
  1.7 4.2 %shard_map.56 = (f32[4,33,32,256]{3,2,1,0:T(8,128)S(1)}, bf16[33,32,256]{2,1,0:T(8,128)(2,1)S(1)}) custom-call(bf16[4,32,2,32,128]{4,3,2,1,0:T(8,128)(2,1)S(1)} %get-tuple-element.37.x_ref.refs_5_, bf16[3,3,128,128]{3,2,1,0:T(8,128)(2,1)S(1)} %copy-done, f32[4,128]{1,0:T(4,128)S(1)} %copy-done.2), custom_call_target="tpu_custom_call" | custom-call | tf_op jit(solution)/shard_map/pallas_call | solution.py:329
  5.9 0.7 %collective-permute-start.4 = (bf16[33,32,256]{2,1,0:T(8,128)(2,1)S(1)}, bf16[33,32,256]{2,1,0:T(8,128)(2,1)S(1)}, u32[]{:S(2)}, u32[]{:S(2)}) collective-permute-start(bf16[33,32,256]{2,1,0:T(8,128)(2,1)S(1)} %get-tuple-element.47), channel_id=1, source_target_pairs={{0,16},{16,0},{1,17},{17,1},{2,18},{18,2},{3,19},{19,3},{4,20},{20... | collective-permute-start | bytes 1622024 | tf_op jit(solution)/shard_map/ppermute | solution.py:36
  6.6 1.2 %collective-permute-start = (bf16[4,32,2,2,128]{4,3,2,1,0:T(2,128)(2,1)S(1)}, bf16[4,32,2,2,128]{4,3,2,1,0:T(2,128)(2,1)S(1)}, u32[]{:S(2)}, u32[]{:S(2)}) collective-permute-start(bf16[4,32,2,2,128]{4,3,2,1,0:T(2,128)(2,1)S(1)} %get-tuple-element.38), channel_id=1, source_target_pairs={{1,2},{2,1},{3,4},{4,3},{5,6},{6,5},{7,8},{8,7},{9,10},{10,9},{11,... | collective-permute-start | bytes 393224 | tf_op jit(solution)/shard_map/ppermute | solution.py:31
  7.8 3.2 %collective-permute-start.1 = (bf16[4,32,2,2,128]{4,3,2,1,0:T(2,128)(2,1)S(1)}, bf16[4,32,2,2,128]{4,3,2,1,0:T(2,128)(2,1)S(1)}, u32[]{:S(2)}, u32[]{:S(2)}) collective-permute-start(bf16[4,32,2,2,128]{4,3,2,1,0:T(2,128)(2,1)S(1)} %get-tuple-element.39), channel_id=1, source_target_pairs={{1,1},{2,3},{3,2},{4,4},{5,5},{6,7},{7,6},{8,8},{9,9},{10,11},{11,... | collective-permute-start | bytes 393224 | tf_op jit(solution)/shard_map/ppermute | solution.py:31
  10.9 1.6 %collective-permute-done.fa_ref = bf16[4,32,2,2,128]{4,3,2,1,0:T(2,128)(2,1)S(1)} collective-permute-done((bf16[4,32,2,2,128]{4,3,2,1,0:T(2,128)(2,1)S(1)}, bf16[4,32,2,2,128]{4,3,2,1,0:T(2,128)(2,1)S(1)}, u32[]{:S(2)}, u32[]{:S(2)}) %collective-permute-start) | collective-permute-done | bytes 131104 | tf_op jit(solution)/shard_map/ppermute | solution.py:31
  12.5 3.1 %collective-permute-done.1.fb_ref = bf16[4,32,2,2,128]{4,3,2,1,0:T(2,128)(2,1)S(1)} collective-permute-done((bf16[4,32,2,2,128]{4,3,2,1,0:T(2,128)(2,1)S(1)}, bf16[4,32,2,2,128]{4,3,2,1,0:T(2,128)(2,1)S(1)}, u32[]{:S(2)}, u32[]{:S(2)}) %collective-permute-start.1) | collective-permute-done | bytes 131104 | tf_op jit(solution)/shard_map/ppermute | solution.py:31
  15.6 0.7 %shard_map.57 = (bf16[4,32,8,256]{3,2,1,0:T(8,128)(2,1)S(1)}, bf16[4,40,256]{2,1,0:T(8,128)(2,1)S(1)}, bf16[4,40,256]{2,1,0:T(8,128)(2,1)S(1)}) custom-call(bf16[4,32,2,32,128]{4,3,2,1,0:T(8,128)(2,1)S(1)} %get-tuple-element.37.x_ref.refs_5_, bf16[4,32,2,2,128]{4,3,2,1,0:T(2,128)(2,1)S(1)} %collective-permute-done.fa_ref, ...), custom_call_target="tpu_custom_call" | custom-call | tf_op jit(solution)/shard_map/pallas_call | solution.py:329
  16.3 2.3 %collective-permute-start.2 = (bf16[4,40,256]{2,1,0:T(8,128)(2,1)S(1)}, bf16[4,40,256]{2,1,0:T(8,128)(2,1)S(1)}, u32[]{:S(2)}, u32[]{:S(2)}) collective-permute-start(bf16[4,40,256]{2,1,0:T(8,128)(2,1)S(1)} %get-tuple-element.43), channel_id=1, source_target_pairs={{1,5},{2,6},{3,7},{4,8},{5,1},{6,2},{7,3},{8,4},{9,13},{10,14},{11... | collective-permute-start | bytes 245768 | tf_op jit(solution)/shard_map/ppermute | solution.py:31
  18.6 2.2 %collective-permute-start.3 = (bf16[4,40,256]{2,1,0:T(8,128)(2,1)S(1)}, bf16[4,40,256]{2,1,0:T(8,128)(2,1)S(1)}, u32[]{:S(2)}, u32[]{:S(2)}) collective-permute-start(bf16[4,40,256]{2,1,0:T(8,128)(2,1)S(1)} %get-tuple-element.44), channel_id=1, source_target_pairs={{1,1},{2,2},{3,3},{4,4},{5,9},{6,10},{7,11},{8,12},{9,5},{10,6},{1... | collective-permute-start | bytes 245768 | tf_op jit(solution)/shard_map/ppermute | solution.py:31
  20.9 0.0 collective-permute-done.4.refs_1_
  20.9 1.1 %shard_map.58.p_ref = f32[4,33,8,256]{3,2,1,0:T(8,128)S(1)} custom-call(bf16[4,32,8,256]{3,2,1,0:T(8,128)(2,1)S(1)} %get-tuple-element.48.e_ref, bf16[3,3,128,128]{3,2,1,0:T(8,128)(2,1)S(1)} %copy-done, f32[4,128]{1,0:T(4,128)S(1)} %copy-done.2), custom_call_target="tpu_custom_call" | custom-call | tf_op jit(solution)/shard_map/pallas_call | solution.py:329
  22.0 0.0 copy-done.1
  22.1 0.0 copy-done.3
  22.1 2.7 %shard_map.59 = (bf16[4,32,2,32,128]{4,3,2,1,0:T(8,128)(2,1)}, f32[2,32,16,256]{3,2,1,0:T(8,128)S(1)}, f32[2,2,16,256]{3,2,1,0:T(8,128)S(1)}) custom-call(f32[4,33,32,256]{3,2,1,0:T(8,128)S(1)} %get-tuple-element.60.refs_0_, bf16[33,32,256]{2,1,0:T(8,128)(2,1)S(1)} %collective-permute-done.4.refs_1_, bf16[3,3,128,128]{3,2,1,0:T(8,128)(2,1)S(1)} %copy-done.1, ...), custom_call_target="tpu_custom_call" | custom-call | tf_op jit(solution)/shard_map/pallas_call | solution.py:329
  24.8 0.0 collective-permute-done.2.va_ref
  24.8 0.0 collective-permute-done.3.vb_ref
  24.8 0.4 %shard_map.60 = (f32[4,33,8,256]{3,2,1,0:T(8,128)S(1)}, f32[4,2,32,256]{3,2,1,0:T(8,128)S(1)}, bf16[41,8,256]{2,1,0:T(8,128)(2,1)S(1)}) custom-call(bf16[4,40,256]{2,1,0:T(8,128)(2,1)S(1)} %collective-permute-done.2.va_ref, bf16[4,40,256]{2,1,0:T(8,128)(2,1)S(1)} %collective-permute-done.3.vb_ref, f32[4,33,8,256]{3,2,1,0:T(8,128)S(1)} %shard_map.58.p_ref, ...), custom_call_target="tpu_custom_call" | custom-call | tf_op jit(solution)/shard_map/pallas_call | solution.py:329
  25.2 1.2 %collective-permute-start.5 = (bf16[41,8,256]{2,1,0:T(8,128)(2,1)S(1)}, bf16[41,8,256]{2,1,0:T(8,128)(2,1)S(1)}, u32[]{:S(2)}, u32[]{:S(2)}) collective-permute-start(bf16[41,8,256]{2,1,0:T(8,128)(2,1)S(1)} %get-tuple-element.59), channel_id=1, source_target_pairs={{0,16},{16,0},{1,17},{17,1},{2,18},{18,2},{3,19},{19,3},{4,20},{20... | collective-permute-start | bytes 503816 | tf_op jit(solution)/shard_map/ppermute | solution.py:36
  26.4 2.7 %shard_map.61 = (bf16[4,32,2,32,128]{4,3,2,1,0:T(8,128)(2,1)}, f32[2,32,16,256]{3,2,1,0:T(8,128)S(1)}, f32[2,2,16,256]{3,2,1,0:T(8,128)S(1)}) custom-call(f32[4,33,32,256]{3,2,1,0:T(8,128)S(1)} %get-tuple-element.60.refs_0_, bf16[33,32,256]{2,1,0:T(8,128)(2,1)S(1)} %collective-permute-done.4.refs_1_, ...), custom_call_target="tpu_custom_call", output_to_operand_aliasing={{0}: (6, {})} | custom-call | tf_op jit(solution)/shard_map/pallas_call | solution.py:329
  29.1 0.0 collective-permute-done.5.m_ref
  29.1 2.0 %shard_map.62 = bf16[4,32,2,32,128]{4,3,2,1,0:T(8,128)(2,1)} custom-call(f32[4,33,8,256]{3,2,1,0:T(8,128)S(1)} %get-tuple-element.57.r_ref, f32[4,2,32,256]{3,2,1,0:T(8,128)S(1)} %get-tuple-element.58.c_ref, bf16[41,8,256]{2,1,0:T(8,128)(2,1)S(1)} %collective-permute-done.5.m_ref, ...), custom_call_target="tpu_custom_call", output_to_operand_aliasing={{}: (9, {})} | custom-call | tf_op jit(solution)/shard_map/pallas_call | solution.py:329
  (4 shorter events, 0.0 us)
Async XLA Ops:
  0.0 1.7 %copy-start.2 = (f32[4,128]{1,0:T(4,128)S(1)}, f32[4,128]{1,0:T(4,128)}, u32[]{:S(2)}) copy-start(f32[4,128]{1,0:T(4,128)} %d_ref.7) | copy-start | bytes 6148
  0.0 1.7 %copy-start = (bf16[3,3,128,128]{3,2,1,0:T(8,128)(2,1)S(1)}, bf16[3,3,128,128]{3,2,1,0:T(8,128)(2,1)}, u32[]{:S(2)}) copy-start(bf16[3,3,128,128]{3,2,1,0:T(8,128)(2,1)} %w_ref.6) | copy-start | bytes 884740
  5.9 15.0 %collective-permute-start.4 = (bf16[33,32,256]{2,1,0:T(8,128)(2,1)S(1)}, bf16[33,32,256]{2,1,0:T(8,128)(2,1)S(1)}, u32[]{:S(2)}, u32[]{:S(2)}) collective-permute-start(bf16[33,32,256]{2,1,0:T(8,128)(2,1)S(1)} %get-tuple-element.47), channel_id=1, source_target_pairs={{0,16},{16,0},{1,17},{17,1},{2,18},{18,2},{3,19},{19,3},{4,20},{20... | collective-permute-start | bytes 1622024 | tf_op jit(solution)/shard_map/ppermute | solution.py:36
  6.6 5.9 %collective-permute-start = (bf16[4,32,2,2,128]{4,3,2,1,0:T(2,128)(2,1)S(1)}, bf16[4,32,2,2,128]{4,3,2,1,0:T(2,128)(2,1)S(1)}, u32[]{:S(2)}, u32[]{:S(2)}) collective-permute-start(bf16[4,32,2,2,128]{4,3,2,1,0:T(2,128)(2,1)S(1)} %get-tuple-element.38), channel_id=1, source_target_pairs={{1,2},{2,1},{3,4},{4,3},{5,6},{6,5},{7,8},{8,7},{9,10},{10,9},{11,... | collective-permute-start | bytes 393224 | tf_op jit(solution)/shard_map/ppermute | solution.py:31
  7.8 7.8 %collective-permute-start.1 = (bf16[4,32,2,2,128]{4,3,2,1,0:T(2,128)(2,1)S(1)}, bf16[4,32,2,2,128]{4,3,2,1,0:T(2,128)(2,1)S(1)}, u32[]{:S(2)}, u32[]{:S(2)}) collective-permute-start(bf16[4,32,2,2,128]{4,3,2,1,0:T(2,128)(2,1)S(1)} %get-tuple-element.39), channel_id=1, source_target_pairs={{1,1},{2,3},{3,2},{4,4},{5,5},{6,7},{7,6},{8,8},{9,9},{10,11},{11,... | collective-permute-start | bytes 393224 | tf_op jit(solution)/shard_map/ppermute | solution.py:31
  15.6 6.5 %copy-start.1 = (bf16[3,3,128,128]{3,2,1,0:T(8,128)(2,1)S(1)}, bf16[3,3,128,128]{3,2,1,0:T(8,128)(2,1)}, u32[]{:S(2)}) copy-start(bf16[3,3,128,128]{3,2,1,0:T(8,128)(2,1)} %w_ref.7) | copy-start | bytes 884740
  15.6 6.5 %copy-start.3 = (f32[128]{0:T(128)S(1)}, f32[128]{0:T(128)}, u32[]{:S(2)}) copy-start(f32[128]{0:T(128)} %param.9) | copy-start | bytes 1540
  16.3 8.5 %collective-permute-start.2 = (bf16[4,40,256]{2,1,0:T(8,128)(2,1)S(1)}, bf16[4,40,256]{2,1,0:T(8,128)(2,1)S(1)}, u32[]{:S(2)}, u32[]{:S(2)}) collective-permute-start(bf16[4,40,256]{2,1,0:T(8,128)(2,1)S(1)} %get-tuple-element.43), channel_id=1, source_target_pairs={{1,5},{2,6},{3,7},{4,8},{5,1},{6,2},{7,3},{8,4},{9,13},{10,14},{11... | collective-permute-start | bytes 245768 | tf_op jit(solution)/shard_map/ppermute | solution.py:31
  18.6 6.2 %collective-permute-start.3 = (bf16[4,40,256]{2,1,0:T(8,128)(2,1)S(1)}, bf16[4,40,256]{2,1,0:T(8,128)(2,1)S(1)}, u32[]{:S(2)}, u32[]{:S(2)}) collective-permute-start(bf16[4,40,256]{2,1,0:T(8,128)(2,1)S(1)} %get-tuple-element.44), channel_id=1, source_target_pairs={{1,1},{2,2},{3,3},{4,4},{5,9},{6,10},{7,11},{8,12},{9,5},{10,6},{1... | collective-permute-start | bytes 245768 | tf_op jit(solution)/shard_map/ppermute | solution.py:31
  25.2 3.9 %collective-permute-start.5 = (bf16[41,8,256]{2,1,0:T(8,128)(2,1)S(1)}, bf16[41,8,256]{2,1,0:T(8,128)(2,1)S(1)}, u32[]{:S(2)}, u32[]{:S(2)}) collective-permute-start(bf16[41,8,256]{2,1,0:T(8,128)(2,1)S(1)} %get-tuple-element.59), channel_id=1, source_target_pairs={{0,16},{16,0},{1,17},{17,1},{2,18},{18,2},{3,19},{19,3},{4,20},{20... | collective-permute-start | bytes 503816 | tf_op jit(solution)/shard_map/ppermute | solution.py:36

commit v4 on v3

--- a/solution.py
+++ b/solution.py
@@ -78,20 +78,25 @@
 
 
 def blocks(pairs):
-    return [(q, min(BLOCK, pairs - q)) for q in range(1, pairs, BLOCK)]
-
-
-def main_kernel(x_ref, w_ref, d_ref, s_ref, m_ref, wide):
+    every = [(0, 1), *((q, min(BLOCK, pairs - q)) for q in range(1, pairs, BLOCK)), (pairs, 1)]
+    cut = pairs // 2 + 1
+    return [b for b in every if b[0] + b[1] <= cut], [b for b in every if b[0] + b[1] > cut]
+
+
+def ahead():
+    return lax.axis_index("tile") == 0
+
+
+def own_states(x_ref, wide, d_ref, s_ref, m_ref, chosen):
     frames, pairs, _, cols, c = x_ref.shape
     n2 = s_ref.shape[3]
-    spread(w_ref, wide)
 
     def rows(f, p, n):
         return jnp.concatenate(
             [x_ref[f, p : p + n, r].reshape(n * cols, c) for r in range(2)], axis=-1
         )
 
-    for q, n in [(0, 1), *blocks(pairs), (pairs, 1)]:
+    for q, n in chosen:
         state = None
         for f in range(frames):
             y = None
@@ -101,10 +106,34 @@
                 low = dot(rows(f, q, n), wide[2 * c :])
                 y = low if y is None else y + low
             y = gathered(y, n, cols, n2)
-            keep = jnp.concatenate([d_ref[f : f + 1]] * 2, axis=-1).reshape(1, 1, n2)
-            state = y if f == 0 else keep * state + y
+            state = y if f == 0 else twice(d_ref, f).reshape(1, 1, n2) * state + y
             s_ref[f, q : q + n] = state
-        m_ref[q : q + n] = state.astype(BF)
+        if m_ref is not None:
+            m_ref[q : q + n] = state.astype(BF)
+
+
+def early_kernel(x_ref, w_ref, d_ref, s_ref, wide):
+    @pl.when(ahead())
+    def _():
+        spread(w_ref, wide)
+        own_states(x_ref, wide, d_ref, s_ref, None, blocks(x_ref.shape[1])[0])
+
+
+def main_kernel(x_ref, w_ref, d_ref, p_ref, s_ref, m_ref, wide):
+    head, tail = blocks(x_ref.shape[1])
+    spread(w_ref, wide)
+
+    @pl.when(jnp.logical_not(ahead()))
+    def _():
+        own_states(x_ref, wide, d_ref, s_ref, m_ref, head)
+
+    own_states(x_ref, wide, d_ref, s_ref, m_ref, tail)
+
+    @pl.when(ahead())
+    def _():
+        done = p_ref.shape[1]
+        s_ref[:, :done] = p_ref[...]
+        m_ref[:done] = p_ref[p_ref.shape[0] - 1].astype(BF)
 
 
 def pack_kernel(f_ref, x_ref, a_ref, b_ref, sems):
@@ -123,26 +152,34 @@
         b_ref[f] = jnp.where(even, low, high)
 
 
-def edge_kernel(x_ref, fa_ref, fb_ref, e_ref, a_ref, b_ref):
+def group_of(x_ref, fa_ref, fb_ref, f, p, e_ref, at):
+    _, _, _, cols, c = x_ref.shape
+    column, _, tcols = place()
+    even = lax.rem(column, 2) == 0
+    for r in range(2):
+        lane = pl.ds(r * c, c)
+        fa, fb = fa_ref[f, p, r], fb_ref[f, p, r]
+        right = jnp.where(column < tcols - 1, jnp.where(even, fa, fb), 0).astype(BF)
+        left = jnp.where(column > 0, jnp.where(even, fb, fa), 0).astype(BF)
+        e_ref[at, :, 0:2, lane] = x_ref[f, p, r, cols - 2 :]
+        e_ref[at, :, 2:4, lane] = right
+        e_ref[at, :, 4:6, lane] = left
+        e_ref[at, :, 6:8, lane] = x_ref[f, p, r, :2]
+
+
+def edge_kernel(x_ref, fa_ref, fb_ref, a_ref, b_ref, e_ref):
     frames, pairs, _, cols, c = x_ref.shape
-    column, row, tcols = place()
-    has_left, has_right = column > 0, column < tcols - 1
-    even = lax.rem(column, 2) == 0
+    _, row, _ = place()
     upper = lax.rem(row, 2) == 0
     for f in range(frames):
+        for k, p in enumerate((0, pairs - 1)):
+            group_of(x_ref, fa_ref, fb_ref, f, slice(p, p + 1), e_ref, 2 * f + k)
         for r in range(2):
             lane = pl.ds(r * c, c)
-            fa, fb = fa_ref[f, :, r], fb_ref[f, :, r]
-            right = jnp.where(has_right, jnp.where(even, fa, fb), 0).astype(BF)
-            left = jnp.where(has_left, jnp.where(even, fb, fa), 0).astype(BF)
-            e_ref[f, :, 0:2, lane] = x_ref[f, :, r, cols - 2 :]
-            e_ref[f, :, 2:4, lane] = right
-            e_ref[f, :, 4:6, lane] = left
-            e_ref[f, :, 6:8, lane] = x_ref[f, :, r, :2]
             top, bottom = x_ref[f, 0, r], x_ref[f, pairs - 1, r]
             a_ref[f, 0:cols, lane] = jnp.where(upper, bottom, top)
             b_ref[f, 0:cols, lane] = jnp.where(upper, top, bottom)
-        top, bottom = e_ref[f, 0], e_ref[f, pairs - 1]
+        top, bottom = e_ref[2 * f, 0], e_ref[2 * f + 1, 0]
         a_ref[f, cols:, :] = jnp.where(upper, bottom, top)
         b_ref[f, cols:, :] = jnp.where(upper, top, bottom)
 
@@ -151,13 +188,13 @@
     return jnp.concatenate([ref[f : f + 1]] * 2, axis=-1)
 
 
-def inner_kernel(e_ref, w_ref, d_ref, r_ref, wide):
+def inner_kernel(x_ref, fa_ref, fb_ref, wide, d_ref, r_ref, e_ref):
     frames, pairs, _, c2 = e_ref.shape
     n2 = r_ref.shape[3]
-    spread(w_ref, wide)
     state = None
     blank = jnp.zeros((8, 3 * n2), F32)
     for f in range(frames):
+        group_of(x_ref, fa_ref, fb_ref, f, slice(None), e_ref, f)
         e = e_ref[f].reshape(pairs * 8, c2)
         high, low = dot(e, wide[:c2]), dot(e, wide[c2:])
         y = jnp.concatenate([blank, high]) + jnp.concatenate([low, blank])
@@ -166,13 +203,12 @@
         r_ref[f] = state
 
 
-def ring_kernel(va_ref, vb_ref, p_ref, w_ref, d_ref, r_ref, c_ref, m_ref, wide):
+def ring_kernel(va_ref, vb_ref, p_ref, wide, d_ref, r_ref, c_ref, m_ref):
     frames, size, c2 = va_ref.shape
     pairs, n2 = r_ref.shape[1] - 1, r_ref.shape[3]
     cols = size - 8
     _, row, _ = place()
     upper = lax.rem(row, 2) == 0
-    spread(w_ref, wide)
     last = frames - 1
     r_ref[...] = p_ref[...]
     for side, there in enumerate((row > 0, row < TROWS - 1)):
@@ -207,11 +243,17 @@
 
 def read_kernel(first, *refs):
     s_ref, m_ref, w_ref, d_ref, skip_ref, x_ref = refs[:6]
-    o_ref, side_ref, rim_ref, wide, held, out, sems = refs[-7:]
+    if first == 0:
+        wide = refs[-4]
+        spread(w_ref, wide)
+        o_ref, side_ref, rim_ref = refs[-7:-4]
+    else:
+        wide = w_ref
+        o_ref, side_ref, rim_ref = refs[-6:-3]
+    held, out, sems = refs[-3:]
     _, pairs, _, cols, _ = x_ref.shape
     n2 = s_ref.shape[3]
     half = n2 // 2
-    spread(w_ref, wide)
     later = (lax.axis_index("tm") > 0).astype(F32)
     gain = skip_ref[...].reshape(1, 1, half)
     factor = jnp.full((1, n2), 1.0, F32) * later
@@ -250,14 +292,13 @@
         copy.wait()
 
 
-def last_kernel(r_ref, c_ref, m_ref, w_ref, d_ref, *refs):
+def last_kernel(r_ref, c_ref, m_ref, wide, d_ref, *refs):
     count = (len(refs) - 7) // 2
     sides, rims = refs[:count], refs[count : 2 * count]
-    o_ref, wide, held, left, right, rows, sems = refs[2 * count :][-7:]
+    o_ref, held, left, right, rows, sems = refs[-6:]
     frames, rest, _, n2 = r_ref.shape
     pairs, half = rest - 1, n2 // 2
     cols = c_ref.shape[2]
-    spread(w_ref, wide)
     column, _, tcols = place()
     later = (lax.axis_index("tm") > 0).astype(F32)
     factor = jnp.full((1, n2), 1.0, F32) * later
@@ -352,70 +393,87 @@
         [pltpu.SemaphoreType.DMA((count,))],
         in_specs=[pl.BlockSpec(memory_space=pltpu.HBM)],
     )
+    wide_in = shape((4 * c, 3 * n2), BF)
+    wide_out = shape((2 * n2, 6 * c), BF)
+    head = blocks(pairs)[0]
+    pre = call(
+        early_kernel,
+        shape((count, head[-1][0] + head[-1][1], cols, n2), F32),
+        (here, w_in, decay),
+        [pltpu.VMEM(wide_in.shape, BF)],
+    )
+    side_a, side_b, pre = lax.optimization_barrier((side_a, side_b, pre))
     from_a = swapped(side_a, True, 0)
     from_b = swapped(side_b, True, 1)
-    wide_in = pltpu.VMEM((4 * c, 3 * n2), BF)
-    wide_out = pltpu.VMEM((2 * n2, 3 * 2 * c), BF)
-    local, message = call(
+    local, message, wide_in = call(
         main_kernel,
-        (shape((count, pairs + 1, cols, n2), F32), shape((pairs + 1, cols, n2), BF)),
-        (here, w_in, decay),
-        [wide_in],
+        (
+            shape((count, pairs + 1, cols, n2), F32),
+            shape((pairs + 1, cols, n2), BF),
+            wide_in,
+        ),
+        (here, w_in, decay, pre),
     )
     before = onward(message)
     from_a, from_b, local = lax.optimization_barrier((from_a, from_b, local))
-    edge, row_a, row_b = call(
-        edge_kernel, (shape((count, pairs, 8, 2 * c), BF), across, across), (here, from_a, from_b)
+    row_a, row_b = call(
+        edge_kernel,
+        (across, across),
+        (here, from_a, from_b),
+        [pltpu.VMEM((2 * count, 1, 8, 2 * c), BF)],
     )
     rows_a = swapped(row_a, False, 0)
     rows_b = swapped(row_b, False, 1)
     edge_states = shape((count, pairs + 1, 8, n2), F32)
-    edge, local, before = lax.optimization_barrier((edge, local, before))
-    partial = call(inner_kernel, edge_states, (edge, w_in, decay), [wide_in])
+    partial = call(
+        inner_kernel,
+        edge_states,
+        (here, from_a, from_b, wide_in, decay),
+        [pltpu.VMEM((count, pairs, 8, 2 * c), BF)],
+    )
     part = count // 2
 
-    def read(first, mixed, local):
-        given = (local, before, w_out, decay, skip.reshape(1, c), here)
+    def read(first, weight, mixed, local):
+        given = (local, before, weight, decay, skip.reshape(1, c), here)
+        extra = [] if first == 0 else [mixed]
+        outs = (
+            shape(video.shape, BF),
+            shape((part, pairs, 16, n2), F32),
+            shape((part, 2, cols - 16, n2), F32),
+        )
+        more = (wide_out,) if first == 0 else ()
         return call(
             functools.partial(read_kernel, first),
-            (
-                shape(video.shape, BF),
-                shape((part, pairs, 16, n2), F32),
-                shape((part, 2, cols - 16, n2), F32),
-            ),
-            given if mixed is None else (*given, mixed),
+            (*outs, *more),
+            (*given, *extra),
             [
-                wide_out,
                 pltpu.VMEM((pairs + 1, cols, n2), BF),
                 pltpu.VMEM((part, pairs, 2, cols - 16, c), BF),
                 pltpu.SemaphoreType.DMA((part,)),
             ],
-            in_specs=[VM] * len(given) + ([] if mixed is None else [ANY]),
-            out_specs=(ANY, VM, VM),
-            aliases={} if mixed is None else {len(given): 0},
+            in_specs=[VM] * len(given) + [ANY] * len(extra),
+            out_specs=(ANY, *[VM] * (len(outs) + len(more) - 1)),
+            aliases={len(given): 0} if extra else {},
         )
 
-    mixed, side_0, rim_0 = read(0, None, local)
+    mixed, side_0, rim_0, wide_out = read(0, w_out, None, local)
     rows_a, rows_b, partial, side_0, local = lax.optimization_barrier(
         (rows_a, rows_b, partial, side_0, local)
     )
     ends, rim, message = call(
         ring_kernel,
         (edge_states, shape((count, 2, cols, n2), F32), shape((pairs + 1 + cols // 4, 8, n2), BF)),
-        (rows_a, rows_b, partial, w_in, decay),
-        [wide_in],
+        (rows_a, rows_b, partial, wide_in, decay),
     )
     ring_before = onward(message)
-    ends, local = lax.optimization_barrier((ends, local))
-    mixed, side_1, rim_1 = read(part, mixed, local)
+    mixed, side_1, rim_1 = read(part, wide_out, mixed, local)
     ring_before, side_1 = lax.optimization_barrier((ring_before, side_1))
-    given = (ends, rim, ring_before, w_out, decay, side_0, side_1, rim_0, rim_1)
+    given = (ends, rim, ring_before, wide_out, decay, side_0, side_1, rim_0, rim_1)
     mixed = call(
         last_kernel,
         shape(video.shape, BF),
         (*given, mixed),
         [
-            wide_out,
             pltpu.VMEM(((count + 1) // 2, pairs + 1, 8, n2), BF),
             pltpu.VMEM((count, pairs, 2, 8, c), BF),
             pltpu.VMEM((count, pairs, 2, 8, c), BF),

time: 31.3 us -> 31.4 us (level)
  Pallas kernels: 15.6 us -> 15.2 us
    pallas_call x8 -> x9, Pallas kernels: 15.6 us -> 15.2 us  [call(): pl.pallas_call(body, out_shape=outs, in_specs=in_specs or [VM] * len(ins)...]
where the time goes in v4:
time: 31.4 us; the launch traced here: 31.2 us
  Pallas kernels  15.2 us (48%)
  starting transfers between devices  11 us (35%)
  waiting for transfers between devices  4.65 us (15%)
  between operations  0.32 us (1%)
    pallas_call x9, Pallas kernels, call(): pl.pallas_call(body, out_shape=outs, in_specs=in_specs or [VM] * len(ins)...  15.2 us
    ppermute x4, starting transfers between devices, swapped(): return lax.ppermute(value, 'tile', pairs)  9.05 us
    ppermute x4, waiting for transfers between devices, swapped(): return lax.ppermute(value, 'tile', pairs)  4.64 us
    ppermute x2, starting transfers between devices, onward(): lax.ppermute(value, 'tm', [(i, (i + 1) % groups) for i in range(groups)])  1.97 us
  transfers between devices with their start and end apart: 6, of which 2 were waited for; matrix products, arithmetic and copies ran while one was open for 0% of the time, Pallas kernels for 23%

profile of v4, /device:TPU:13, one launch (start us, length us, event | category | flops | bytes accessed | tf_op | source)
XLA Modules:
  0.0 31.2 jit_solution(1979918542154085515)
XLA Ops:
  0.0 1.7 %shard_map.55 = (bf16[4,32,2,32,128]{4,3,2,1,0:T(8,128)(2,1)S(1)}, bf16[4,32,2,2,128]{4,3,2,1,0:T(2,128)(2,1)S(1)}, bf16[4,32,2,2,128]{4,3,2,1,0:T(2,128)(2,1)S(1)}) custom-call(bf16[4,32,2,32,128]{4,3,2,1,0:T(8,128)(2,1)} %bitcast.7), custom_call_target="tpu_custom_call" | custom-call | tf_op jit(solution)/shard_map/pallas_call | solution.py:370
  1.7 0.0 copy-done
  1.7 0.0 copy-done.2
  1.7 4.2 %shard_map.57 = (f32[4,33,32,256]{3,2,1,0:T(8,128)S(1)}, bf16[33,32,256]{2,1,0:T(8,128)(2,1)S(1)}, bf16[512,768]{1,0:T(8,128)(2,1)S(1)}) custom-call(bf16[4,32,2,32,128]{4,3,2,1,0:T(8,128)(2,1)S(1)} %get-tuple-element.36.x_ref.refs_5_, bf16[3,3,128,128]{3,2,1,0:T(8,128)(2,1)S(1)} %copy-done, f32[4,128]{1,0:T(4,128)S(1)} %copy-done.2, ...), custom_call_target="tpu_custom_call" | custom-call | tf_op jit(solution)/shard_map/pallas_call | solution.py:370
  6.0 0.7 %collective-permute-start.4 = (bf16[33,32,256]{2,1,0:T(8,128)(2,1)S(1)}, bf16[33,32,256]{2,1,0:T(8,128)(2,1)S(1)}, u32[]{:S(2)}, u32[]{:S(2)}) collective-permute-start(bf16[33,32,256]{2,1,0:T(8,128)(2,1)S(1)} %get-tuple-element.49), channel_id=1, source_target_pairs={{0,16},{16,0},{1,17},{17,1},{2,18},{18,2},{3,19},{19,3},{4,20},{20... | collective-permute-start | bytes 1622024 | tf_op jit(solution)/shard_map/ppermute | solution.py:36
  6.7 1.2 %collective-permute-start = (bf16[4,32,2,2,128]{4,3,2,1,0:T(2,128)(2,1)S(1)}, bf16[4,32,2,2,128]{4,3,2,1,0:T(2,128)(2,1)S(1)}, u32[]{:S(2)}, u32[]{:S(2)}) collective-permute-start(bf16[4,32,2,2,128]{4,3,2,1,0:T(2,128)(2,1)S(1)} %get-tuple-element.39), channel_id=1, source_target_pairs={{1,2},{2,1},{3,4},{4,3},{5,6},{6,5},{7,8},{8,7},{9,10},{10,9},{11,... | collective-permute-start | bytes 393224 | tf_op jit(solution)/shard_map/ppermute | solution.py:31
  7.8 3.2 %collective-permute-start.1 = (bf16[4,32,2,2,128]{4,3,2,1,0:T(2,128)(2,1)S(1)}, bf16[4,32,2,2,128]{4,3,2,1,0:T(2,128)(2,1)S(1)}, u32[]{:S(2)}, u32[]{:S(2)}) collective-permute-start(bf16[4,32,2,2,128]{4,3,2,1,0:T(2,128)(2,1)S(1)} %get-tuple-element.40), channel_id=1, source_target_pairs={{1,1},{2,3},{3,2},{4,4},{5,5},{6,7},{7,6},{8,8},{9,9},{10,11},{11,... | collective-permute-start | bytes 393224 | tf_op jit(solution)/shard_map/ppermute | solution.py:31
  11.0 1.6 %collective-permute-done.fa_ref = bf16[4,32,2,2,128]{4,3,2,1,0:T(2,128)(2,1)S(1)} collective-permute-done((bf16[4,32,2,2,128]{4,3,2,1,0:T(2,128)(2,1)S(1)}, bf16[4,32,2,2,128]{4,3,2,1,0:T(2,128)(2,1)S(1)}, u32[]{:S(2)}, u32[]{:S(2)}) %collective-permute-start) | collective-permute-done | bytes 131104 | tf_op jit(solution)/shard_map/ppermute | solution.py:31
  12.6 3.1 %collective-permute-done.1.fb_ref = bf16[4,32,2,2,128]{4,3,2,1,0:T(2,128)(2,1)S(1)} collective-permute-done((bf16[4,32,2,2,128]{4,3,2,1,0:T(2,128)(2,1)S(1)}, bf16[4,32,2,2,128]{4,3,2,1,0:T(2,128)(2,1)S(1)}, u32[]{:S(2)}, u32[]{:S(2)}) %collective-permute-start.1) | collective-permute-done | bytes 131104 | tf_op jit(solution)/shard_map/ppermute | solution.py:31
  15.7 0.1 shard_map.58
  15.7 2.3 %collective-permute-start.2 = (bf16[4,40,256]{2,1,0:T(8,128)(2,1)S(1)}, bf16[4,40,256]{2,1,0:T(8,128)(2,1)S(1)}, u32[]{:S(2)}, u32[]{:S(2)}) collective-permute-start(bf16[4,40,256]{2,1,0:T(8,128)(2,1)S(1)} %get-tuple-element.45), channel_id=1, source_target_pairs={{1,5},{2,6},{3,7},{4,8},{5,1},{6,2},{7,3},{8,4},{9,13},{10,14},{11... | collective-permute-start | bytes 245768 | tf_op jit(solution)/shard_map/ppermute | solution.py:31
  18.0 2.4 %collective-permute-start.3 = (bf16[4,40,256]{2,1,0:T(8,128)(2,1)S(1)}, bf16[4,40,256]{2,1,0:T(8,128)(2,1)S(1)}, u32[]{:S(2)}, u32[]{:S(2)}) collective-permute-start(bf16[4,40,256]{2,1,0:T(8,128)(2,1)S(1)} %get-tuple-element.46), channel_id=1, source_target_pairs={{1,1},{2,2},{3,3},{4,4},{5,9},{6,10},{7,11},{8,12},{9,5},{10,6},{1... | collective-permute-start | bytes 245768 | tf_op jit(solution)/shard_map/ppermute | solution.py:31
  20.5 0.0 copy-start.1
  20.5 0.0 copy-start.3
  20.5 1.5 %shard_map.59.p_ref = f32[4,33,8,256]{3,2,1,0:T(8,128)S(1)} custom-call(bf16[4,32,2,32,128]{4,3,2,1,0:T(8,128)(2,1)S(1)} %get-tuple-element.36.x_ref.refs_5_, bf16[4,32,2,2,128]{4,3,2,1,0:T(2,128)(2,1)S(1)} %collective-permute-done.fa_ref, bf16[4,32,2,2,128]{4,3,2,1,0:T(2,128)(2,1)S(1)} %collective-permute-done.1.fb_ref, ...), custom_call_target="tpu_custom_call" | custom-call | tf_op jit(solution)/shard_map/pallas_call | solution.py:370
  22.0 0.0 collective-permute-done.4.refs_1_
  22.0 2.8 %shard_map.60 = (bf16[4,32,2,32,128]{4,3,2,1,0:T(8,128)(2,1)}, f32[2,32,16,256]{3,2,1,0:T(8,128)S(1)}, f32[2,2,16,256]{3,2,1,0:T(8,128)S(1)}, bf16[512,768]{1,0:T(8,128)(2,1)S(1)}) custom-call(f32[4,33,32,256]{3,2,1,0:T(8,128)S(1)} %get-tuple-element.57.refs_0_, bf16[33,32,256]{2,1,0:T(8,128)(2,1)S(1)} %collective-permute-done.4.refs_1_, ...), custom_call_target="tpu_custom_call" | custom-call | tf_op jit(solution)/shard_map/pallas_call | solution.py:370
  24.8 0.0 collective-permute-done.2.va_ref
  24.8 0.0 collective-permute-done.3.vb_ref
  24.8 0.3 %shard_map.61 = (f32[4,33,8,256]{3,2,1,0:T(8,128)S(1)}, f32[4,2,32,256]{3,2,1,0:T(8,128)S(1)}, bf16[41,8,256]{2,1,0:T(8,128)(2,1)S(1)}) custom-call(bf16[4,40,256]{2,1,0:T(8,128)(2,1)S(1)} %collective-permute-done.2.va_ref, bf16[4,40,256]{2,1,0:T(8,128)(2,1)S(1)} %collective-permute-done.3.vb_ref, f32[4,33,8,256]{3,2,1,0:T(8,128)S(1)} %shard_map.59.p_ref, ...), custom_call_target="tpu_custom_call" | custom-call | tf_op jit(solution)/shard_map/pallas_call | solution.py:370
  25.2 1.2 %collective-permute-start.5 = (bf16[41,8,256]{2,1,0:T(8,128)(2,1)S(1)}, bf16[41,8,256]{2,1,0:T(8,128)(2,1)S(1)}, u32[]{:S(2)}, u32[]{:S(2)}) collective-permute-start(bf16[41,8,256]{2,1,0:T(8,128)(2,1)S(1)} %get-tuple-element.56), channel_id=1, source_target_pairs={{0,16},{16,0},{1,17},{17,1},{2,18},{18,2},{3,19},{19,3},{4,20},{20... | collective-permute-start | bytes 503816 | tf_op jit(solution)/shard_map/ppermute | solution.py:36
  26.4 2.7 %shard_map.62 = (bf16[4,32,2,32,128]{4,3,2,1,0:T(8,128)(2,1)}, f32[2,32,16,256]{3,2,1,0:T(8,128)S(1)}, f32[2,2,16,256]{3,2,1,0:T(8,128)S(1)}) custom-call(f32[4,33,32,256]{3,2,1,0:T(8,128)S(1)} %get-tuple-element.57.refs_0_, bf16[33,32,256]{2,1,0:T(8,128)(2,1)S(1)} %collective-permute-done.4.refs_1_, ...), custom_call_target="tpu_custom_call", output_to_operand_aliasing={{0}: (6, {})} | custom-call | tf_op jit(solution)/shard_map/pallas_call | solution.py:370
  29.1 0.0 collective-permute-done.5.m_ref
  29.1 1.9 %shard_map.63 = bf16[4,32,2,32,128]{4,3,2,1,0:T(8,128)(2,1)} custom-call(f32[4,33,8,256]{3,2,1,0:T(8,128)S(1)} %get-tuple-element.54.r_ref, f32[4,2,32,256]{3,2,1,0:T(8,128)S(1)} %get-tuple-element.55.c_ref, bf16[41,8,256]{2,1,0:T(8,128)(2,1)S(1)} %collective-permute-done.5.m_ref, ...), custom_call_target="tpu_custom_call", output_to_operand_aliasing={{}: (9, {})} | custom-call | tf_op jit(solution)/shard_map/pallas_call | solution.py:370
  (5 shorter events, 0.0 us)
Async XLA Ops:
  0.0 1.7 %copy-start = (bf16[3,3,128,128]{3,2,1,0:T(8,128)(2,1)S(1)}, bf16[3,3,128,128]{3,2,1,0:T(8,128)(2,1)}, u32[]{:S(2)}) copy-start(bf16[3,3,128,128]{3,2,1,0:T(8,128)(2,1)} %w_ref.3) | copy-start | bytes 884740
  0.0 1.7 %copy-start.2 = (f32[4,128]{1,0:T(4,128)S(1)}, f32[4,128]{1,0:T(4,128)}, u32[]{:S(2)}) copy-start(f32[4,128]{1,0:T(4,128)} %d_ref.9) | copy-start | bytes 6148
  6.0 16.1 %collective-permute-start.4 = (bf16[33,32,256]{2,1,0:T(8,128)(2,1)S(1)}, bf16[33,32,256]{2,1,0:T(8,128)(2,1)S(1)}, u32[]{:S(2)}, u32[]{:S(2)}) collective-permute-start(bf16[33,32,256]{2,1,0:T(8,128)(2,1)S(1)} %get-tuple-element.49), channel_id=1, source_target_pairs={{0,16},{16,0},{1,17},{17,1},{2,18},{18,2},{3,19},{19,3},{4,20},{20... | collective-permute-start | bytes 1622024 | tf_op jit(solution)/shard_map/ppermute | solution.py:36
  6.7 5.9 %collective-permute-start = (bf16[4,32,2,2,128]{4,3,2,1,0:T(2,128)(2,1)S(1)}, bf16[4,32,2,2,128]{4,3,2,1,0:T(2,128)(2,1)S(1)}, u32[]{:S(2)}, u32[]{:S(2)}) collective-permute-start(bf16[4,32,2,2,128]{4,3,2,1,0:T(2,128)(2,1)S(1)} %get-tuple-element.39), channel_id=1, source_target_pairs={{1,2},{2,1},{3,4},{4,3},{5,6},{6,5},{7,8},{8,7},{9,10},{10,9},{11,... | collective-permute-start | bytes 393224 | tf_op jit(solution)/shard_map/ppermute | solution.py:31
  7.8 7.8 %collective-permute-start.1 = (bf16[4,32,2,2,128]{4,3,2,1,0:T(2,128)(2,1)S(1)}, bf16[4,32,2,2,128]{4,3,2,1,0:T(2,128)(2,1)S(1)}, u32[]{:S(2)}, u32[]{:S(2)}) collective-permute-start(bf16[4,32,2,2,128]{4,3,2,1,0:T(2,128)(2,1)S(1)} %get-tuple-element.40), channel_id=1, source_target_pairs={{1,1},{2,3},{3,2},{4,4},{5,5},{6,7},{7,6},{8,8},{9,9},{10,11},{11,... | collective-permute-start | bytes 393224 | tf_op jit(solution)/shard_map/ppermute | solution.py:31
  15.7 9.1 %collective-permute-start.2 = (bf16[4,40,256]{2,1,0:T(8,128)(2,1)S(1)}, bf16[4,40,256]{2,1,0:T(8,128)(2,1)S(1)}, u32[]{:S(2)}, u32[]{:S(2)}) collective-permute-start(bf16[4,40,256]{2,1,0:T(8,128)(2,1)S(1)} %get-tuple-element.45), channel_id=1, source_target_pairs={{1,5},{2,6},{3,7},{4,8},{5,1},{6,2},{7,3},{8,4},{9,13},{10,14},{11... | collective-permute-start | bytes 245768 | tf_op jit(solution)/shard_map/ppermute | solution.py:31
  18.0 6.8 %collective-permute-start.3 = (bf16[4,40,256]{2,1,0:T(8,128)(2,1)S(1)}, bf16[4,40,256]{2,1,0:T(8,128)(2,1)S(1)}, u32[]{:S(2)}, u32[]{:S(2)}) collective-permute-start(bf16[4,40,256]{2,1,0:T(8,128)(2,1)S(1)} %get-tuple-element.46), channel_id=1, source_target_pairs={{1,1},{2,2},{3,3},{4,4},{5,9},{6,10},{7,11},{8,12},{9,5},{10,6},{1... | collective-permute-start | bytes 245768 | tf_op jit(solution)/shard_map/ppermute | solution.py:31
  20.5 1.5 %copy-start.1 = (bf16[3,3,128,128]{3,2,1,0:T(8,128)(2,1)S(1)}, bf16[3,3,128,128]{3,2,1,0:T(8,128)(2,1)}, u32[]{:S(2)}) copy-start(bf16[3,3,128,128]{3,2,1,0:T(8,128)(2,1)} %refs_2_.1) | copy-start | bytes 884740
  20.5 1.5 %copy-start.3 = (f32[128]{0:T(128)S(1)}, f32[128]{0:T(128)}, u32[]{:S(2)}) copy-start(f32[128]{0:T(128)} %param.9) | copy-start | bytes 1540
  25.2 3.9 %collective-permute-start.5 = (bf16[41,8,256]{2,1,0:T(8,128)(2,1)S(1)}, bf16[41,8,256]{2,1,0:T(8,128)(2,1)S(1)}, u32[]{:S(2)}, u32[]{:S(2)}) collective-permute-start(bf16[41,8,256]{2,1,0:T(8,128)(2,1)S(1)} %get-tuple-element.56), channel_id=1, source_target_pairs={{0,16},{16,0},{1,17},{17,1},{2,18},{18,2},{3,19},{19,3},{4,20},{20... | collective-permute-start | bytes 503816 | tf_op jit(solution)/shard_map/ppermute | solution.py:36

commit v5 on v4

--- a/solution.py
+++ b/solution.py
@@ -16,19 +16,25 @@
 ANY = pl.BlockSpec(memory_space=pl.ANY)
 
 
-def swapped(value, across, first):
+def swapped(value, across, first, spare=False):
     count = lax.axis_size("tile")
     tcols = count // TROWS
-    pairs = []
+    there, left = {}, []
     for number in range(count):
         row, column = divmod(number, tcols)
         at, size = (column, tcols) if across else (row, TROWS)
         other = at + 1 if at >= first and (at - first) % 2 == 0 else at - 1
-        if not first <= other < size:
-            other = at
-        there = row * tcols + other if across else other * tcols + column
-        pairs.append(((number + 1) % count, (there + 1) % count))
-    return lax.ppermute(value, "tile", pairs)
+        me = (number + 1) % count
+        if first <= other < size:
+            there[me] = ((row * tcols + other if across else other * tcols + column) + 1) % count
+        else:
+            there[me] = me
+            left.append(me)
+    left.sort()
+    if spare:
+        for a, b in zip(left[::2], left[1::2]):
+            there[a], there[b] = b, a
+    return lax.ppermute(value, "tile", sorted(there.items()))
 
 
 def onward(value):
@@ -78,9 +84,9 @@
 
 
 def blocks(pairs):
-    every = [(0, 1), *((q, min(BLOCK, pairs - q)) for q in range(1, pairs, BLOCK)), (pairs, 1)]
-    cut = pairs // 2 + 1
-    return [b for b in every if b[0] + b[1] <= cut], [b for b in every if b[0] + b[1] > cut]
+    cut = pairs // 4 + 1
+    head = [(0, 1), (1, cut - 1)]
+    return head, [*((q, min(BLOCK, pairs - q)) for q in range(cut, pairs, BLOCK)), (pairs, 1)]
 
 
 def ahead():
@@ -423,7 +429,7 @@
         [pltpu.VMEM((2 * count, 1, 8, 2 * c), BF)],
     )
     rows_a = swapped(row_a, False, 0)
-    rows_b = swapped(row_b, False, 1)
+    rows_b = swapped(row_b, False, 1, True)
     edge_states = shape((count, pairs + 1, 8, n2), F32)
     partial = call(
         inner_kernel,

time: 31.4 us -> 29.7 us (0.946)
  the two profiles are of different devices: /device:TPU:13 before, /device:TPU:0 now
where the time goes in v5:
time: 29.7 us; the launch traced here: 29.6 us
  Pallas kernels  15.5 us (52%)
  starting transfers between devices  9.61 us (32%)
  waiting for transfers between devices  4.16 us (14%)
    pallas_call x9, Pallas kernels, call(): pl.pallas_call(body, out_shape=outs, in_specs=in_specs or [VM] * len(ins)...  15.5 us
    ppermute x4, starting transfers between devices, swapped(): return lax.ppermute(value, 'tile', sorted(there.items()))  8.98 us
    ppermute x4, waiting for transfers between devices, swapped(): return lax.ppermute(value, 'tile', sorted(there.items()))  4.16 us
    ppermute x2, starting transfers between devices, onward(): lax.ppermute(value, 'tm', [(i, (i + 1) % groups) for i in range(groups)])  0.63 us
  transfers between devices with their start and end apart: 6, of which 2 were waited for; matrix products, arithmetic and copies ran while one was open for 0% of the time, Pallas kernels for 24%

profile of v5, /device:TPU:0, one launch (start us, length us, event | category | flops | bytes accessed | tf_op | source)
XLA Modules:
  0.0 29.6 jit_solution(7172558653916087915)
XLA Ops:
  0.0 1.7 %shard_map.55 = (bf16[4,32,2,32,128]{4,3,2,1,0:T(8,128)(2,1)S(1)}, bf16[4,32,2,2,128]{4,3,2,1,0:T(2,128)(2,1)S(1)}, bf16[4,32,2,2,128]{4,3,2,1,0:T(2,128)(2,1)S(1)}) custom-call(bf16[4,32,2,32,128]{4,3,2,1,0:T(8,128)(2,1)} %bitcast.7), custom_call_target="tpu_custom_call" | custom-call | tf_op jit(solution)/shard_map/pallas_call | solution.py:376
  1.7 0.0 copy-done
  1.7 0.0 copy-done.2
  1.7 1.4 %shard_map.56.p_ref = f32[4,9,32,256]{3,2,1,0:T(8,128)S(1)} custom-call(bf16[4,32,2,32,128]{4,3,2,1,0:T(8,128)(2,1)S(1)} %get-tuple-element.36.x_ref.refs_5_, bf16[3,3,128,128]{3,2,1,0:T(8,128)(2,1)S(1)} %copy-done, f32[4,128]{1,0:T(4,128)S(1)} %copy-done.2), custom_call_target="tpu_custom_call" | custom-call | tf_op jit(solution)/shard_map/pallas_call | solution.py:376
  3.1 3.1 %shard_map.57 = (f32[4,33,32,256]{3,2,1,0:T(8,128)S(1)}, bf16[33,32,256]{2,1,0:T(8,128)(2,1)S(1)}, bf16[512,768]{1,0:T(8,128)(2,1)S(1)}) custom-call(bf16[4,32,2,32,128]{4,3,2,1,0:T(8,128)(2,1)S(1)} %get-tuple-element.36.x_ref.refs_5_, bf16[3,3,128,128]{3,2,1,0:T(8,128)(2,1)S(1)} %copy-done, f32[4,128]{1,0:T(4,128)S(1)} %copy-done.2, ...), custom_call_target="tpu_custom_call" | custom-call | tf_op jit(solution)/shard_map/pallas_call | solution.py:376
  6.2 0.6 %collective-permute-start.4 = (bf16[33,32,256]{2,1,0:T(8,128)(2,1)S(1)}, bf16[33,32,256]{2,1,0:T(8,128)(2,1)S(1)}, u32[]{:S(2)}, u32[]{:S(2)}) collective-permute-start(bf16[33,32,256]{2,1,0:T(8,128)(2,1)S(1)} %get-tuple-element.49), channel_id=1, source_target_pairs={{0,16},{16,0},{1,17},{17,1},{2,18},{18,2},{3,19},{19,3},{4,20},{20... | collective-permute-start | bytes 1622024 | tf_op jit(solution)/shard_map/ppermute | solution.py:42
  6.8 6.5 %collective-permute-start = (bf16[4,32,2,2,128]{4,3,2,1,0:T(2,128)(2,1)S(1)}, bf16[4,32,2,2,128]{4,3,2,1,0:T(2,128)(2,1)S(1)}, u32[]{:S(2)}, u32[]{:S(2)}) collective-permute-start(bf16[4,32,2,2,128]{4,3,2,1,0:T(2,128)(2,1)S(1)} %get-tuple-element.39), channel_id=1, source_target_pairs={{0,15},{1,2},{2,1},{3,4},{4,3},{5,6},{6,5},{7,8},{8,7},{9,10},{10,... | collective-permute-start | bytes 393224 | tf_op jit(solution)/shard_map/ppermute | solution.py:37
  13.2 0.8 %collective-permute-start.1 = (bf16[4,32,2,2,128]{4,3,2,1,0:T(2,128)(2,1)S(1)}, bf16[4,32,2,2,128]{4,3,2,1,0:T(2,128)(2,1)S(1)}, u32[]{:S(2)}, u32[]{:S(2)}) collective-permute-start(bf16[4,32,2,2,128]{4,3,2,1,0:T(2,128)(2,1)S(1)} %get-tuple-element.40), channel_id=1, source_target_pairs={{0,0},{1,1},{2,3},{3,2},{4,4},{5,5},{6,7},{7,6},{8,8},{9,9},{10,11... | collective-permute-start | bytes 393224 | tf_op jit(solution)/shard_map/ppermute | solution.py:37
  14.1 3.3 %collective-permute-done.fa_ref = bf16[4,32,2,2,128]{4,3,2,1,0:T(2,128)(2,1)S(1)} collective-permute-done((bf16[4,32,2,2,128]{4,3,2,1,0:T(2,128)(2,1)S(1)}, bf16[4,32,2,2,128]{4,3,2,1,0:T(2,128)(2,1)S(1)}, u32[]{:S(2)}, u32[]{:S(2)}) %collective-permute-start) | collective-permute-done | bytes 131104 | tf_op jit(solution)/shard_map/ppermute | solution.py:37
  17.4 0.0 collective-permute-done.1.fb_ref
  17.4 0.1 shard_map.58
  17.5 1.7 %collective-permute-start.2 = (bf16[4,40,256]{2,1,0:T(8,128)(2,1)S(1)}, bf16[4,40,256]{2,1,0:T(8,128)(2,1)S(1)}, u32[]{:S(2)}, u32[]{:S(2)}) collective-permute-start(bf16[4,40,256]{2,1,0:T(8,128)(2,1)S(1)} %get-tuple-element.45), channel_id=1, source_target_pairs={{0,12},{1,5},{2,6},{3,7},{4,8},{5,1},{6,2},{7,3},{8,4},{9,13},{10,... | collective-permute-start | bytes 245768 | tf_op jit(solution)/shard_map/ppermute | solution.py:37
  19.2 0.0 collective-permute-start.3
  19.2 1.5 %shard_map.59.p_ref = f32[4,33,8,256]{3,2,1,0:T(8,128)S(1)} custom-call(bf16[4,32,2,32,128]{4,3,2,1,0:T(8,128)(2,1)S(1)} %get-tuple-element.36.x_ref.refs_5_, bf16[4,32,2,2,128]{4,3,2,1,0:T(2,128)(2,1)S(1)} %collective-permute-done.fa_ref, bf16[4,32,2,2,128]{4,3,2,1,0:T(2,128)(2,1)S(1)} %collective-permute-done.1.fb_ref, ...), custom_call_target="tpu_custom_call" | custom-call | tf_op jit(solution)/shard_map/pallas_call | solution.py:376
  20.7 0.0 collective-permute-done.4.refs_1_
  20.8 0.0 copy-done.1
  20.8 2.8 %shard_map.60 = (bf16[4,32,2,32,128]{4,3,2,1,0:T(8,128)(2,1)}, f32[2,32,16,256]{3,2,1,0:T(8,128)S(1)}, f32[2,2,16,256]{3,2,1,0:T(8,128)S(1)}, bf16[512,768]{1,0:T(8,128)(2,1)S(1)}) custom-call(f32[4,33,32,256]{3,2,1,0:T(8,128)S(1)} %get-tuple-element.57.refs_0_, bf16[33,32,256]{2,1,0:T(8,128)(2,1)S(1)} %collective-permute-done.4.refs_1_, ...), custom_call_target="tpu_custom_call" | custom-call | tf_op jit(solution)/shard_map/pallas_call | solution.py:376
  23.5 0.8 %collective-permute-done.2.va_ref = bf16[4,40,256]{2,1,0:T(8,128)(2,1)S(1)} collective-permute-done((bf16[4,40,256]{2,1,0:T(8,128)(2,1)S(1)}, bf16[4,40,256]{2,1,0:T(8,128)(2,1)S(1)}, u32[]{:S(2)}, u32[]{:S(2)}) %collective-permute-start.2) | collective-permute-done | bytes 81952 | tf_op jit(solution)/shard_map/ppermute | solution.py:37
  24.4 0.0 collective-permute-done.3.vb_ref
  24.4 0.3 %shard_map.61 = (f32[4,33,8,256]{3,2,1,0:T(8,128)S(1)}, f32[4,2,32,256]{3,2,1,0:T(8,128)S(1)}, bf16[41,8,256]{2,1,0:T(8,128)(2,1)S(1)}) custom-call(bf16[4,40,256]{2,1,0:T(8,128)(2,1)S(1)} %collective-permute-done.2.va_ref, bf16[4,40,256]{2,1,0:T(8,128)(2,1)S(1)} %collective-permute-done.3.vb_ref, f32[4,33,8,256]{3,2,1,0:T(8,128)S(1)} %shard_map.59.p_ref, ...), custom_call_target="tpu_custom_call" | custom-call | tf_op jit(solution)/shard_map/pallas_call | solution.py:376
  24.7 0.1 collective-permute-start.5
  24.7 2.7 %shard_map.62 = (bf16[4,32,2,32,128]{4,3,2,1,0:T(8,128)(2,1)}, f32[2,32,16,256]{3,2,1,0:T(8,128)S(1)}, f32[2,2,16,256]{3,2,1,0:T(8,128)S(1)}) custom-call(f32[4,33,32,256]{3,2,1,0:T(8,128)S(1)} %get-tuple-element.57.refs_0_, bf16[33,32,256]{2,1,0:T(8,128)(2,1)S(1)} %collective-permute-done.4.refs_1_, ...), custom_call_target="tpu_custom_call", output_to_operand_aliasing={{0}: (6, {})} | custom-call | tf_op jit(solution)/shard_map/pallas_call | solution.py:376
  27.5 0.0 collective-permute-done.5.m_ref
  27.5 1.9 %shard_map.63 = bf16[4,32,2,32,128]{4,3,2,1,0:T(8,128)(2,1)} custom-call(f32[4,33,8,256]{3,2,1,0:T(8,128)S(1)} %get-tuple-element.54.r_ref, f32[4,2,32,256]{3,2,1,0:T(8,128)S(1)} %get-tuple-element.55.c_ref, bf16[41,8,256]{2,1,0:T(8,128)(2,1)S(1)} %collective-permute-done.5.m_ref, ...), custom_call_target="tpu_custom_call", output_to_operand_aliasing={{}: (9, {})} | custom-call | tf_op jit(solution)/shard_map/pallas_call | solution.py:376
  (5 shorter events, 0.0 us)
Async XLA Ops:
  0.0 1.7 %copy-start = (bf16[3,3,128,128]{3,2,1,0:T(8,128)(2,1)S(1)}, bf16[3,3,128,128]{3,2,1,0:T(8,128)(2,1)}, u32[]{:S(2)}) copy-start(bf16[3,3,128,128]{3,2,1,0:T(8,128)(2,1)} %w_ref.3) | copy-start | bytes 884740
  0.0 1.7 %copy-start.2 = (f32[4,128]{1,0:T(4,128)S(1)}, f32[4,128]{1,0:T(4,128)}, u32[]{:S(2)}) copy-start(f32[4,128]{1,0:T(4,128)} %d_ref.9) | copy-start | bytes 6148
  6.2 14.5 %collective-permute-start.4 = (bf16[33,32,256]{2,1,0:T(8,128)(2,1)S(1)}, bf16[33,32,256]{2,1,0:T(8,128)(2,1)S(1)}, u32[]{:S(2)}, u32[]{:S(2)}) collective-permute-start(bf16[33,32,256]{2,1,0:T(8,128)(2,1)S(1)} %get-tuple-element.49), channel_id=1, source_target_pairs={{0,16},{16,0},{1,17},{17,1},{2,18},{18,2},{3,19},{19,3},{4,20},{20... | collective-permute-start | bytes 1622024 | tf_op jit(solution)/shard_map/ppermute | solution.py:42
  6.8 10.6 %collective-permute-start = (bf16[4,32,2,2,128]{4,3,2,1,0:T(2,128)(2,1)S(1)}, bf16[4,32,2,2,128]{4,3,2,1,0:T(2,128)(2,1)S(1)}, u32[]{:S(2)}, u32[]{:S(2)}) collective-permute-start(bf16[4,32,2,2,128]{4,3,2,1,0:T(2,128)(2,1)S(1)} %get-tuple-element.39), channel_id=1, source_target_pairs={{0,15},{1,2},{2,1},{3,4},{4,3},{5,6},{6,5},{7,8},{8,7},{9,10},{10,... | collective-permute-start | bytes 393224 | tf_op jit(solution)/shard_map/ppermute | solution.py:37
  13.2 4.2 %collective-permute-start.1 = (bf16[4,32,2,2,128]{4,3,2,1,0:T(2,128)(2,1)S(1)}, bf16[4,32,2,2,128]{4,3,2,1,0:T(2,128)(2,1)S(1)}, u32[]{:S(2)}, u32[]{:S(2)}) collective-permute-start(bf16[4,32,2,2,128]{4,3,2,1,0:T(2,128)(2,1)S(1)} %get-tuple-element.40), channel_id=1, source_target_pairs={{0,0},{1,1},{2,3},{3,2},{4,4},{5,5},{6,7},{7,6},{8,8},{9,9},{10,11... | collective-permute-start | bytes 393224 | tf_op jit(solution)/shard_map/ppermute | solution.py:37
  17.5 6.8 %collective-permute-start.2 = (bf16[4,40,256]{2,1,0:T(8,128)(2,1)S(1)}, bf16[4,40,256]{2,1,0:T(8,128)(2,1)S(1)}, u32[]{:S(2)}, u32[]{:S(2)}) collective-permute-start(bf16[4,40,256]{2,1,0:T(8,128)(2,1)S(1)} %get-tuple-element.45), channel_id=1, source_target_pairs={{0,12},{1,5},{2,6},{3,7},{4,8},{5,1},{6,2},{7,3},{8,4},{9,13},{10,... | collective-permute-start | bytes 245768 | tf_op jit(solution)/shard_map/ppermute | solution.py:37
  19.2 5.2 %collective-permute-start.3 = (bf16[4,40,256]{2,1,0:T(8,128)(2,1)S(1)}, bf16[4,40,256]{2,1,0:T(8,128)(2,1)S(1)}, u32[]{:S(2)}, u32[]{:S(2)}) collective-permute-start(bf16[4,40,256]{2,1,0:T(8,128)(2,1)S(1)} %get-tuple-element.46), channel_id=1, source_target_pairs={{0,1},{1,0},{2,3},{3,2},{4,13},{5,9},{6,10},{7,11},{8,12},{9,5},{1... | collective-permute-start | bytes 245768 | tf_op jit(solution)/shard_map/ppermute | solution.py:37
  19.2 1.6 %copy-start.1 = (bf16[3,3,128,128]{3,2,1,0:T(8,128)(2,1)S(1)}, bf16[3,3,128,128]{3,2,1,0:T(8,128)(2,1)}, u32[]{:S(2)}) copy-start(bf16[3,3,128,128]{3,2,1,0:T(8,128)(2,1)} %refs_2_.1) | copy-start | bytes 884740
  19.2 1.6 %copy-start.3 = (f32[128]{0:T(128)S(1)}, f32[128]{0:T(128)}, u32[]{:S(2)}) copy-start(f32[128]{0:T(128)} %param.9) | copy-start | bytes 1540
  24.7 2.8 %collective-permute-start.5 = (bf16[41,8,256]{2,1,0:T(8,128)(2,1)S(1)}, bf16[41,8,256]{2,1,0:T(8,128)(2,1)S(1)}, u32[]{:S(2)}, u32[]{:S(2)}) collective-permute-start(bf16[41,8,256]{2,1,0:T(8,128)(2,1)S(1)} %get-tuple-element.56), channel_id=1, source_target_pairs={{0,16},{16,0},{1,17},{17,1},{2,18},{18,2},{3,19},{19,3},{4,20},{20... | collective-permute-start | bytes 503816 | tf_op jit(solution)/shard_map/ppermute | solution.py:42

commit v6 on v5

--- a/solution.py
+++ b/solution.py
@@ -12,6 +12,7 @@
 F32 = jnp.float32
 LIMIT = 24 << 20
 BLOCK = 16
+WIDE = 12
 VM = pl.BlockSpec(memory_space=pltpu.VMEM)
 ANY = pl.BlockSpec(memory_space=pl.ANY)
 
@@ -85,8 +86,7 @@
 
 def blocks(pairs):
     cut = pairs // 4 + 1
-    head = [(0, 1), (1, cut - 1)]
-    return head, [*((q, min(BLOCK, pairs - q)) for q in range(cut, pairs, BLOCK)), (pairs, 1)]
+    return [(0, cut)], [(q, min(WIDE, pairs + 1 - q)) for q in range(cut, pairs + 1, WIDE)]
 
 
 def ahead():
@@ -104,13 +104,16 @@
 
     for q, n in chosen:
         state = None
+        blank = jnp.zeros((cols, 3 * n2), F32)
         for f in range(frames):
-            y = None
-            if q > 0:
-                y = dot(rows(f, q - 1, n), wide[: 2 * c])
-            if q < pairs:
-                low = dot(rows(f, q, n), wide[2 * c :])
-                y = low if y is None else y + low
+            above, below = max(q - 1, 0), min(q + n, pairs)
+            high = dot(rows(f, above, q + n - 1 - above), wide[: 2 * c])
+            low = dot(rows(f, q, below - q), wide[2 * c :])
+            if q == 0:
+                high = jnp.concatenate([blank, high])
+            if q + n > pairs:
+                low = jnp.concatenate([low, blank])
+            y = high + low
             y = gathered(y, n, cols, n2)
             state = y if f == 0 else twice(d_ref, f).reshape(1, 1, n2) * state + y
             s_ref[f, q : q + n] = state
@@ -197,13 +200,15 @@
 def inner_kernel(x_ref, fa_ref, fb_ref, wide, d_ref, r_ref, e_ref):
     frames, pairs, _, c2 = e_ref.shape
     n2 = r_ref.shape[3]
-    state = None
-    blank = jnp.zeros((8, 3 * n2), F32)
     for f in range(frames):
         group_of(x_ref, fa_ref, fb_ref, f, slice(None), e_ref, f)
-        e = e_ref[f].reshape(pairs * 8, c2)
-        high, low = dot(e, wide[:c2]), dot(e, wide[c2:])
-        y = jnp.concatenate([blank, high]) + jnp.concatenate([low, blank])
+    e = e_ref[...].reshape(frames * pairs * 8, c2)
+    high = dot(e, wide[:c2]).reshape(frames, pairs * 8, 3 * n2)
+    low = dot(e, wide[c2:]).reshape(frames, pairs * 8, 3 * n2)
+    blank = jnp.zeros((8, 3 * n2), F32)
+    state = None
+    for f in range(frames):
+        y = jnp.concatenate([blank, high[f]]) + jnp.concatenate([low[f], blank])
         y = gathered_edge(y, pairs + 1, n2)
         state = y if f == 0 else twice(d_ref, f).reshape(1, 1, n2) * state + y
         r_ref[f] = state
@@ -331,12 +336,13 @@
         y = dot(v, wide[n2:] if side else wide[:n2])
         edge_rows.append(gathered(y, frames, cols, n2))
     copies = []
+    size = held.shape[0] * pairs * 8
+    both = dot(held[:, :pairs].reshape(size, n2), wide[:n2])
+    both = both + dot(held[:, 1:].reshape(size, n2), wide[n2:])
+    both = both.reshape(held.shape[0], pairs, 8, 3 * n2)
     for f in range(frames):
         if f % 2 == 0:
-            e = held[f // 2]
-            y = dot(e[:pairs].reshape(pairs * 8, n2), wide[:n2])
-            y = y + dot(e[1:].reshape(pairs * 8, n2), wide[n2:])
-            y = y.reshape(pairs, 8, 3 * n2)
+            y = both[f // 2]
             y0, y1, y2 = y[:, :, :n2], y[:, :, n2 : 2 * n2], y[:, :, 2 * n2 :]
         col = lax.broadcasted_iota(jnp.int32, (pairs, 8, n2), 1)
         a, b, d, g = (3, 2, 5, 6) if f % 2 == 0 else (1, 0, 3, 4)

time: 29.7 us -> 29.3 us (0.987)
  Pallas kernels: 15.5 us -> 15.1 us
  waiting for transfers between devices: 4.16 us -> 4.48 us
    pallas_call x9, Pallas kernels: 15.5 us -> 15.1 us  [call(): pl.pallas_call(body, out_shape=outs, in_specs=in_specs or [VM] * len(ins)...]
    ppermute x4, waiting for transfers between devices: 4.16 us -> 4.47 us  [swapped(): return lax.ppermute(value, 'tile', sorted(there.items()))]
where the time goes in v6:
time: 29.3 us; the launch traced here: 29.1 us
  Pallas kernels  15.1 us (52%)
  starting transfers between devices  9.43 us (32%)
  waiting for transfers between devices  4.48 us (15%)
    pallas_call x9, Pallas kernels, call(): pl.pallas_call(body, out_shape=outs, in_specs=in_specs or [VM] * len(ins)...  15.1 us
    ppermute x4, starting transfers between devices, swapped(): return lax.ppermute(value, 'tile', sorted(there.items()))  8.8 us
    ppermute x4, waiting for transfers between devices, swapped(): return lax.ppermute(value, 'tile', sorted(there.items()))  4.47 us
    ppermute x2, starting transfers between devices, onward(): lax.ppermute(value, 'tm', [(i, (i + 1) % groups) for i in range(groups)])  0.63 us
  transfers between devices with their start and end apart: 6, of which 2 were waited for; matrix products, arithmetic and copies ran while one was open for 0% of the time, Pallas kernels for 24%

profile of v6, /device:TPU:0, one launch (start us, length us, event | category | flops | bytes accessed | tf_op | source)
XLA Modules:
  0.0 29.1 jit_solution(2630298642799476779)
XLA Ops:
  0.0 1.7 %shard_map.55 = (bf16[4,32,2,32,128]{4,3,2,1,0:T(8,128)(2,1)S(1)}, bf16[4,32,2,2,128]{4,3,2,1,0:T(2,128)(2,1)S(1)}, bf16[4,32,2,2,128]{4,3,2,1,0:T(2,128)(2,1)S(1)}) custom-call(bf16[4,32,2,32,128]{4,3,2,1,0:T(8,128)(2,1)} %bitcast.7), custom_call_target="tpu_custom_call" | custom-call | tf_op jit(solution)/shard_map/pallas_call | solution.py:382
  1.7 0.0 copy-done
  1.7 0.0 copy-done.2
  1.7 1.1 %shard_map.56.p_ref = f32[4,9,32,256]{3,2,1,0:T(8,128)S(1)} custom-call(bf16[4,32,2,32,128]{4,3,2,1,0:T(8,128)(2,1)S(1)} %get-tuple-element.36.x_ref.refs_5_, bf16[3,3,128,128]{3,2,1,0:T(8,128)(2,1)S(1)} %copy-done, f32[4,128]{1,0:T(4,128)S(1)} %copy-done.2), custom_call_target="tpu_custom_call" | custom-call | tf_op jit(solution)/shard_map/pallas_call | solution.py:382
  2.8 3.0 %shard_map.57 = (f32[4,33,32,256]{3,2,1,0:T(8,128)S(1)}, bf16[33,32,256]{2,1,0:T(8,128)(2,1)S(1)}, bf16[512,768]{1,0:T(8,128)(2,1)S(1)}) custom-call(bf16[4,32,2,32,128]{4,3,2,1,0:T(8,128)(2,1)S(1)} %get-tuple-element.36.x_ref.refs_5_, bf16[3,3,128,128]{3,2,1,0:T(8,128)(2,1)S(1)} %copy-done, f32[4,128]{1,0:T(4,128)S(1)} %copy-done.2, ...), custom_call_target="tpu_custom_call" | custom-call | tf_op jit(solution)/shard_map/pallas_call | solution.py:382
  5.9 0.6 %collective-permute-start.4 = (bf16[33,32,256]{2,1,0:T(8,128)(2,1)S(1)}, bf16[33,32,256]{2,1,0:T(8,128)(2,1)S(1)}, u32[]{:S(2)}, u32[]{:S(2)}) collective-permute-start(bf16[33,32,256]{2,1,0:T(8,128)(2,1)S(1)} %get-tuple-element.49), channel_id=1, source_target_pairs={{0,16},{16,0},{1,17},{17,1},{2,18},{18,2},{3,19},{19,3},{4,20},{20... | collective-permute-start | bytes 1622024 | tf_op jit(solution)/shard_map/ppermute | solution.py:43
  6.4 6.5 %collective-permute-start = (bf16[4,32,2,2,128]{4,3,2,1,0:T(2,128)(2,1)S(1)}, bf16[4,32,2,2,128]{4,3,2,1,0:T(2,128)(2,1)S(1)}, u32[]{:S(2)}, u32[]{:S(2)}) collective-permute-start(bf16[4,32,2,2,128]{4,3,2,1,0:T(2,128)(2,1)S(1)} %get-tuple-element.39), channel_id=1, source_target_pairs={{0,15},{1,2},{2,1},{3,4},{4,3},{5,6},{6,5},{7,8},{8,7},{9,10},{10,... | collective-permute-start | bytes 393224 | tf_op jit(solution)/shard_map/ppermute | solution.py:38
  12.9 0.7 %collective-permute-start.1 = (bf16[4,32,2,2,128]{4,3,2,1,0:T(2,128)(2,1)S(1)}, bf16[4,32,2,2,128]{4,3,2,1,0:T(2,128)(2,1)S(1)}, u32[]{:S(2)}, u32[]{:S(2)}) collective-permute-start(bf16[4,32,2,2,128]{4,3,2,1,0:T(2,128)(2,1)S(1)} %get-tuple-element.40), channel_id=1, source_target_pairs={{0,0},{1,1},{2,3},{3,2},{4,4},{5,5},{6,7},{7,6},{8,8},{9,9},{10,11... | collective-permute-start | bytes 393224 | tf_op jit(solution)/shard_map/ppermute | solution.py:38
  13.5 3.5 %collective-permute-done.fa_ref = bf16[4,32,2,2,128]{4,3,2,1,0:T(2,128)(2,1)S(1)} collective-permute-done((bf16[4,32,2,2,128]{4,3,2,1,0:T(2,128)(2,1)S(1)}, bf16[4,32,2,2,128]{4,3,2,1,0:T(2,128)(2,1)S(1)}, u32[]{:S(2)}, u32[]{:S(2)}) %collective-permute-start) | collective-permute-done | bytes 131104 | tf_op jit(solution)/shard_map/ppermute | solution.py:38
  17.1 0.0 collective-permute-done.1.fb_ref
  17.1 0.1 shard_map.58
  17.1 1.7 %collective-permute-start.2 = (bf16[4,40,256]{2,1,0:T(8,128)(2,1)S(1)}, bf16[4,40,256]{2,1,0:T(8,128)(2,1)S(1)}, u32[]{:S(2)}, u32[]{:S(2)}) collective-permute-start(bf16[4,40,256]{2,1,0:T(8,128)(2,1)S(1)} %get-tuple-element.45), channel_id=1, source_target_pairs={{0,12},{1,5},{2,6},{3,7},{4,8},{5,1},{6,2},{7,3},{8,4},{9,13},{10,... | collective-permute-start | bytes 245768 | tf_op jit(solution)/shard_map/ppermute | solution.py:38
  18.8 0.0 collective-permute-start.3
  18.8 1.4 %shard_map.59.p_ref = f32[4,33,8,256]{3,2,1,0:T(8,128)S(1)} custom-call(bf16[4,32,2,32,128]{4,3,2,1,0:T(8,128)(2,1)S(1)} %get-tuple-element.36.x_ref.refs_5_, bf16[4,32,2,2,128]{4,3,2,1,0:T(2,128)(2,1)S(1)} %collective-permute-done.fa_ref, bf16[4,32,2,2,128]{4,3,2,1,0:T(2,128)(2,1)S(1)} %collective-permute-done.1.fb_ref, ...), custom_call_target="tpu_custom_call" | custom-call | tf_op jit(solution)/shard_map/pallas_call | solution.py:382
  20.2 0.0 collective-permute-done.4.refs_1_
  20.3 0.0 copy-done.1
  20.3 2.8 %shard_map.60 = (bf16[4,32,2,32,128]{4,3,2,1,0:T(8,128)(2,1)}, f32[2,32,16,256]{3,2,1,0:T(8,128)S(1)}, f32[2,2,16,256]{3,2,1,0:T(8,128)S(1)}, bf16[512,768]{1,0:T(8,128)(2,1)S(1)}) custom-call(f32[4,33,32,256]{3,2,1,0:T(8,128)S(1)} %get-tuple-element.57.refs_0_, bf16[33,32,256]{2,1,0:T(8,128)(2,1)S(1)} %collective-permute-done.4.refs_1_, ...), custom_call_target="tpu_custom_call" | custom-call | tf_op jit(solution)/shard_map/pallas_call | solution.py:382
  23.0 0.9 %collective-permute-done.2.va_ref = bf16[4,40,256]{2,1,0:T(8,128)(2,1)S(1)} collective-permute-done((bf16[4,40,256]{2,1,0:T(8,128)(2,1)S(1)}, bf16[4,40,256]{2,1,0:T(8,128)(2,1)S(1)}, u32[]{:S(2)}, u32[]{:S(2)}) %collective-permute-start.2) | collective-permute-done | bytes 81952 | tf_op jit(solution)/shard_map/ppermute | solution.py:38
  24.0 0.0 collective-permute-done.3.vb_ref
  24.0 0.3 %shard_map.61 = (f32[4,33,8,256]{3,2,1,0:T(8,128)S(1)}, f32[4,2,32,256]{3,2,1,0:T(8,128)S(1)}, bf16[41,8,256]{2,1,0:T(8,128)(2,1)S(1)}) custom-call(bf16[4,40,256]{2,1,0:T(8,128)(2,1)S(1)} %collective-permute-done.2.va_ref, bf16[4,40,256]{2,1,0:T(8,128)(2,1)S(1)} %collective-permute-done.3.vb_ref, f32[4,33,8,256]{3,2,1,0:T(8,128)S(1)} %shard_map.59.p_ref, ...), custom_call_target="tpu_custom_call" | custom-call | tf_op jit(solution)/shard_map/pallas_call | solution.py:382
  24.3 0.1 collective-permute-start.5
  24.4 2.7 %shard_map.62 = (bf16[4,32,2,32,128]{4,3,2,1,0:T(8,128)(2,1)}, f32[2,32,16,256]{3,2,1,0:T(8,128)S(1)}, f32[2,2,16,256]{3,2,1,0:T(8,128)S(1)}) custom-call(f32[4,33,32,256]{3,2,1,0:T(8,128)S(1)} %get-tuple-element.57.refs_0_, bf16[33,32,256]{2,1,0:T(8,128)(2,1)S(1)} %collective-permute-done.4.refs_1_, ...), custom_call_target="tpu_custom_call", output_to_operand_aliasing={{0}: (6, {})} | custom-call | tf_op jit(solution)/shard_map/pallas_call | solution.py:382
  27.1 0.0 collective-permute-done.5.m_ref
  27.1 2.0 %shard_map.63 = bf16[4,32,2,32,128]{4,3,2,1,0:T(8,128)(2,1)} custom-call(f32[4,33,8,256]{3,2,1,0:T(8,128)S(1)} %get-tuple-element.54.r_ref, f32[4,2,32,256]{3,2,1,0:T(8,128)S(1)} %get-tuple-element.55.c_ref, bf16[41,8,256]{2,1,0:T(8,128)(2,1)S(1)} %collective-permute-done.5.m_ref, ...), custom_call_target="tpu_custom_call", output_to_operand_aliasing={{}: (9, {})} | custom-call | tf_op jit(solution)/shard_map/pallas_call | solution.py:382
  (5 shorter events, 0.0 us)
Async XLA Ops:
  0.0 1.7 %copy-start = (bf16[3,3,128,128]{3,2,1,0:T(8,128)(2,1)S(1)}, bf16[3,3,128,128]{3,2,1,0:T(8,128)(2,1)}, u32[]{:S(2)}) copy-start(bf16[3,3,128,128]{3,2,1,0:T(8,128)(2,1)} %w_ref.3) | copy-start | bytes 884740
  0.0 1.7 %copy-start.2 = (f32[4,128]{1,0:T(4,128)S(1)}, f32[4,128]{1,0:T(4,128)}, u32[]{:S(2)}) copy-start(f32[4,128]{1,0:T(4,128)} %d_ref.9) | copy-start | bytes 6148
  5.9 14.4 %collective-permute-start.4 = (bf16[33,32,256]{2,1,0:T(8,128)(2,1)S(1)}, bf16[33,32,256]{2,1,0:T(8,128)(2,1)S(1)}, u32[]{:S(2)}, u32[]{:S(2)}) collective-permute-start(bf16[33,32,256]{2,1,0:T(8,128)(2,1)S(1)} %get-tuple-element.49), channel_id=1, source_target_pairs={{0,16},{16,0},{1,17},{17,1},{2,18},{18,2},{3,19},{19,3},{4,20},{20... | collective-permute-start | bytes 1622024 | tf_op jit(solution)/shard_map/ppermute | solution.py:43
  6.4 10.6 %collective-permute-start = (bf16[4,32,2,2,128]{4,3,2,1,0:T(2,128)(2,1)S(1)}, bf16[4,32,2,2,128]{4,3,2,1,0:T(2,128)(2,1)S(1)}, u32[]{:S(2)}, u32[]{:S(2)}) collective-permute-start(bf16[4,32,2,2,128]{4,3,2,1,0:T(2,128)(2,1)S(1)} %get-tuple-element.39), channel_id=1, source_target_pairs={{0,15},{1,2},{2,1},{3,4},{4,3},{5,6},{6,5},{7,8},{8,7},{9,10},{10,... | collective-permute-start | bytes 393224 | tf_op jit(solution)/shard_map/ppermute | solution.py:38
  12.9 4.2 %collective-permute-start.1 = (bf16[4,32,2,2,128]{4,3,2,1,0:T(2,128)(2,1)S(1)}, bf16[4,32,2,2,128]{4,3,2,1,0:T(2,128)(2,1)S(1)}, u32[]{:S(2)}, u32[]{:S(2)}) collective-permute-start(bf16[4,32,2,2,128]{4,3,2,1,0:T(2,128)(2,1)S(1)} %get-tuple-element.40), channel_id=1, source_target_pairs={{0,0},{1,1},{2,3},{3,2},{4,4},{5,5},{6,7},{7,6},{8,8},{9,9},{10,11... | collective-permute-start | bytes 393224 | tf_op jit(solution)/shard_map/ppermute | solution.py:38
  17.1 6.8 %collective-permute-start.2 = (bf16[4,40,256]{2,1,0:T(8,128)(2,1)S(1)}, bf16[4,40,256]{2,1,0:T(8,128)(2,1)S(1)}, u32[]{:S(2)}, u32[]{:S(2)}) collective-permute-start(bf16[4,40,256]{2,1,0:T(8,128)(2,1)S(1)} %get-tuple-element.45), channel_id=1, source_target_pairs={{0,12},{1,5},{2,6},{3,7},{4,8},{5,1},{6,2},{7,3},{8,4},{9,13},{10,... | collective-permute-start | bytes 245768 | tf_op jit(solution)/shard_map/ppermute | solution.py:38
  18.8 5.2 %collective-permute-start.3 = (bf16[4,40,256]{2,1,0:T(8,128)(2,1)S(1)}, bf16[4,40,256]{2,1,0:T(8,128)(2,1)S(1)}, u32[]{:S(2)}, u32[]{:S(2)}) collective-permute-start(bf16[4,40,256]{2,1,0:T(8,128)(2,1)S(1)} %get-tuple-element.46), channel_id=1, source_target_pairs={{0,1},{1,0},{2,3},{3,2},{4,13},{5,9},{6,10},{7,11},{8,12},{9,5},{1... | collective-permute-start | bytes 245768 | tf_op jit(solution)/shard_map/ppermute | solution.py:38
  18.8 1.4 %copy-start.1 = (bf16[3,3,128,128]{3,2,1,0:T(8,128)(2,1)S(1)}, bf16[3,3,128,128]{3,2,1,0:T(8,128)(2,1)}, u32[]{:S(2)}) copy-start(bf16[3,3,128,128]{3,2,1,0:T(8,128)(2,1)} %refs_2_.1) | copy-start | bytes 884740
  18.8 1.4 %copy-start.3 = (f32[128]{0:T(128)S(1)}, f32[128]{0:T(128)}, u32[]{:S(2)}) copy-start(f32[128]{0:T(128)} %param.9) | copy-start | bytes 1540
  24.3 2.8 %collective-permute-start.5 = (bf16[41,8,256]{2,1,0:T(8,128)(2,1)S(1)}, bf16[41,8,256]{2,1,0:T(8,128)(2,1)S(1)}, u32[]{:S(2)}, u32[]{:S(2)}) collective-permute-start(bf16[41,8,256]{2,1,0:T(8,128)(2,1)S(1)} %get-tuple-element.56), channel_id=1, source_target_pairs={{0,16},{16,0},{1,17},{17,1},{2,18},{18,2},{3,19},{19,3},{4,20},{20... | collective-permute-start | bytes 503816 | tf_op jit(solution)/shard_map/ppermute | solution.py:43

commit v7 on v6

--- a/solution.py
+++ b/solution.py
@@ -11,7 +11,6 @@
 BF = jnp.bfloat16
 F32 = jnp.float32
 LIMIT = 24 << 20
-BLOCK = 16
 WIDE = 12
 VM = pl.BlockSpec(memory_space=pltpu.VMEM)
 ANY = pl.BlockSpec(memory_space=pl.ANY)
@@ -252,9 +251,9 @@
     return jnp.where(off, 0.0, value)
 
 
-def read_kernel(first, *refs):
+def read_kernel(p, n, *refs):
     s_ref, m_ref, w_ref, d_ref, skip_ref, x_ref = refs[:6]
-    if first == 0:
+    if p == 0:
         wide = refs[-4]
         spread(w_ref, wide)
         o_ref, side_ref, rim_ref = refs[-7:-4]
@@ -262,40 +261,35 @@
         wide = w_ref
         o_ref, side_ref, rim_ref = refs[-6:-3]
     held, out, sems = refs[-3:]
-    _, pairs, _, cols, _ = x_ref.shape
+    frames, pairs, _, cols, _ = x_ref.shape
     n2 = s_ref.shape[3]
     half = n2 // 2
     later = (lax.axis_index("tm") > 0).astype(F32)
     gain = skip_ref[...].reshape(1, 1, half)
     factor = jnp.full((1, n2), 1.0, F32) * later
-    for f in range(first):
+    copies = []
+    for f in range(frames):
         factor = factor * twice(d_ref, f)
-    copies = []
-    for i in range(side_ref.shape[0]):
-        f = first + i
-        factor = factor * twice(d_ref, f)
-        body = s_ref[f] + factor.reshape(1, 1, n2) * m_ref[...].astype(F32)
+        body = s_ref[f, p : p + n + 1]
+        body = body + factor.reshape(1, 1, n2) * m_ref[p : p + n + 1].astype(F32)
         held[...] = body.astype(BF)
-        held[0:1] = row_masked(body[0:1], 0, pairs).astype(BF)
-        held[pairs:] = row_masked(body[pairs:], pairs, pairs).astype(BF)
-        for p in range(0, pairs, BLOCK):
-            n = min(BLOCK, pairs - p)
-            y = dot(held[p : p + n].reshape(n * cols, n2), wide[:n2])
-            y = y + dot(held[p + 1 : p + 1 + n].reshape(n * cols, n2), wide[n2:])
-            y = gathered(y, n, cols, n2)
-            for r in range(2):
-                lane = pl.ds(r * half, half)
-                v = y[:, :, r * half : (r + 1) * half]
-                v = v + gain * x_ref[f, p : p + n, r].astype(F32)
-                out[i, p : p + n, r] = v[:, 8 : cols - 8].astype(BF)
-                side_ref[i, p : p + n, 0:8, lane] = v[:, :8]
-                side_ref[i, p : p + n, 8:16, lane] = v[:, cols - 8 :]
-                if p == 0:
-                    rim_ref[i, 0, :, lane] = v[0, 8 : cols - 8]
-                if p + n == pairs:
-                    rim_ref[i, 1, :, lane] = v[n - 1, 8 : cols - 8]
+        if p == 0:
+            held[:1] = row_masked(body[:1], 0, pairs).astype(BF)
+        else:
+            held[n:] = row_masked(body[n:], pairs, pairs).astype(BF)
+        y = dot(held[:n].reshape(n * cols, n2), wide[:n2])
+        y = y + dot(held[1:].reshape(n * cols, n2), wide[n2:])
+        y = gathered(y, n, cols, n2)
+        for r in range(2):
+            lane = pl.ds(r * half, half)
+            v = y[:, :, r * half : (r + 1) * half]
+            v = v + gain * x_ref[f, p : p + n, r].astype(F32)
+            out[f, :, r] = v[:, 8 : cols - 8].astype(BF)
+            side_ref[f, :, 0:8, lane] = v[:, :8]
+            side_ref[f, :, 8:16, lane] = v[:, cols - 8 :]
+            rim_ref[f, :, lane] = v[0 if p == 0 else n - 1, 8 : cols - 8]
         copy = pltpu.make_async_copy(
-            out.at[i], o_ref.at[f, :, :, pl.ds(8, cols - 16)], sems.at[i]
+            out.at[f], o_ref.at[f, pl.ds(p, n), :, pl.ds(8, cols - 16)], sems.at[f]
         )
         copy.start()
         copies.append(copy)
@@ -350,9 +344,8 @@
         near = near + jnp.where(col == 0, pltpu.roll(y1, b, 1) if b else y1, 0.0)
         far = jnp.where(col >= 6, pltpu.roll(y2, d, 1), 0.0)
         far = far + jnp.where(col == 7, pltpu.roll(y1, g, 1), 0.0)
-        which, i = divmod(f, sides[0].shape[0])
         for at, part, ref, base in ((0, near, left, 0), (8, far, right, cols - 8)):
-            total = sides[which][i, :, at : at + 8] + part
+            total = jnp.concatenate([own[f, :, at : at + 8] for own in sides]) + part
             for r in range(2):
                 ref[f, :, r] = total[:, :, r * half : (r + 1) * half].astype(BF)
                 lane = slice(r * half, (r + 1) * half)
@@ -361,7 +354,7 @@
                 ref[f, 0:1, r] = top.astype(BF)
                 ref[f, pairs - 1 :, r] = low.astype(BF)
         for k in range(2):
-            v = rims[which][i, k] + edge_rows[k][f, 8 : cols - 8]
+            v = rims[k][f] + edge_rows[k][f, 8 : cols - 8]
             for r in range(2):
                 rows[f, k, r] = v[:, r * half : (r + 1) * half].astype(BF)
         ends_of = ((0, 0), (pairs - 1, 1))
@@ -443,32 +436,32 @@
         (here, from_a, from_b, wide_in, decay),
         [pltpu.VMEM((count, pairs, 8, 2 * c), BF)],
     )
-    part = count // 2
-
-    def read(first, weight, mixed, local):
+    most = 5 * pairs // 8
+
+    def read(p, n, weight, mixed, local):
         given = (local, before, weight, decay, skip.reshape(1, c), here)
-        extra = [] if first == 0 else [mixed]
+        extra = [] if p == 0 else [mixed]
         outs = (
             shape(video.shape, BF),
-            shape((part, pairs, 16, n2), F32),
-            shape((part, 2, cols - 16, n2), F32),
+            shape((count, n, 16, n2), F32),
+            shape((count, cols - 16, n2), F32),
         )
-        more = (wide_out,) if first == 0 else ()
+        more = (wide_out,) if p == 0 else ()
         return call(
-            functools.partial(read_kernel, first),
+            functools.partial(read_kernel, p, n),
             (*outs, *more),
             (*given, *extra),
             [
-                pltpu.VMEM((pairs + 1, cols, n2), BF),
-                pltpu.VMEM((part, pairs, 2, cols - 16, c), BF),
-                pltpu.SemaphoreType.DMA((part,)),
+                pltpu.VMEM((n + 1, cols, n2), BF),
+                pltpu.VMEM((count, n, 2, cols - 16, c), BF),
+                pltpu.SemaphoreType.DMA((count,)),
             ],
             in_specs=[VM] * len(given) + [ANY] * len(extra),
             out_specs=(ANY, *[VM] * (len(outs) + len(more) - 1)),
             aliases={len(given): 0} if extra else {},
         )
 
-    mixed, side_0, rim_0, wide_out = read(0, w_out, None, local)
+    mixed, side_0, rim_0, wide_out = read(0, most, w_out, None, local)
     rows_a, rows_b, partial, side_0, local = lax.optimization_barrier(
         (rows_a, rows_b, partial, side_0, local)
     )
@@ -478,7 +471,7 @@
         (rows_a, rows_b, partial, wide_in, decay),
     )
     ring_before = onward(message)
-    mixed, side_1, rim_1 = read(part, wide_out, mixed, local)
+    mixed, side_1, rim_1 = read(most, pairs - most, wide_out, mixed, local)
     ring_before, side_1 = lax.optimization_barrier((ring_before, side_1))
     given = (ends, rim, ring_before, wide_out, decay, side_0, side_1, rim_0, rim_1)
     mixed = call(

time: 29.3 us -> 28.8 us (0.983)
  waiting for transfers between devices: 4.48 us -> 3.98 us
    ppermute x4, waiting for transfers between devices: 4.47 us -> 3.98 us  [swapped(): return lax.ppermute(value, 'tile', sorted(there.items()))]
where the time goes in v7:
time: 28.8 us; the launch traced here: 28.5 us
  Pallas kernels  15 us (52%)
  starting transfers between devices  9.4 us (33%)
  waiting for transfers between devices  3.98 us (14%)
    pallas_call x9, Pallas kernels, call(): pl.pallas_call(body, out_shape=outs, in_specs=in_specs or [VM] * len(ins)...  15 us
    ppermute x4, starting transfers between devices, swapped(): return lax.ppermute(value, 'tile', sorted(there.items()))  8.77 us
    ppermute x4, waiting for transfers between devices, swapped(): return lax.ppermute(value, 'tile', sorted(there.items()))  3.98 us
    ppermute x2, starting transfers between devices, onward(): lax.ppermute(value, 'tm', [(i, (i + 1) % groups) for i in range(groups)])  0.63 us
  transfers between devices with their start and end apart: 6, of which 2 were waited for; matrix products, arithmetic and copies ran while one was open for 0% of the time, Pallas kernels for 24%

profile of v7, /device:TPU:0, one launch (start us, length us, event | category | flops | bytes accessed | tf_op | source)
XLA Modules:
  0.0 28.5 jit_solution(15894991745950922437)
XLA Ops:
  0.0 1.7 %shard_map.55 = (bf16[4,32,2,32,128]{4,3,2,1,0:T(8,128)(2,1)S(1)}, bf16[4,32,2,2,128]{4,3,2,1,0:T(2,128)(2,1)S(1)}, bf16[4,32,2,2,128]{4,3,2,1,0:T(2,128)(2,1)S(1)}) custom-call(bf16[4,32,2,32,128]{4,3,2,1,0:T(8,128)(2,1)} %bitcast.7), custom_call_target="tpu_custom_call" | custom-call | tf_op jit(solution)/shard_map/pallas_call | solution.py:375
  1.7 0.0 copy-done
  1.7 0.0 copy-done.2
  1.7 1.2 %shard_map.56.p_ref = f32[4,9,32,256]{3,2,1,0:T(8,128)S(1)} custom-call(bf16[4,32,2,32,128]{4,3,2,1,0:T(8,128)(2,1)S(1)} %get-tuple-element.36.x_ref.refs_5_, bf16[3,3,128,128]{3,2,1,0:T(8,128)(2,1)S(1)} %copy-done, f32[4,128]{1,0:T(4,128)S(1)} %copy-done.2), custom_call_target="tpu_custom_call" | custom-call | tf_op jit(solution)/shard_map/pallas_call | solution.py:375
  2.9 2.9 %shard_map.57 = (f32[4,33,32,256]{3,2,1,0:T(8,128)S(1)}, bf16[33,32,256]{2,1,0:T(8,128)(2,1)S(1)}, bf16[512,768]{1,0:T(8,128)(2,1)S(1)}) custom-call(bf16[4,32,2,32,128]{4,3,2,1,0:T(8,128)(2,1)S(1)} %get-tuple-element.36.x_ref.refs_5_, bf16[3,3,128,128]{3,2,1,0:T(8,128)(2,1)S(1)} %copy-done, f32[4,128]{1,0:T(4,128)S(1)} %copy-done.2, ...), custom_call_target="tpu_custom_call" | custom-call | tf_op jit(solution)/shard_map/pallas_call | solution.py:375
  5.8 0.6 %collective-permute-start.4 = (bf16[33,32,256]{2,1,0:T(8,128)(2,1)S(1)}, bf16[33,32,256]{2,1,0:T(8,128)(2,1)S(1)}, u32[]{:S(2)}, u32[]{:S(2)}) collective-permute-start(bf16[33,32,256]{2,1,0:T(8,128)(2,1)S(1)} %get-tuple-element.49), channel_id=1, source_target_pairs={{0,16},{16,0},{1,17},{17,1},{2,18},{18,2},{3,19},{19,3},{4,20},{20... | collective-permute-start | bytes 1622024 | tf_op jit(solution)/shard_map/ppermute | solution.py:42
  6.4 6.4 %collective-permute-start = (bf16[4,32,2,2,128]{4,3,2,1,0:T(2,128)(2,1)S(1)}, bf16[4,32,2,2,128]{4,3,2,1,0:T(2,128)(2,1)S(1)}, u32[]{:S(2)}, u32[]{:S(2)}) collective-permute-start(bf16[4,32,2,2,128]{4,3,2,1,0:T(2,128)(2,1)S(1)} %get-tuple-element.39), channel_id=1, source_target_pairs={{0,15},{1,2},{2,1},{3,4},{4,3},{5,6},{6,5},{7,8},{8,7},{9,10},{10,... | collective-permute-start | bytes 393224 | tf_op jit(solution)/shard_map/ppermute | solution.py:37
  12.8 0.7 %collective-permute-start.1 = (bf16[4,32,2,2,128]{4,3,2,1,0:T(2,128)(2,1)S(1)}, bf16[4,32,2,2,128]{4,3,2,1,0:T(2,128)(2,1)S(1)}, u32[]{:S(2)}, u32[]{:S(2)}) collective-permute-start(bf16[4,32,2,2,128]{4,3,2,1,0:T(2,128)(2,1)S(1)} %get-tuple-element.40), channel_id=1, source_target_pairs={{0,0},{1,1},{2,3},{3,2},{4,4},{5,5},{6,7},{7,6},{8,8},{9,9},{10,11... | collective-permute-start | bytes 393224 | tf_op jit(solution)/shard_map/ppermute | solution.py:37
  13.5 3.5 %collective-permute-done.fa_ref = bf16[4,32,2,2,128]{4,3,2,1,0:T(2,128)(2,1)S(1)} collective-permute-done((bf16[4,32,2,2,128]{4,3,2,1,0:T(2,128)(2,1)S(1)}, bf16[4,32,2,2,128]{4,3,2,1,0:T(2,128)(2,1)S(1)}, u32[]{:S(2)}, u32[]{:S(2)}) %collective-permute-start) | collective-permute-done | bytes 131104 | tf_op jit(solution)/shard_map/ppermute | solution.py:37
  17.0 0.0 collective-permute-done.1.fb_ref
  17.0 0.1 shard_map.58
  17.1 1.7 %collective-permute-start.2 = (bf16[4,40,256]{2,1,0:T(8,128)(2,1)S(1)}, bf16[4,40,256]{2,1,0:T(8,128)(2,1)S(1)}, u32[]{:S(2)}, u32[]{:S(2)}) collective-permute-start(bf16[4,40,256]{2,1,0:T(8,128)(2,1)S(1)} %get-tuple-element.45), channel_id=1, source_target_pairs={{0,12},{1,5},{2,6},{3,7},{4,8},{5,1},{6,2},{7,3},{8,4},{9,13},{10,... | collective-permute-start | bytes 245768 | tf_op jit(solution)/shard_map/ppermute | solution.py:37
  18.8 0.0 collective-permute-start.3
  18.8 1.4 %shard_map.59.p_ref = f32[4,33,8,256]{3,2,1,0:T(8,128)S(1)} custom-call(bf16[4,32,2,32,128]{4,3,2,1,0:T(8,128)(2,1)S(1)} %get-tuple-element.36.x_ref.refs_5_, bf16[4,32,2,2,128]{4,3,2,1,0:T(2,128)(2,1)S(1)} %collective-permute-done.fa_ref, bf16[4,32,2,2,128]{4,3,2,1,0:T(2,128)(2,1)S(1)} %collective-permute-done.1.fb_ref, ...), custom_call_target="tpu_custom_call" | custom-call | tf_op jit(solution)/shard_map/pallas_call | solution.py:375
  20.2 0.0 collective-permute-done.4.refs_1_
  20.2 0.0 copy-done.1
  20.2 3.3 %shard_map.60 = (bf16[4,32,2,32,128]{4,3,2,1,0:T(8,128)(2,1)}, f32[4,20,16,256]{3,2,1,0:T(8,128)S(1)}, f32[4,16,256]{2,1,0:T(8,128)S(1)}, bf16[512,768]{1,0:T(8,128)(2,1)S(1)}) custom-call(f32[4,33,32,256]{3,2,1,0:T(8,128)S(1)} %get-tuple-element.57.refs_0_, bf16[33,32,256]{2,1,0:T(8,128)(2,1)S(1)} %collective-permute-done.4.refs_1_, ...), custom_call_target="tpu_custom_call" | custom-call | tf_op jit(solution)/shard_map/pallas_call | solution.py:375
  23.5 0.4 %collective-permute-done.2.va_ref = bf16[4,40,256]{2,1,0:T(8,128)(2,1)S(1)} collective-permute-done((bf16[4,40,256]{2,1,0:T(8,128)(2,1)S(1)}, bf16[4,40,256]{2,1,0:T(8,128)(2,1)S(1)}, u32[]{:S(2)}, u32[]{:S(2)}) %collective-permute-start.2) | collective-permute-done | bytes 81952 | tf_op jit(solution)/shard_map/ppermute | solution.py:37
  23.9 0.0 collective-permute-done.3.vb_ref
  23.9 0.3 %shard_map.61 = (f32[4,33,8,256]{3,2,1,0:T(8,128)S(1)}, f32[4,2,32,256]{3,2,1,0:T(8,128)S(1)}, bf16[41,8,256]{2,1,0:T(8,128)(2,1)S(1)}) custom-call(bf16[4,40,256]{2,1,0:T(8,128)(2,1)S(1)} %collective-permute-done.2.va_ref, bf16[4,40,256]{2,1,0:T(8,128)(2,1)S(1)} %collective-permute-done.3.vb_ref, f32[4,33,8,256]{3,2,1,0:T(8,128)S(1)} %shard_map.59.p_ref, ...), custom_call_target="tpu_custom_call" | custom-call | tf_op jit(solution)/shard_map/pallas_call | solution.py:375
  24.2 0.1 collective-permute-start.5
  24.3 2.2 %shard_map.62 = (bf16[4,32,2,32,128]{4,3,2,1,0:T(8,128)(2,1)}, f32[4,12,16,256]{3,2,1,0:T(8,128)S(1)}, f32[4,16,256]{2,1,0:T(8,128)S(1)}) custom-call(f32[4,33,32,256]{3,2,1,0:T(8,128)S(1)} %get-tuple-element.57.refs_0_, bf16[33,32,256]{2,1,0:T(8,128)(2,1)S(1)} %collective-permute-done.4.refs_1_, ...), custom_call_target="tpu_custom_call", output_to_operand_aliasing={{0}: (6, {})} | custom-call | tf_op jit(solution)/shard_map/pallas_call | solution.py:375
  26.5 0.0 collective-permute-done.5.m_ref
  26.5 2.0 %shard_map.63 = bf16[4,32,2,32,128]{4,3,2,1,0:T(8,128)(2,1)} custom-call(f32[4,33,8,256]{3,2,1,0:T(8,128)S(1)} %get-tuple-element.54.r_ref, f32[4,2,32,256]{3,2,1,0:T(8,128)S(1)} %get-tuple-element.55.c_ref, bf16[41,8,256]{2,1,0:T(8,128)(2,1)S(1)} %collective-permute-done.5.m_ref, ...), custom_call_target="tpu_custom_call", output_to_operand_aliasing={{}: (9, {})} | custom-call | tf_op jit(solution)/shard_map/pallas_call | solution.py:375
  (5 shorter events, 0.0 us)
Async XLA Ops:
  0.0 1.7 %copy-start = (bf16[3,3,128,128]{3,2,1,0:T(8,128)(2,1)S(1)}, bf16[3,3,128,128]{3,2,1,0:T(8,128)(2,1)}, u32[]{:S(2)}) copy-start(bf16[3,3,128,128]{3,2,1,0:T(8,128)(2,1)} %w_ref.3) | copy-start | bytes 884740
  0.0 1.7 %copy-start.2 = (f32[4,128]{1,0:T(4,128)S(1)}, f32[4,128]{1,0:T(4,128)}, u32[]{:S(2)}) copy-start(f32[4,128]{1,0:T(4,128)} %d_ref.9) | copy-start | bytes 6148
  5.8 14.4 %collective-permute-start.4 = (bf16[33,32,256]{2,1,0:T(8,128)(2,1)S(1)}, bf16[33,32,256]{2,1,0:T(8,128)(2,1)S(1)}, u32[]{:S(2)}, u32[]{:S(2)}) collective-permute-start(bf16[33,32,256]{2,1,0:T(8,128)(2,1)S(1)} %get-tuple-element.49), channel_id=1, source_target_pairs={{0,16},{16,0},{1,17},{17,1},{2,18},{18,2},{3,19},{19,3},{4,20},{20... | collective-permute-start | bytes 1622024 | tf_op jit(solution)/shard_map/ppermute | solution.py:42
  6.4 10.6 %collective-permute-start = (bf16[4,32,2,2,128]{4,3,2,1,0:T(2,128)(2,1)S(1)}, bf16[4,32,2,2,128]{4,3,2,1,0:T(2,128)(2,1)S(1)}, u32[]{:S(2)}, u32[]{:S(2)}) collective-permute-start(bf16[4,32,2,2,128]{4,3,2,1,0:T(2,128)(2,1)S(1)} %get-tuple-element.39), channel_id=1, source_target_pairs={{0,15},{1,2},{2,1},{3,4},{4,3},{5,6},{6,5},{7,8},{8,7},{9,10},{10,... | collective-permute-start | bytes 393224 | tf_op jit(solution)/shard_map/ppermute | solution.py:37
  12.8 4.2 %collective-permute-start.1 = (bf16[4,32,2,2,128]{4,3,2,1,0:T(2,128)(2,1)S(1)}, bf16[4,32,2,2,128]{4,3,2,1,0:T(2,128)(2,1)S(1)}, u32[]{:S(2)}, u32[]{:S(2)}) collective-permute-start(bf16[4,32,2,2,128]{4,3,2,1,0:T(2,128)(2,1)S(1)} %get-tuple-element.40), channel_id=1, source_target_pairs={{0,0},{1,1},{2,3},{3,2},{4,4},{5,5},{6,7},{7,6},{8,8},{9,9},{10,11... | collective-permute-start | bytes 393224 | tf_op jit(solution)/shard_map/ppermute | solution.py:37
  17.1 6.8 %collective-permute-start.2 = (bf16[4,40,256]{2,1,0:T(8,128)(2,1)S(1)}, bf16[4,40,256]{2,1,0:T(8,128)(2,1)S(1)}, u32[]{:S(2)}, u32[]{:S(2)}) collective-permute-start(bf16[4,40,256]{2,1,0:T(8,128)(2,1)S(1)} %get-tuple-element.45), channel_id=1, source_target_pairs={{0,12},{1,5},{2,6},{3,7},{4,8},{5,1},{6,2},{7,3},{8,4},{9,13},{10,... | collective-permute-start | bytes 245768 | tf_op jit(solution)/shard_map/ppermute | solution.py:37
  18.8 5.2 %collective-permute-start.3 = (bf16[4,40,256]{2,1,0:T(8,128)(2,1)S(1)}, bf16[4,40,256]{2,1,0:T(8,128)(2,1)S(1)}, u32[]{:S(2)}, u32[]{:S(2)}) collective-permute-start(bf16[4,40,256]{2,1,0:T(8,128)(2,1)S(1)} %get-tuple-element.46), channel_id=1, source_target_pairs={{0,1},{1,0},{2,3},{3,2},{4,13},{5,9},{6,10},{7,11},{8,12},{9,5},{1... | collective-permute-start | bytes 245768 | tf_op jit(solution)/shard_map/ppermute | solution.py:37
  18.8 1.4 %copy-start.1 = (bf16[3,3,128,128]{3,2,1,0:T(8,128)(2,1)S(1)}, bf16[3,3,128,128]{3,2,1,0:T(8,128)(2,1)}, u32[]{:S(2)}) copy-start(bf16[3,3,128,128]{3,2,1,0:T(8,128)(2,1)} %refs_2_.1) | copy-start | bytes 884740
  18.8 1.4 %copy-start.3 = (f32[128]{0:T(128)S(1)}, f32[128]{0:T(128)}, u32[]{:S(2)}) copy-start(f32[128]{0:T(128)} %param.9) | copy-start | bytes 1540
  24.2 2.3 %collective-permute-start.5 = (bf16[41,8,256]{2,1,0:T(8,128)(2,1)S(1)}, bf16[41,8,256]{2,1,0:T(8,128)(2,1)S(1)}, u32[]{:S(2)}, u32[]{:S(2)}) collective-permute-start(bf16[41,8,256]{2,1,0:T(8,128)(2,1)S(1)} %get-tuple-element.56), channel_id=1, source_target_pairs={{0,16},{16,0},{1,17},{17,1},{2,18},{18,2},{3,19},{19,3},{4,20},{20... | collective-permute-start | bytes 503816 | tf_op jit(solution)/shard_map/ppermute | solution.py:42
